TPU v7x, 256 devices: a whole 4x4x8 slice. The times are simulated.
256 devices in a mesh: dp: 64 (over z, x, core), tensor: 4 (over y).
Axes of the slice: x: 4, y: 4, z: 8, core: 2. Of those that a mesh axis runs over, the one named last changes fastest.
Arguments:
- tokens: bfloat16 [32768, 8192], P('dp', 'tensor'), may hold values from -6 to 6
- cotangent: bfloat16 [32768, 1024], P('dp', 'tensor'), may hold values from -6 to 6
- frozen_key_weight: bfloat16 [8192, 1024], P(None, 'tensor'), may hold values from -0.0625 to 0.0625
- counts: int32 [64, 64], P('dp'), may hold values from 1 to 12, 512 in all within a row
- holder_assignment: int32 [64], replicated, may hold values from 0 to 63, each once
- adapter_down_matrix: float32 [64, 64, 8192], P('dp', None, 'tensor'), may hold values from -0.0625 to 0.0625
- adapter_up_matrix: float32 [64, 64, 1024], P('dp', None, 'tensor'), may hold values from -0.06 to 0.06
- down_first_moment: float32 [64, 64, 8192], P('dp', None, 'tensor'), may hold values from -12 to 12
- down_second_moment: float32 [64, 64, 8192], P('dp', None, 'tensor'), may hold values from 1 to 100
- up_first_moment: float32 [64, 64, 1024], P('dp', None, 'tensor'), may hold values from -30 to 30
- up_second_moment: float32 [64, 64, 1024], P('dp', None, 'tensor'), may hold values from 10 to 1000
Outputs:
- layer_out: bfloat16 [32768, 1024], P('dp', 'tensor')
- input_grad: bfloat16 [32768, 8192], P('dp', 'tensor')
- fresh_down_matrix: float32 [64, 64, 8192], P('dp', None, 'tensor')
- fresh_down_first: float32 [64, 64, 8192], P('dp', None, 'tensor')
- fresh_down_second: float32 [64, 64, 8192], P('dp', None, 'tensor')
- fresh_up_matrix: float32 [64, 64, 1024], P('dp', None, 'tensor')
- fresh_up_first: float32 [64, 64, 1024], P('dp', None, 'tensor')
- fresh_up_second: float32 [64, 64, 1024], P('dp', None, 'tensor')
Inputs may be any that keep to these rules, and one draw needn't show every extreme that they name: `counts`: row j gives, adapter by adapter in order, how many of dp index j's tokens belong to each adapter; dp index j's rows of tokens and cotangent are grouped in that order; each row sums to 512, and some entry of each row equals 12. A permutation: holder_assignment[a] is the dp index that holds adapter a.
All inputs are finite; a program needn't handle non-finite values.
Results may differ from a plain program's by a relative error of at most 0.0021.
Values may be sent and summed in bfloat16 or wider, within the bound.
No kernel may reach another device: no remote copies, remote signals or barrier semaphores. Data moves between devices by JAX's collectives and lax.ppermute only.
A program may use at most 128 MiB of HBM per device.

v0:
```python
import jax
import jax.numpy as jnp
from jax import lax
from jax.experimental import pallas as pl
from jax.experimental.pallas import tpu as pltpu
from jax.sharding import Mesh, PartitionSpec as P


adapter_scale = 2.0
learn_rate = 0.01
beta_one = 0.9
beta_two = 0.999
adam_eps = 1e-08
adam_step = 10

NZ, NX, NC, NT = 8, 4, 2, 4
NS = NX * NC
CAP = 12
ROWS = NZ * CAP


bf16 = jnp.bfloat16
f32 = jnp.float32
R = NS * ROWS
MID = R // 2
RANK = 64
PAIR = 2 * RANK
WIDE = NZ * RANK


def optimizer_update(weight, moment, second, grad):
    moment_new = beta_one * moment + (1.0 - beta_one) * grad
    second_new = beta_two * second + (1.0 - beta_two) * grad * grad
    first_fix = 1.0 - beta_one**adam_step
    second_fix = 1.0 - beta_two**adam_step
    weight_new = weight - learn_rate * (moment_new / first_fix) / (
        jnp.sqrt(second_new / second_fix) + adam_eps
    )
    return (weight_new, moment_new, second_new)


def shift(v, k):
    return lax.ppermute(v, "t", [(i, (i + k) % NT) for i in range(NT)])


def dot(a, b, dims=((1,), (0,)), out=f32):
    return lax.dot_general(a, b, (dims, ((), ())), preferred_element_type=out)


def call(body, outs, specs=None, out_specs=None, grid=(), scratch=()):
    vm = pl.BlockSpec(memory_space=pltpu.VMEM)
    kw = {}
    if grid:
        kw["grid"] = grid
    one = not isinstance(outs, (tuple, list))
    return pl.pallas_call(
        body,
        out_shape=outs,
        in_specs=specs,
        out_specs=out_specs or (vm if one else [vm] * len(outs)),
        scratch_shapes=list(scratch),
        **kw,
    )


VM = pl.BlockSpec(memory_space=pltpu.VMEM)


def whole(shape):
    return pl.BlockSpec(shape, lambda *_: (0,) * len(shape))


def row_mask():
    r = lax.broadcasted_iota(jnp.int32, (ROWS, WIDE), 0)
    first = lax.shift_right_logical(lax.broadcasted_iota(jnp.int32, (ROWS, WIDE), 1), 6) * CAP
    return (r >= first) & (r < first + CAP)


def fold(v):
    mask = row_mask()
    rows = []
    for s in range(NS):
        m = jnp.where(mask, v[s * ROWS : (s + 1) * ROWS], 0.0)
        rows.append(sum(m[:, q * PAIR : (q + 1) * PAIR] for q in range(1, NZ // 2)) + m[:, :PAIR])
    half = NS // 2
    return jnp.concatenate(
        [rows[s] + pltpu.roll(rows[s + half], RANK, 1) for s in range(half)], axis=0
    )


def spread_rows(total, out_ref):
    mask = row_mask()
    both = (total, pltpu.roll(total, RANK, 1))
    for s in range(NS):
        half, at = s // (NS // 2), s % (NS // 2) * ROWS
        v = both[half][at : at + ROWS]
        out_ref[pl.ds(s * ROWS, ROWS), :] = jnp.where(
            mask, jnp.concatenate([v] * (NZ // 2), axis=1), 0.0
        ).astype(bf16)


def spread_cols(total, out_ref):
    lo = total.T
    hi = jnp.concatenate([lo[RANK:], lo[:RANK]], axis=0)
    both = jnp.concatenate([lo, hi], axis=1)
    col = lax.broadcasted_iota(jnp.int32, (RANK, R), 1)
    for s in range(1, NS):
        col = jnp.where(lax.broadcasted_iota(jnp.int32, (RANK, R), 1) >= s * ROWS, col - ROWS, col)
    for a in range(NZ):
        keep = (col >= a * CAP) & (col < (a + 1) * CAP)
        v = both[(a % 2) * RANK : (a % 2 + 1) * RANK]
        out_ref[pl.ds(a * RANK, RANK), :] = jnp.where(keep, v, 0.0).astype(bf16)


def back_kernel(g, up, out):
    out[...] = fold(dot(g[...], up[...], ((1,), (1,))))


def grad_kernel(a, b, c, d, x, back16, grad, cols):
    @pl.when(pl.program_id(0) == 0)
    def _():
        total = adapter_scale * (a[...] + b[...] + c[...] + d[...])
        spread_rows(total, back16)
        spread_cols(total, cols)

    grad[...] = dot(cols[...], x[...])


def adg_kernel(back16, down, out):
    out[...] = dot(back16[...], down[...]).astype(bf16)


def hid_kernel(x, down, out, acc):
    @pl.when(pl.program_id(0) == 0)
    def _():
        acc[...] = jnp.zeros_like(acc)

    acc[...] += dot(x[...], down[...], ((1,), (1,)))

    @pl.when(pl.program_id(0) == pl.num_programs(0) - 1)
    def _():
        out[...] = fold(acc[...])


def up_kernel(a, b, c, d, g, up, out, grad, rows, cols):
    total = a[...] + b[...] + c[...] + d[...]
    spread_rows(total, rows)
    spread_cols(total, cols)
    out[...] = (adapter_scale * dot(rows[...], up[...])).astype(bf16)
    grad[...] = dot(cols[...], g[...])


def base_kernel(c, tokens, own, m1, m2, m3, o1, o2, o3, w, p0, p1, p2, p3):
    half = m1.shape[0]
    keyw = m1.shape[1]
    w[:, :keyw] = own[...]
    for k, (m, o) in enumerate(((m1, o1), (m2, o2), (m3, o3))):
        cols = pl.ds((k + 1) * keyw, keyw)

        @pl.when(c[0] == 0)
        def _():
            w[:half, cols] = m[...]
            w[half:, cols] = o[...]

        @pl.when(c[0] == 1)
        def _():
            w[:half, cols] = o[...]
            w[half:, cols] = m[...]

    for k, p in enumerate((p0, p1, p2, p3)):
        p[...] = dot(tokens[...], w[:, k * keyw : (k + 1) * keyw])


def run_back(g_rows, all16, feat, keyw):
    return call(
        back_kernel,
        jax.ShapeDtypeStruct((MID, PAIR), f32),
        [whole((R, keyw)), pl.BlockSpec((WIDE, keyw), lambda i: (0, feat // keyw))],
        whole((MID, PAIR)),
        (1,),
    )(g_rows, all16)


def run_grad(parts, x_rows):
    feat = x_rows.shape[1]
    nb = 4
    return call(
        grad_kernel,
        [jax.ShapeDtypeStruct((R, WIDE), bf16), jax.ShapeDtypeStruct((WIDE, feat), f32)],
        [whole((MID, PAIR))] * 4 + [pl.BlockSpec((R, feat // nb), lambda j: (0, j))],
        [whole((R, WIDE)), pl.BlockSpec((WIDE, feat // nb), lambda j: (0, j))],
        (nb,),
        [pltpu.VMEM((WIDE, R), bf16)],
    )(*parts, x_rows)


def run_adg(back16, all16, feat):
    nb = 4
    return call(
        adg_kernel,
        jax.ShapeDtypeStruct((R, feat), bf16),
        [whole((R, WIDE)), pl.BlockSpec((WIDE, feat // nb), lambda j: (0, j))],
        pl.BlockSpec((R, feat // nb), lambda j: (0, j)),
        (nb,),
    )(back16, all16)


def run_hid(x_rows, all16):
    feat = x_rows.shape[1]
    nb = 4
    return call(
        hid_kernel,
        jax.ShapeDtypeStruct((MID, PAIR), f32),
        [
            pl.BlockSpec((R, feat // nb), lambda j: (0, j)),
            pl.BlockSpec((WIDE, feat // nb), lambda j: (0, j)),
        ],
        whole((MID, PAIR)),
        (nb,),
        [pltpu.VMEM((R, WIDE), f32)],
    )(x_rows, all16)


def run_up(parts, g_rows, all16, feat):
    keyw = g_rows.shape[1]
    return call(
        up_kernel,
        [jax.ShapeDtypeStruct((R, keyw), bf16), jax.ShapeDtypeStruct((WIDE, keyw), f32)],
        [whole((MID, PAIR))] * 4
        + [whole((R, keyw)), pl.BlockSpec((WIDE, keyw), lambda i: (0, feat // keyw))],
        [whole((R, keyw)), whole((WIDE, keyw))],
        (1,),
        [pltpu.VMEM((R, WIDE), bf16), pltpu.VMEM((WIDE, R), bf16)],
    )(*parts, g_rows, all16)


def run_base(c, tokens, own, mine, other):
    rows, feat = tokens.shape
    keyw = own.shape[1]
    return call(
        base_kernel,
        [jax.ShapeDtypeStruct((feat, NT * keyw), bf16)]
        + [jax.ShapeDtypeStruct((rows, keyw), f32)] * NT,
        [pl.BlockSpec(memory_space=pltpu.SMEM)] + [VM] * 8,
        [VM] * (1 + NT),
    )(c.reshape(1), tokens, own, *mine, *other)


def step(
    tokens,
    cotangent,
    frozen_key_weight,
    counts,
    holder_assignment,
    adapter_down_matrix,
    adapter_up_matrix,
    down_first_moment,
    down_second_moment,
    up_first_moment,
    up_second_moment,
):
    tok_rows, feat = tokens.shape
    keyw = cotangent.shape[1]
    rank = adapter_down_matrix.shape[1]
    t = lax.axis_index("t")
    c = lax.axis_index("c")

    both16 = jnp.concatenate([adapter_down_matrix[0], adapter_up_matrix[0]], axis=1).astype(bf16)
    all16 = lax.all_gather(both16, "z", axis=0, tiled=True)

    own_counts = counts[0]
    upper = jnp.cumsum(own_counts)
    lower = upper - own_counts
    slot = jnp.arange(NS * ROWS, dtype=jnp.int32)
    slot_owner = (slot % ROWS) // CAP * NS + slot // ROWS
    slot_k = slot % CAP
    pick = holder_assignment[None, :] == slot_owner[:, None]
    start = jnp.sum(jnp.where(pick, lower[None, :], 0), axis=1)
    count = jnp.sum(jnp.where(pick, own_counts[None, :], 0), axis=1)
    source = jnp.where(slot_k < count, start + slot_k, -1)
    route = (source[:, None] == jnp.arange(tok_rows, dtype=jnp.int32)[None, :]).astype(bf16)

    x_send = dot(route, tokens, out=bf16)
    x_rows = lax.all_to_all(x_send, ("x", "c"), 0, 0, tiled=True)
    g_send = dot(route, cotangent, out=bf16)
    g_rows = lax.all_to_all(g_send, ("x", "c"), 0, 0, tiled=True)

    half = feat // NC
    halves = []
    for k in range(1, NT):
        piece = lax.dynamic_slice(
            frozen_key_weight, (((t + k) % NT) * feat + c * half, 0), (half, keyw)
        )
        halves.append(shift(piece, k))
    other = [lax.ppermute(v, "c", [(0, 1), (1, 0)]) for v in halves]
    own_w = lax.dynamic_slice(frozen_key_weight, (t * feat, 0), (feat, keyw))
    weight, base_out, *outs = run_base(c, tokens, own_w, halves, other)
    for k in range(1, NT):
        base_out = base_out + shift(outs[k - 1], -k)
    cots = [cotangent] + [shift(cotangent, k) for k in range(1, NT)]
    base_grad = dot(jnp.concatenate(cots, axis=1), weight, ((1,), (1,)))

    def parts_of(own):
        return [own] + [shift(own, k) for k in range(1, NT)]

    back16, grad_part = run_grad(parts_of(run_back(g_rows, all16, feat, keyw)), x_rows)
    grad_down = lax.psum_scatter(grad_part, "z", scatter_dimension=0, tiled=True)
    adapter_grad = run_adg(back16, all16, feat)
    ret_grad = lax.all_to_all(adapter_grad, ("x", "c"), 0, 0, tiled=True)

    hidden = parts_of(run_hid(x_rows, all16))
    adapter_out, up_part = run_up(hidden, g_rows, all16, feat)
    ret_out = lax.all_to_all(adapter_out, ("x", "c"), 0, 0, tiled=True)
    parts = lax.all_to_all(up_part, "z", 0, 0, tiled=True)
    grad_up = jnp.sum(parts.reshape(NZ, rank, keyw), axis=0)

    layer_out = (base_out + dot(route, ret_out, ((0,), (0,)))).astype(bf16)
    input_grad = (base_grad + dot(route, ret_grad, ((0,), (0,)))).astype(bf16)
    fresh_down = optimizer_update(
        adapter_down_matrix[0], down_first_moment[0], down_second_moment[0], grad_down
    )
    fresh_up = optimizer_update(
        adapter_up_matrix[0], up_first_moment[0], up_second_moment[0], adapter_scale * grad_up
    )
    return (layer_out, input_grad) + tuple(v[None] for v in fresh_down + fresh_up)


def solution(mesh):
    split = Mesh(mesh.devices.reshape(NZ, NX, NC, NT), ("z", "x", "c", "t"))
    dp = ("z", "x", "c")
    act = P(dp, "t")
    state = P(dp, None, "t")
    return jax.shard_map(
        step,
        mesh=split,
        in_specs=(act, act, P(None, "t"), P(dp, None), P()) + (state,) * 6,
        out_specs=(act, act) + (state,) * 6,
        check_vma=False,
    )
```

profile of v0, /device:TPU:2, one launch (start us, length us, event | category | flops | bytes accessed | tf_op | source)
XLA Modules:
  0.0 242.9 jit_solution(14917791432256960958)
XLA Ops:
  14.6 5.6 %all-to-all-start.1 = ((bf16[8,96,256]{2,1,0:T(8,128)(2,1)}), bf16[8,96,256]{2,1,0:T(8,128)(2,1)S(1)}, u32[]{:S(2)}, u32[]{:S(2)}) async-start(bf16[8,96,256]{2,1,0:T(8,128)(2,1)} %bitcast.7), calls=%async_computation.1 | async-start | bytes 786432 | tf_op jit(solution)/shard_map/all_to_all | solution.py:286
  20.2 3.5 %fusion.3 = bf16[768,2048]{1,0:T(8,128)(2,1)} fusion(bf16[512,2048]{1,0:T(8,128)(2,1)S(1)} %copy-done.2, s32[768]{0:T(1024)S(1)} %add_select_fusion.3), kind=kOutput, calls=%fused_computation.5 | convolution fusion | flops 1611005952 | bytes 5245952 | tf_op jit(solution)/shard_map/dot_general | solution.py:47
  23.6 4.0 %all-to-all-done.1 = bf16[8,96,256]{2,1,0:T(8,128)(2,1)S(1)} async-done(((bf16[8,96,256]{2,1,0:T(8,128)(2,1)}), bf16[8,96,256]{2,1,0:T(8,128)(2,1)S(1)}, u32[]{:S(2)}, u32[]{:S(2)}) %all-to-all-start.1) | async-done | bytes 393248 | tf_op jit(solution)/shard_map/all_to_all | solution.py:286
  28.4 5.0 %all-to-all-start = ((bf16[8,96,2048]{2,1,0:T(8,128)(2,1)}), bf16[8,96,2048]{2,1,0:T(8,128)(2,1)S(1)}, u32[]{:S(2)}, u32[]{:S(2)}) async-start(bf16[8,96,2048]{2,1,0:T(8,128)(2,1)} %bitcast.55), calls=%async_computation | async-start | bytes 6291456 | tf_op jit(solution)/shard_map/all_to_all | solution.py:284
  33.4 21.1 %all-gather.2.cloned.1.call-done.down.up = bf16[512,2304]{1,0:T(8,128)(2,1)} async-done(((bf16[64,2304]{1,0:T(8,128)(2,1)}), bf16[512,2304]{1,0:T(8,128)(2,1)}) %all-gather.2.cloned.1.call-update) | async-done | bytes 2359312 | tf_op jit(solution)/shard_map/all_gather | solution.py:269
  56.8 2.7 %collective-permute-start.17 = (f32[384,128]{1,0:T(8,128)}, f32[384,128]{1,0:T(8,128)S(1)}, u32[]{:S(2)}, u32[]{:S(2)}) collective-permute-start(f32[384,128]{1,0:T(8,128)} %shard_map.173.a), channel_id=1, source_target_pairs={{0,3},{1,0},{2,1},{3,2},{4,7},{5,4},{6,5},{7,6},{8,11},{9,8},{10,9... | collective-permute-start | bytes 589832 | tf_op jit(solution)/shard_map/ppermute | solution.py:43
  61.2 9.2 %all-to-all-done = bf16[8,96,2048]{2,1,0:T(8,128)(2,1)S(1)} async-done(((bf16[8,96,2048]{2,1,0:T(8,128)(2,1)}), bf16[8,96,2048]{2,1,0:T(8,128)(2,1)S(1)}, u32[]{:S(2)}, u32[]{:S(2)}) %all-to-all-start) | async-done | bytes 3145760 | tf_op jit(solution)/shard_map/all_to_all | solution.py:284
  72.2 6.1 %shard_map.174 = (bf16[768,512]{1,0:T(8,128)(2,1)}, f32[512,2048]{1,0:T(8,128)}) custom-call(f32[384,128]{1,0:T(8,128)} %shard_map.173.a, f32[384,128]{1,0:T(8,128)} %collective-permute-done.15.b, f32[384,128]{1,0:T(8,128)} %copy-done.11, f32[384,128]{1,0:T(8,128)} %copy-done.10, bf16[768,2048]{1,0:T(8,128)(2,1)} %bitcast.49), custom_call_target="tpu_custom_call" | custom-call | tf_op jit(solution)/shard_map/pallas_call | solution.py:187
  78.2 5.5 %shard_map.171.a = f32[384,128]{1,0:T(8,128)} custom-call(bf16[768,2048]{1,0:T(8,128)(2,1)} %bitcast.50, bf16[512,2304]{1,0:T(8,128)(2,1)} %all-gather.2.cloned.1.call-done.down.up), custom_call_target="tpu_custom_call" | custom-call | tf_op jit(solution)/shard_map/pallas_call | solution.py:211
  87.5 6.8 %collective-permute-done.11.d = f32[384,128]{1,0:T(8,128)S(1)} collective-permute-done((f32[384,128]{1,0:T(8,128)}, f32[384,128]{1,0:T(8,128)S(1)}, u32[]{:S(2)}, u32[]{:S(2)}) %collective-permute-start.11) | collective-permute-done | bytes 196640 | tf_op jit(solution)/shard_map/ppermute | solution.py:43
  98.6 2.9 %shard_map.172 = (bf16[768,256]{1,0:T(8,128)(2,1)}, f32[512,256]{1,0:T(8,128)}) custom-call(f32[384,128]{1,0:T(8,128)} %shard_map.171.a, f32[384,128]{1,0:T(8,128)} %copy-done.9, f32[384,128]{1,0:T(8,128)} %copy-done.8, f32[384,128]{1,0:T(8,128)} %copy-done.7, bf16[768,256]{1,0:T(8,128)(2,1)} %bitcast.53, bf16[512,2304]{1,0:T(8,128)(2,1)} %all-gather.2.cloned.1.call-done.down.up), custom_call_target="tpu_custom_call" | custom-call | tf_op jit(solution)/shard_map/pallas_call | solution.py:226
  101.6 12.3 %all_to_all.55 = bf16[8,96,256]{2,1,0:T(8,128)(2,1)S(1)} all-to-all(bf16[8,96,256]{2,1,0:T(8,128)(2,1)} %bitcast.58), channel_id=1, replica_groups=mesh['z'=8,'x'=4,'c'=2,'t'=4] {'x','c'}, dimensions={0} | all-to-all | bytes 786432 | tf_op jit(solution)/shard_map/all_to_all | solution.py:313
  113.8 8.5 %all-to-all-start.4 = ((f32[8,64,256]{2,1,0:T(8,128)}), f32[8,64,256]{2,1,0:T(8,128)S(1)}, u32[]{:S(2)}, u32[]{:S(2)}) async-start(f32[8,64,256]{2,1,0:T(8,128)} %bitcast.56), calls=%async_computation.5 | async-start | bytes 1048576 | tf_op jit(solution)/shard_map/all_to_all | solution.py:314
  122.3 5.4 %shard_map.175 = bf16[768,2048]{1,0:T(8,128)(2,1)} custom-call(bf16[768,512]{1,0:T(8,128)(2,1)} %get-tuple-element.23.back16, bf16[512,2304]{1,0:T(8,128)(2,1)} %all-gather.2.cloned.1.call-done.down.up), custom_call_target="tpu_custom_call" | custom-call | tf_op jit(solution)/shard_map/pallas_call | solution.py:199
  127.7 18.5 %all-to-all-done.4 = f32[8,64,256]{2,1,0:T(8,128)S(1)} async-done(((f32[8,64,256]{2,1,0:T(8,128)}), f32[8,64,256]{2,1,0:T(8,128)S(1)}, u32[]{:S(2)}, u32[]{:S(2)}) %all-to-all-start.4) | async-done | bytes 524320 | tf_op jit(solution)/shard_map/all_to_all | solution.py:314
  147.0 4.8 %all-to-all-start.3 = ((bf16[8,96,2048]{2,1,0:T(8,128)(2,1)}), bf16[8,96,2048]{2,1,0:T(8,128)(2,1)S(1)}, u32[]{:S(2)}, u32[]{:S(2)}) async-start(bf16[8,96,2048]{2,1,0:T(8,128)(2,1)} %bitcast.51), calls=%async_computation.3 | async-start | bytes 6291456 | tf_op jit(solution)/shard_map/all_to_all | solution.py:309
  156.0 12.2 %collective-permute-done.2.m3 = bf16[1024,256]{1,0:T(8,128)(2,1)} collective-permute-done((bf16[1024,256]{1,0:T(8,128)(2,1)S(1)}, bf16[1024,256]{1,0:T(8,128)(2,1)}, u32[]{:S(2)}, u32[]{:S(2)}) %collective-permute-start.2) | collective-permute-done | bytes 524320 | tf_op jit(solution)/shard_map/ppermute | solution.py:43
  168.3 12.1 %collective-permute-done.m1 = bf16[1024,256]{1,0:T(8,128)(2,1)} collective-permute-done((bf16[1024,256]{1,0:T(8,128)(2,1)S(1)}, bf16[1024,256]{1,0:T(8,128)(2,1)}, u32[]{:S(2)}, u32[]{:S(2)}) %collective-permute-start) | collective-permute-done | bytes 524320 | tf_op jit(solution)/shard_map/ppermute | solution.py:43
  183.4 6.7 %shard_map.170 = (bf16[2048,1024]{1,0:T(8,128)(2,1)}, f32[512,256]{1,0:T(8,128)}, f32[512,256]{1,0:T(8,128)}, f32[512,256]{1,0:T(8,128)}, f32[512,256]{1,0:T(8,128)}) custom-call(s32[1]{0:T(128)} %bitcast.c, bf16[512,2048]{1,0:T(8,128)(2,1)} %tokens.1, bf16[2048,256]{1,0:T(8,128)(2,1)} %constant_dynamic-slice_fusion.3.own, ...), custom_call_target="tpu_custom_call" | custom-call | tf_op jit(solution)/shard_map/pallas_call | solution.py:240
  192.3 3.9 %collective-permute-start.13 = (bf16[512,256]{1,0:T(8,128)(2,1)}, bf16[512,256]{1,0:T(8,128)(2,1)}, u32[]{:S(2)}, u32[]{:S(2)}) collective-permute-start(bf16[512,256]{1,0:T(8,128)(2,1)} %param.12), channel_id=1, source_target_pairs={{0,2},{1,3},{2,0},{3,1},{4,6},{5,7},{6,4},{7,5},{8,10},{9,11},{10,... | collective-permute-start | bytes 786440 | tf_op jit(solution)/shard_map/ppermute | solution.py:43
  196.9 8.1 %collective-permute-done.6 = f32[512,256]{1,0:T(8,128)S(1)} collective-permute-done((f32[512,256]{1,0:T(8,128)}, f32[512,256]{1,0:T(8,128)S(1)}, u32[]{:S(2)}, u32[]{:S(2)}) %collective-permute-start.6) | collective-permute-done | bytes 524320 | tf_op jit(solution)/shard_map/ppermute | solution.py:43
  206.8 11.3 %collective-permute-done.8 = f32[512,256]{1,0:T(8,128)S(1)} collective-permute-done((f32[512,256]{1,0:T(8,128)}, f32[512,256]{1,0:T(8,128)S(1)}, u32[]{:S(2)}, u32[]{:S(2)}) %collective-permute-start.8) | collective-permute-done | bytes 524320 | tf_op jit(solution)/shard_map/ppermute | solution.py:43
  224.7 3.9 %collective-permute-done.12 = bf16[512,256]{1,0:T(8,128)(2,1)} collective-permute-done((bf16[512,256]{1,0:T(8,128)(2,1)}, bf16[512,256]{1,0:T(8,128)(2,1)}, u32[]{:S(2)}, u32[]{:S(2)}) %collective-permute-start.12) | collective-permute-done | bytes 262176 | tf_op jit(solution)/shard_map/ppermute | solution.py:43
  228.7 4.9 %add_convert_fusion = bf16[512,2048]{1,0:T(8,128)(2,1)} fusion(f32[512,2048]{1,0:T(8,128)S(1)} %fusion, bf16[2048,1024]{1,0:T(8,128)(2,1)S(1)} %copy-done.12, bf16[512,256]{1,0:T(8,128)(2,1)S(1)} %collective-permute-done.14, bf16[512,256]{1,0:T(8,128)(2,1)} %collective-permute-done.13, bf16[512,256]{1,0:T(8,128)(2,1)} %collective-permute-done.12, ...), kind=kOutput, calls=%fused_computation | convolution fusion | flops 2153775104 | bytes 11534336 | tf_op jit(solution)/shard_map/dot_general | solution.py:47
  (80 shorter events, 43.8 us)
Async XLA Ops:
  7.2 47.3 %all-gather.2.cloned.1.call-start = ((), (), s32[]{:S(2)}) async-start(), calls=%async_computation.6 | async-start | bytes 2654208 | tf_op jit(solution)/shard_map/all_gather | solution.py:269
  14.6 13.1 %all-to-all-start.1 = ((bf16[8,96,256]{2,1,0:T(8,128)(2,1)}), bf16[8,96,256]{2,1,0:T(8,128)(2,1)S(1)}, u32[]{:S(2)}, u32[]{:S(2)}) async-start(bf16[8,96,256]{2,1,0:T(8,128)(2,1)} %bitcast.7), calls=%async_computation.1 | async-start | bytes 786432 | tf_op jit(solution)/shard_map/all_to_all | solution.py:286
  28.4 42.0 %all-to-all-start = ((bf16[8,96,2048]{2,1,0:T(8,128)(2,1)}), bf16[8,96,2048]{2,1,0:T(8,128)(2,1)S(1)}, u32[]{:S(2)}, u32[]{:S(2)}) async-start(bf16[8,96,2048]{2,1,0:T(8,128)(2,1)} %bitcast.55), calls=%async_computation | async-start | bytes 6291456 | tf_op jit(solution)/shard_map/all_to_all | solution.py:284
  33.4 200.2 %reduce-scatter.2.cloned.1.call-start = ((), (), s32[]{:S(2)}) async-start(), calls=%async_computation.7 | async-start | bytes 4718592 | tf_op jit(solution)/shard_map/reduce_scatter | solution.py:307
  56.8 13.6 %collective-permute-start.17 = (f32[384,128]{1,0:T(8,128)}, f32[384,128]{1,0:T(8,128)S(1)}, u32[]{:S(2)}, u32[]{:S(2)}) collective-permute-start(f32[384,128]{1,0:T(8,128)} %shard_map.173.a), channel_id=1, source_target_pairs={{0,3},{1,0},{2,1},{3,2},{4,7},{5,4},{6,5},{7,6},{8,11},{9,8},{10,9... | collective-permute-start | bytes 589832 | tf_op jit(solution)/shard_map/ppermute | solution.py:43
  59.5 10.9 %collective-permute-start.16 = (f32[384,128]{1,0:T(8,128)}, f32[384,128]{1,0:T(8,128)S(1)}, u32[]{:S(2)}, u32[]{:S(2)}) collective-permute-start(f32[384,128]{1,0:T(8,128)} %shard_map.173.a), channel_id=1, source_target_pairs={{0,2},{1,3},{2,0},{3,1},{4,6},{5,7},{6,4},{7,5},{8,10},{9,11},{10,... | collective-permute-start | bytes 589832 | tf_op jit(solution)/shard_map/ppermute | solution.py:43
  60.3 10.1 %collective-permute-start.15 = (f32[384,128]{1,0:T(8,128)}, f32[384,128]{1,0:T(8,128)}, u32[]{:S(2)}, u32[]{:S(2)}) collective-permute-start(f32[384,128]{1,0:T(8,128)} %shard_map.173.a), channel_id=1, source_target_pairs={{0,1},{1,2},{2,3},{3,0},{4,5},{5,6},{6,7},{7,4},{8,9},{9,10},{10,1... | collective-permute-start | bytes 589832 | tf_op jit(solution)/shard_map/ppermute | solution.py:43
  83.7 10.7 %collective-permute-start.11 = (f32[384,128]{1,0:T(8,128)}, f32[384,128]{1,0:T(8,128)S(1)}, u32[]{:S(2)}, u32[]{:S(2)}) collective-permute-start(f32[384,128]{1,0:T(8,128)} %shard_map.171.a), channel_id=1, source_target_pairs={{0,3},{1,0},{2,1},{3,2},{4,7},{5,4},{6,5},{7,6},{8,11},{9,8},{10,9... | collective-permute-start | bytes 589832 | tf_op jit(solution)/shard_map/ppermute | solution.py:43
  85.9 9.5 %collective-permute-start.10 = (f32[384,128]{1,0:T(8,128)}, f32[384,128]{1,0:T(8,128)S(1)}, u32[]{:S(2)}, u32[]{:S(2)}) collective-permute-start(f32[384,128]{1,0:T(8,128)} %shard_map.171.a), channel_id=1, source_target_pairs={{0,2},{1,3},{2,0},{3,1},{4,6},{5,7},{6,4},{7,5},{8,10},{9,11},{10,... | collective-permute-start | bytes 589832 | tf_op jit(solution)/shard_map/ppermute | solution.py:43
  86.6 11.4 %collective-permute-start.9 = (f32[384,128]{1,0:T(8,128)}, f32[384,128]{1,0:T(8,128)S(1)}, u32[]{:S(2)}, u32[]{:S(2)}) collective-permute-start(f32[384,128]{1,0:T(8,128)} %shard_map.171.a), channel_id=1, source_target_pairs={{0,1},{1,2},{2,3},{3,0},{4,5},{5,6},{6,7},{7,4},{8,9},{9,10},{10,1... | collective-permute-start | bytes 589832 | tf_op jit(solution)/shard_map/ppermute | solution.py:43
  113.8 32.4 %all-to-all-start.4 = ((f32[8,64,256]{2,1,0:T(8,128)}), f32[8,64,256]{2,1,0:T(8,128)S(1)}, u32[]{:S(2)}, u32[]{:S(2)}) async-start(f32[8,64,256]{2,1,0:T(8,128)} %bitcast.56), calls=%async_computation.5 | async-start | bytes 1048576 | tf_op jit(solution)/shard_map/all_to_all | solution.py:314
  147.0 75.7 %all-to-all-start.3 = ((bf16[8,96,2048]{2,1,0:T(8,128)(2,1)}), bf16[8,96,2048]{2,1,0:T(8,128)(2,1)S(1)}, u32[]{:S(2)}, u32[]{:S(2)}) async-start(bf16[8,96,2048]{2,1,0:T(8,128)(2,1)} %bitcast.51), calls=%async_computation.3 | async-start | bytes 6291456 | tf_op jit(solution)/shard_map/all_to_all | solution.py:309
  153.3 15.0 %collective-permute-start.2 = (bf16[1024,256]{1,0:T(8,128)(2,1)S(1)}, bf16[1024,256]{1,0:T(8,128)(2,1)}, u32[]{:S(2)}, u32[]{:S(2)}) collective-permute-start(bf16[1024,256]{1,0:T(8,128)(2,1)S(1)} %get-tuple-element.31), channel_id=1, source_target_pairs={{0,3},{1,0},{2,1},{3,2},{4,7},{5,4},{6,5},{7,6},{8,11},{9,8},{10,9... | collective-permute-start | bytes 1572872 | tf_op jit(solution)/shard_map/ppermute | solution.py:43
  154.1 26.2 %collective-permute-start = (bf16[1024,256]{1,0:T(8,128)(2,1)S(1)}, bf16[1024,256]{1,0:T(8,128)(2,1)}, u32[]{:S(2)}, u32[]{:S(2)}) collective-permute-start(bf16[1024,256]{1,0:T(8,128)(2,1)S(1)} %get-tuple-element.32), channel_id=1, source_target_pairs={{0,1},{1,2},{2,3},{3,0},{4,5},{5,6},{6,7},{7,4},{8,9},{9,10},{10,1... | collective-permute-start | bytes 1572872 | tf_op jit(solution)/shard_map/ppermute | solution.py:43
  155.4 25.0 %collective-permute-start.1 = (bf16[1024,256]{1,0:T(8,128)(2,1)S(1)}, bf16[1024,256]{1,0:T(8,128)(2,1)}, u32[]{:S(2)}, u32[]{:S(2)}) collective-permute-start(bf16[1024,256]{1,0:T(8,128)(2,1)S(1)} %get-tuple-element.33), channel_id=1, source_target_pairs={{0,2},{1,3},{2,0},{3,1},{4,6},{5,7},{6,4},{7,5},{8,10},{9,11},{10,... | collective-permute-start | bytes 1572872 | tf_op jit(solution)/shard_map/ppermute | solution.py:43
  168.3 14.9 %collective-permute-start.5 = (bf16[1024,256]{1,0:T(8,128)(2,1)}, bf16[1024,256]{1,0:T(8,128)(2,1)}, u32[]{:S(2)}, u32[]{:S(2)}) collective-permute-start(bf16[1024,256]{1,0:T(8,128)(2,1)} %collective-permute-done.2.m3), channel_id=1, source_target_pairs={{0,4},{4,0},{1,5},{5,1},{2,6},{6,2},{3,7},{7,3},{8,12},{12,8},{9,1... | collective-permute-start | bytes 1572872 | tf_op jit(solution)/shard_map/ppermute | solution.py:295
  180.4 2.8 %collective-permute-start.3 = (bf16[1024,256]{1,0:T(8,128)(2,1)}, bf16[1024,256]{1,0:T(8,128)(2,1)}, u32[]{:S(2)}, u32[]{:S(2)}) collective-permute-start(bf16[1024,256]{1,0:T(8,128)(2,1)} %collective-permute-done.m1), channel_id=1, source_target_pairs={{0,4},{4,0},{1,5},{5,1},{2,6},{6,2},{3,7},{7,3},{8,12},{12,8},{9,1... | collective-permute-start | bytes 1572872 | tf_op jit(solution)/shard_map/ppermute | solution.py:295
  180.4 3.0 %collective-permute-start.4 = (bf16[1024,256]{1,0:T(8,128)(2,1)}, bf16[1024,256]{1,0:T(8,128)(2,1)}, u32[]{:S(2)}, u32[]{:S(2)}) collective-permute-start(bf16[1024,256]{1,0:T(8,128)(2,1)} %collective-permute-done.1.m2), channel_id=1, source_target_pairs={{0,4},{4,0},{1,5},{5,1},{2,6},{6,2},{3,7},{7,3},{8,12},{12,8},{9,1... | collective-permute-start | bytes 1572872 | tf_op jit(solution)/shard_map/ppermute | solution.py:295
  190.1 15.0 %collective-permute-start.6 = (f32[512,256]{1,0:T(8,128)}, f32[512,256]{1,0:T(8,128)S(1)}, u32[]{:S(2)}, u32[]{:S(2)}) collective-permute-start(f32[512,256]{1,0:T(8,128)} %get-tuple-element.18), channel_id=1, source_target_pairs={{0,3},{1,0},{2,1},{3,2},{4,7},{5,4},{6,5},{7,6},{8,11},{9,8},{10,9... | collective-permute-start | bytes 1572872 | tf_op jit(solution)/shard_map/ppermute | solution.py:43
  190.3 16.6 %collective-permute-start.7 = (f32[512,256]{1,0:T(8,128)}, f32[512,256]{1,0:T(8,128)S(1)}, u32[]{:S(2)}, u32[]{:S(2)}) collective-permute-start(f32[512,256]{1,0:T(8,128)} %get-tuple-element.19), channel_id=1, source_target_pairs={{0,2},{1,3},{2,0},{3,1},{4,6},{5,7},{6,4},{7,5},{8,10},{9,11},{10,... | collective-permute-start | bytes 1572872 | tf_op jit(solution)/shard_map/ppermute | solution.py:43
  190.9 27.3 %collective-permute-start.8 = (f32[512,256]{1,0:T(8,128)}, f32[512,256]{1,0:T(8,128)S(1)}, u32[]{:S(2)}, u32[]{:S(2)}) collective-permute-start(f32[512,256]{1,0:T(8,128)} %get-tuple-element.20), channel_id=1, source_target_pairs={{0,1},{1,2},{2,3},{3,0},{4,5},{5,6},{6,7},{7,4},{8,9},{9,10},{10,1... | collective-permute-start | bytes 1572872 | tf_op jit(solution)/shard_map/ppermute | solution.py:43
  192.3 32.4 %collective-permute-start.13 = (bf16[512,256]{1,0:T(8,128)(2,1)}, bf16[512,256]{1,0:T(8,128)(2,1)}, u32[]{:S(2)}, u32[]{:S(2)}) collective-permute-start(bf16[512,256]{1,0:T(8,128)(2,1)} %param.12), channel_id=1, source_target_pairs={{0,2},{1,3},{2,0},{3,1},{4,6},{5,7},{6,4},{7,5},{8,10},{9,11},{10,... | collective-permute-start | bytes 786440 | tf_op jit(solution)/shard_map/ppermute | solution.py:43
  196.2 32.4 %collective-permute-start.12 = (bf16[512,256]{1,0:T(8,128)(2,1)}, bf16[512,256]{1,0:T(8,128)(2,1)}, u32[]{:S(2)}, u32[]{:S(2)}) collective-permute-start(bf16[512,256]{1,0:T(8,128)(2,1)} %param.12), channel_id=1, source_target_pairs={{0,1},{1,2},{2,3},{3,0},{4,5},{5,6},{6,7},{7,4},{8,9},{9,10},{10,1... | collective-permute-start | bytes 786440 | tf_op jit(solution)/shard_map/ppermute | solution.py:43
  205.1 23.6 %collective-permute-start.14 = (bf16[512,256]{1,0:T(8,128)(2,1)}, bf16[512,256]{1,0:T(8,128)(2,1)S(1)}, u32[]{:S(2)}, u32[]{:S(2)}) collective-permute-start(bf16[512,256]{1,0:T(8,128)(2,1)} %param.12), channel_id=1, source_target_pairs={{0,3},{1,0},{2,1},{3,2},{4,7},{5,4},{6,5},{7,6},{8,11},{9,8},{10,9... | collective-permute-start | bytes 786440 | tf_op jit(solution)/shard_map/ppermute | solution.py:43
  (14 other events, 53.1 us)
Sparse Core Ops, SparseCore 0:
  10.3 44.1 all-gather.1
  78.4 67.3 reduce-scatter.1
where the time goes:
time: 245 us; the launch traced here: 243 us
  waiting for transfers between devices  112 us (46%)
  starting transfers between devices  42.6 us (17%)
  Pallas kernels  28.8 us (12%)
  between operations  14.2 us (6%)
  matrix products  13.2 us (5%)
  blocking collectives  12.3 us (5%)
  other arithmetic  12.2 us (5%)
  local copies, waits for them, and re-layouts  7.76 us (3%)
    ppermute x15, waiting for transfers between devices, shift(): return lax.ppermute(v, 't', [(i, (i + k) % NT) for i in range(NT)])  58.9 us
    all_gather x1, waiting for transfers between devices, step(): all16 = lax.all_gather(both16, 'z', axis=0, tiled=True)  21.1 us
    all_to_all x1, waiting for transfers between devices, step(): parts = lax.all_to_all(up_part, 'z', 0, 0, tiled=True)  18.5 us
    ppermute x15, starting transfers between devices, shift(): return lax.ppermute(v, 't', [(i, (i + k) % NT) for i in range(NT)])  18.2 us
    dot_general x5, matrix products, dot(): return lax.dot_general(a, b, (dims, ((), ())), preferred_element_type=out)  13.2 us
    all_to_all x1, blocking collectives, step(): ret_out = lax.all_to_all(adapter_out, ('x', 'c'), 0, 0, tiled=True)  12.3 us
    all_to_all x1, waiting for transfers between devices, step(): x_rows = lax.all_to_all(x_send, ('x', 'c'), 0, 0, tiled=True)  9.2 us
    all_to_all x1, starting transfers between devices, step(): parts = lax.all_to_all(up_part, 'z', 0, 0, tiled=True)  8.45 us
  transfers between devices with their start and end apart: 24, of which 14 were waited for; matrix products, arithmetic and copies ran while one was open for 10% of the time, Pallas kernels for 9%

commit v1 on v0

--- a/solution.py
+++ b/solution.py
@@ -150,25 +150,57 @@
     grad[...] = dot(cols[...], g[...])
 
 
-def base_kernel(c, tokens, own, m1, m2, m3, o1, o2, o3, w, p0, p1, p2, p3):
-    half = m1.shape[0]
-    keyw = m1.shape[1]
-    w[:, :keyw] = own[...]
-    for k, (m, o) in enumerate(((m1, o1), (m2, o2), (m3, o3))):
-        cols = pl.ds((k + 1) * keyw, keyw)
-
-        @pl.when(c[0] == 0)
-        def _():
-            w[:half, cols] = m[...]
-            w[half:, cols] = o[...]
-
-        @pl.when(c[0] == 1)
-        def _():
-            w[:half, cols] = o[...]
-            w[half:, cols] = m[...]
-
-    for k, p in enumerate((p0, p1, p2, p3)):
-        p[...] = dot(tokens[...], w[:, k * keyw : (k + 1) * keyw])
+def base_kernel(at, tokens, own, *refs):
+    cots, mine, other = refs[:NT], refs[NT : 2 * NT - 1], refs[2 * NT - 1 : 3 * NT - 2]
+    grad, parts = refs[3 * NT - 2], refs[3 * NT - 1 :]
+    step = pl.program_id(0)
+
+    def half(pieces):
+        total = dot(cots[0][...], own[...], ((1,), (1,)))
+        for cot, w in zip(cots[1:], pieces):
+            total = total + dot(cot[...], w[...], ((1,), (1,)))
+        grad[...] = total
+        for part, w in zip(parts, (own,) + pieces):
+            v = dot(tokens[...], w[...])
+
+            @pl.when(step == 0)
+            def _():
+                part[...] = v
+
+            @pl.when(step != 0)
+            def _():
+                part[...] += v
+
+    @pl.when(step == at[0])
+    def _():
+        half(mine)
+
+    @pl.when(step != at[0])
+    def _():
+        half(other)
+
+
+def cast_kernel(down, up, out):
+    feat = down.shape[2]
+    out[:, :feat] = down[0].astype(bf16)
+    out[:, feat:] = up[0].astype(bf16)
+
+
+def route_kernel(counts, holder, cot, route, out):
+    n = counts.shape[1]
+    before = lax.broadcasted_iota(jnp.int32, (n, n), 0) < lax.broadcasted_iota(jnp.int32, (n, n), 1)
+    rows = jnp.broadcast_to(counts[...].astype(f32), (16, n)).astype(bf16)
+    lower = dot(rows, jnp.where(before, 1.0, 0.0).astype(bf16))[:1].astype(jnp.int32)
+    code = lower * 16 + counts[...]
+    r = lax.broadcasted_iota(jnp.int32, (ROWS, n), 0)
+    zi = sum(jnp.where(r >= q * CAP, 1, 0) for q in range(1, NZ))
+    k = (r - zi * CAP)[:, :1]
+    tok = lax.broadcasted_iota(jnp.int32, (ROWS, route.shape[1]), 1)
+    for s in range(NS):
+        mine = jnp.sum(jnp.where(holder[...] == zi * NS + s, code, 0), axis=1, keepdims=True)
+        src = jnp.where(k < (mine & 15), lax.shift_right_logical(mine, 4) + k, -1)
+        route[pl.ds(s * ROWS, ROWS), :] = jnp.where(tok == src, 1.0, 0.0).astype(bf16)
+    out[...] = dot(route[...], cot[...]).astype(bf16)
 
 
 def run_back(g_rows, all16, feat, keyw):
@@ -234,16 +266,28 @@
     )(*parts, g_rows, all16)
 
 
-def run_base(c, tokens, own, mine, other):
+def run_base(c, t, tokens, weight, cots, mine, other):
     rows, feat = tokens.shape
-    keyw = own.shape[1]
-    return call(
+    keyw = weight.shape[1]
+    half = feat // NC
+    return pl.pallas_call(
         base_kernel,
-        [jax.ShapeDtypeStruct((feat, NT * keyw), bf16)]
+        out_shape=[jax.ShapeDtypeStruct((rows, feat), f32)]
         + [jax.ShapeDtypeStruct((rows, keyw), f32)] * NT,
-        [pl.BlockSpec(memory_space=pltpu.SMEM)] + [VM] * 8,
-        [VM] * (1 + NT),
-    )(c.reshape(1), tokens, own, *mine, *other)
+        grid_spec=pltpu.PrefetchScalarGridSpec(
+            num_scalar_prefetch=1,
+            grid=(NC,),
+            in_specs=[
+                pl.BlockSpec((rows, half), lambda i, at: (0, i)),
+                pl.BlockSpec((half, keyw), lambda i, at: (at[1] * NC + i, 0)),
+            ]
+            + [whole((rows, keyw))] * NT
+            + [whole((half, keyw))] * (2 * NT - 2),
+            out_specs=[pl.BlockSpec((rows, half), lambda i, at: (0, i))]
+            + [whole((rows, keyw))] * NT,
+        ),
+        name="base_kernel",
+    )(jnp.stack([c, t]), tokens, weight, *cots, *mine, *other)
 
 
 def step(
@@ -264,25 +308,20 @@
     rank = adapter_down_matrix.shape[1]
     t = lax.axis_index("t")
     c = lax.axis_index("c")
-
-    both16 = jnp.concatenate([adapter_down_matrix[0], adapter_up_matrix[0]], axis=1).astype(bf16)
+    z = lax.axis_index("z")
+
+    both16 = call(cast_kernel, jax.ShapeDtypeStruct((rank, feat + keyw), bf16), [VM] * 2)(
+        adapter_down_matrix, adapter_up_matrix
+    )
     all16 = lax.all_gather(both16, "z", axis=0, tiled=True)
 
-    own_counts = counts[0]
-    upper = jnp.cumsum(own_counts)
-    lower = upper - own_counts
-    slot = jnp.arange(NS * ROWS, dtype=jnp.int32)
-    slot_owner = (slot % ROWS) // CAP * NS + slot // ROWS
-    slot_k = slot % CAP
-    pick = holder_assignment[None, :] == slot_owner[:, None]
-    start = jnp.sum(jnp.where(pick, lower[None, :], 0), axis=1)
-    count = jnp.sum(jnp.where(pick, own_counts[None, :], 0), axis=1)
-    source = jnp.where(slot_k < count, start + slot_k, -1)
-    route = (source[:, None] == jnp.arange(tok_rows, dtype=jnp.int32)[None, :]).astype(bf16)
-
+    route, g_send = call(
+        route_kernel,
+        [jax.ShapeDtypeStruct((R, tok_rows), bf16), jax.ShapeDtypeStruct((R, keyw), bf16)],
+        [VM] * 3,
+    )(counts, holder_assignment.reshape(1, -1), cotangent)
     x_send = dot(route, tokens, out=bf16)
     x_rows = lax.all_to_all(x_send, ("x", "c"), 0, 0, tiled=True)
-    g_send = dot(route, cotangent, out=bf16)
     g_rows = lax.all_to_all(g_send, ("x", "c"), 0, 0, tiled=True)
 
     half = feat // NC
@@ -293,12 +332,10 @@
         )
         halves.append(shift(piece, k))
     other = [lax.ppermute(v, "c", [(0, 1), (1, 0)]) for v in halves]
-    own_w = lax.dynamic_slice(frozen_key_weight, (t * feat, 0), (feat, keyw))
-    weight, base_out, *outs = run_base(c, tokens, own_w, halves, other)
+    cots = [cotangent] + [shift(cotangent, k) for k in range(1, NT)]
+    base_grad, base_out, *outs = run_base(c, t, tokens, frozen_key_weight, cots, halves, other)
     for k in range(1, NT):
         base_out = base_out + shift(outs[k - 1], -k)
-    cots = [cotangent] + [shift(cotangent, k) for k in range(1, NT)]
-    base_grad = dot(jnp.concatenate(cots, axis=1), weight, ((1,), (1,)))
 
     def parts_of(own):
         return [own] + [shift(own, k) for k in range(1, NT)]
@@ -311,8 +348,14 @@
     hidden = parts_of(run_hid(x_rows, all16))
     adapter_out, up_part = run_up(hidden, g_rows, all16, feat)
     ret_out = lax.all_to_all(adapter_out, ("x", "c"), 0, 0, tiled=True)
-    parts = lax.all_to_all(up_part, "z", 0, 0, tiled=True)
-    grad_up = jnp.sum(parts.reshape(NZ, rank, keyw), axis=0)
+    grad_up = up_part
+    for bit in range(3):
+        split = grad_up.reshape(-1, 2, rank, keyw)
+        here = lax.shift_right_logical(z, bit) & 1
+        keep = lax.dynamic_index_in_dim(split, here, 1, keepdims=False)
+        give = lax.dynamic_index_in_dim(split, 1 - here, 1, keepdims=False)
+        grad_up = keep + lax.ppermute(give, "z", [(i, i ^ (1 << bit)) for i in range(NZ)])
+    grad_up = grad_up.reshape(rank, keyw)
 
     layer_out = (base_out + dot(route, ret_out, ((0,), (0,)))).astype(bf16)
     input_grad = (base_grad + dot(route, ret_grad, ((0,), (0,)))).astype(bf16)

time: 245 us -> 220 us (0.90)
  waiting for transfers between devices: 112 us -> 92.4 us
  blocking collectives: 12.3 us -> 0 us
  Pallas kernels: 28.8 us -> 40.2 us
  starting transfers between devices: 42.6 us -> 48.3 us
  other arithmetic: 12.2 us -> 7.68 us
  matrix products: 13.2 us -> 9.95 us
    all_to_all x1, waiting for transfers between devices: 18.5 us -> 2.08 us  [step(): ret_out = lax.all_to_all(adapter_out, ('x', 'c'), 0, 0, tiled=True)]
    all_to_all x1 -> x0, blocking collectives: 12.3 us -> none  [step(): ret_out = lax.all_to_all(adapter_out, ('x', 'c'), 0, 0, tiled=True)]
    ppermute x0 -> x3, starting transfers between devices: none -> 12.2 us  [step(): lax.ppermute(give, 'z', [(i, i ^ 1 << bit) for i in range(NZ)])]
    pallas_call x1 -> x3, Pallas kernels: 6.69 us -> 18 us  [the longest x1 13.7 us: run_base(): pl.pallas_call(base_kernel, out_shape=[jax.ShapeDtypeStruct((rows, feat),...]
    ppermute x15, waiting for transfers between devices: 58.9 us -> 53.3 us  [shift(): return lax.ppermute(v, 't', [(i, (i + k) % NT) for i in range(NT)])]
    ppermute x0 -> x3, waiting for transfers between devices: none -> 4.38 us  [step(): lax.ppermute(give, 'z', [(i, i ^ 1 << bit) for i in range(NZ)])]
    all_to_all x1, starting transfers between devices: 8.45 us -> 4.82 us  [step(): ret_out = lax.all_to_all(adapter_out, ('x', 'c'), 0, 0, tiled=True)]
    dot_general x5 -> x3, matrix products: 13.2 us -> 9.95 us  [dot(): return lax.dot_general(a, b, (dims, ((), ())), preferred_element_type=out)]
  transfers between devices with their start and end apart: 24 -> 27, of which waited for: 14 -> 16; matrix products, arithmetic and copies ran while one was open for 10% -> 8% of each run, Pallas kernels for 9% -> 15%
where the time goes in v1:
time: 220 us; the launch traced here: 218 us
  waiting for transfers between devices  92.4 us (42%)
  starting transfers between devices  48.3 us (22%)
  Pallas kernels  40.2 us (18%)
  between operations  14.2 us (6%)
  matrix products  9.95 us (5%)
  other arithmetic  7.68 us (3%)
  local copies, waits for them, and re-layouts  5.56 us (3%)
    ppermute x15, waiting for transfers between devices, shift(): return lax.ppermute(v, 't', [(i, (i + k) % NT) for i in range(NT)])  53.3 us
    all_gather x1, waiting for transfers between devices, step(): all16 = lax.all_gather(both16, 'z', axis=0, tiled=True)  24.1 us
    ppermute x15, starting transfers between devices, shift(): return lax.ppermute(v, 't', [(i, (i + k) % NT) for i in range(NT)])  15.6 us
    pallas_call x1, Pallas kernels, run_base(): pl.pallas_call(base_kernel, out_shape=[jax.ShapeDtypeStruct((rows, feat),...  13.7 us
    ppermute x3, starting transfers between devices, step(): lax.ppermute(give, 'z', [(i, i ^ 1 << bit) for i in range(NZ)])  12.2 us
    dot_general x3, matrix products, dot(): return lax.dot_general(a, b, (dims, ((), ())), preferred_element_type=out)  9.95 us
    all_to_all x1, waiting for transfers between devices, step(): x_rows = lax.all_to_all(x_send, ('x', 'c'), 0, 0, tiled=True)  6.22 us
    pallas_call x1, Pallas kernels, run_grad(): call(grad_kernel, [jax.ShapeDtypeStruct((R, WIDE), bf16), jax.ShapeDtypeS...  6.15 us
  transfers between devices with their start and end apart: 27, of which 16 were waited for; matrix products, arithmetic and copies ran while one was open for 8% of the time, Pallas kernels for 15%

profile of v1, /device:TPU:2, one launch (start us, length us, event | category | flops | bytes accessed | tf_op | source)
XLA Modules:
  0.0 218.3 jit_solution(220376027344372496)
XLA Ops:
  11.6 5.6 %all-to-all-start.1 = ((bf16[8,96,256]{2,1,0:T(8,128)(2,1)}), bf16[8,96,256]{2,1,0:T(8,128)(2,1)S(1)}, u32[]{:S(2)}, u32[]{:S(2)}) async-start(bf16[8,96,256]{2,1,0:T(8,128)(2,1)} %bitcast.62), calls=%async_computation.1 | async-start | bytes 786432 | tf_op jit(solution)/shard_map/all_to_all | solution.py:325
  17.2 5.3 %fusion.4 = bf16[768,2048]{1,0:T(8,128)(2,1)} fusion(bf16[768,512]{1,0:T(8,128)(2,1)} %get-tuple-element.23, bf16[512,2048]{1,0:T(8,128)(2,1)} %tokens.1), kind=kOutput, calls=%fused_computation.22 | convolution fusion | flops 1610612736 | bytes 6029312 | tf_op jit(solution)/shard_map/dot_general | solution.py:47
  25.4 5.0 %all-to-all-start = ((bf16[8,96,2048]{2,1,0:T(8,128)(2,1)}), bf16[8,96,2048]{2,1,0:T(8,128)(2,1)S(1)}, u32[]{:S(2)}, u32[]{:S(2)}) async-start(bf16[8,96,2048]{2,1,0:T(8,128)(2,1)} %bitcast.55), calls=%async_computation | async-start | bytes 6291456 | tf_op jit(solution)/shard_map/all_to_all | solution.py:324
  30.4 24.1 %all-gather.2.cloned.1.call-done.down.up = bf16[512,2304]{1,0:T(8,128)(2,1)} async-done(((bf16[64,2304]{1,0:T(8,128)(2,1)}), bf16[512,2304]{1,0:T(8,128)(2,1)}) %all-gather.2.cloned.1.call-update) | async-done | bytes 2359312 | tf_op jit(solution)/shard_map/all_gather | solution.py:316
  56.7 2.7 %collective-permute-start.17 = (f32[384,128]{1,0:T(8,128)}, f32[384,128]{1,0:T(8,128)S(1)}, u32[]{:S(2)}, u32[]{:S(2)}) collective-permute-start(f32[384,128]{1,0:T(8,128)} %shard_map.174.a), channel_id=1, source_target_pairs={{0,3},{1,0},{2,1},{3,2},{4,7},{5,4},{6,5},{7,6},{8,11},{9,8},{10,9... | collective-permute-start | bytes 589832 | tf_op jit(solution)/shard_map/ppermute | solution.py:43
  61.2 6.2 %all-to-all-done = bf16[8,96,2048]{2,1,0:T(8,128)(2,1)S(1)} async-done(((bf16[8,96,2048]{2,1,0:T(8,128)(2,1)}), bf16[8,96,2048]{2,1,0:T(8,128)(2,1)S(1)}, u32[]{:S(2)}, u32[]{:S(2)}) %all-to-all-start) | async-done | bytes 3145760 | tf_op jit(solution)/shard_map/all_to_all | solution.py:324
  69.2 6.1 %shard_map.175 = (bf16[768,512]{1,0:T(8,128)(2,1)}, f32[512,2048]{1,0:T(8,128)}) custom-call(f32[384,128]{1,0:T(8,128)} %shard_map.174.a, f32[384,128]{1,0:T(8,128)} %collective-permute-done.15.b, f32[384,128]{1,0:T(8,128)} %copy-done.15, f32[384,128]{1,0:T(8,128)} %copy-done.14, bf16[768,2048]{1,0:T(8,128)(2,1)} %bitcast.49), custom_call_target="tpu_custom_call" | custom-call | tf_op jit(solution)/shard_map/pallas_call | solution.py:219
  75.3 5.5 %shard_map.172.a = f32[384,128]{1,0:T(8,128)} custom-call(bf16[768,2048]{1,0:T(8,128)(2,1)} %bitcast.50, bf16[512,2304]{1,0:T(8,128)(2,1)} %all-gather.2.cloned.1.call-done.down.up), custom_call_target="tpu_custom_call" | custom-call | tf_op jit(solution)/shard_map/pallas_call | solution.py:243
  84.6 6.8 %collective-permute-done.14.d = f32[384,128]{1,0:T(8,128)S(1)} collective-permute-done((f32[384,128]{1,0:T(8,128)}, f32[384,128]{1,0:T(8,128)S(1)}, u32[]{:S(2)}, u32[]{:S(2)}) %collective-permute-start.14) | collective-permute-done | bytes 196640 | tf_op jit(solution)/shard_map/ppermute | solution.py:43
  95.7 2.9 %shard_map.173 = (bf16[768,256]{1,0:T(8,128)(2,1)}, f32[512,256]{1,0:T(8,128)}) custom-call(f32[384,128]{1,0:T(8,128)} %shard_map.172.a, f32[384,128]{1,0:T(8,128)} %copy-done.13, f32[384,128]{1,0:T(8,128)} %copy-done.12, f32[384,128]{1,0:T(8,128)} %copy-done.11, bf16[768,256]{1,0:T(8,128)(2,1)} %bitcast.54, ...), custom_call_target="tpu_custom_call" | custom-call | tf_op jit(solution)/shard_map/pallas_call | solution.py:258
  98.7 4.8 %all-to-all-start.2 = ((bf16[8,96,256]{2,1,0:T(8,128)(2,1)}), bf16[8,96,256]{2,1,0:T(8,128)(2,1)S(1)}, u32[]{:S(2)}, u32[]{:S(2)}) async-start(bf16[8,96,256]{2,1,0:T(8,128)(2,1)} %bitcast.61), calls=%async_computation.2 | async-start | bytes 786432 | tf_op jit(solution)/shard_map/all_to_all | solution.py:350
  103.5 5.4 %shard_map.176 = bf16[768,2048]{1,0:T(8,128)(2,1)} custom-call(bf16[768,512]{1,0:T(8,128)(2,1)} %get-tuple-element.27.back16, bf16[512,2304]{1,0:T(8,128)(2,1)} %all-gather.2.cloned.1.call-done.down.up), custom_call_target="tpu_custom_call" | custom-call | tf_op jit(solution)/shard_map/pallas_call | solution.py:231
  111.7 5.0 %all-to-all-start.3 = ((bf16[8,96,2048]{2,1,0:T(8,128)(2,1)}), bf16[8,96,2048]{2,1,0:T(8,128)(2,1)S(1)}, u32[]{:S(2)}, u32[]{:S(2)}) async-start(bf16[8,96,2048]{2,1,0:T(8,128)(2,1)} %bitcast.52), calls=%async_computation.3 | async-start | bytes 6291456 | tf_op jit(solution)/shard_map/all_to_all | solution.py:346
  120.4 2.7 %collective-permute-start.2 = (bf16[512,256]{1,0:T(8,128)(2,1)S(1)}, bf16[512,256]{1,0:T(8,128)(2,1)}, u32[]{:S(2)}, u32[]{:S(2)}) collective-permute-start(bf16[512,256]{1,0:T(8,128)(2,1)S(1)} %copy-done.4), channel_id=1, source_target_pairs={{0,3},{1,0},{2,1},{3,2},{4,7},{5,4},{6,5},{7,6},{8,11},{9,8},{10,9... | collective-permute-start | bytes 786440 | tf_op jit(solution)/shard_map/ppermute | solution.py:43
  123.0 10.2 %collective-permute-done.5.refs_6_ = bf16[1024,256]{1,0:T(8,128)(2,1)} collective-permute-done((bf16[1024,256]{1,0:T(8,128)(2,1)S(1)}, bf16[1024,256]{1,0:T(8,128)(2,1)}, u32[]{:S(2)}, u32[]{:S(2)}) %collective-permute-start.5) | collective-permute-done | bytes 524320 | tf_op jit(solution)/shard_map/ppermute | solution.py:43
  135.5 10.0 %collective-permute-done.3.refs_4_ = bf16[1024,256]{1,0:T(8,128)(2,1)} collective-permute-done((bf16[1024,256]{1,0:T(8,128)(2,1)S(1)}, bf16[1024,256]{1,0:T(8,128)(2,1)}, u32[]{:S(2)}, u32[]{:S(2)}) %collective-permute-start.3) | collective-permute-done | bytes 524320 | tf_op jit(solution)/shard_map/ppermute | solution.py:43
  146.1 3.3 %collective-permute-done.2.refs_3_ = bf16[512,256]{1,0:T(8,128)(2,1)} collective-permute-done((bf16[512,256]{1,0:T(8,128)(2,1)S(1)}, bf16[512,256]{1,0:T(8,128)(2,1)}, u32[]{:S(2)}, u32[]{:S(2)}) %collective-permute-start.2) | collective-permute-done | bytes 262176 | tf_op jit(solution)/shard_map/ppermute | solution.py:43
  151.0 5.4 %collective-permute-done.1.refs_2_ = bf16[512,256]{1,0:T(8,128)(2,1)} collective-permute-done((bf16[512,256]{1,0:T(8,128)(2,1)S(1)}, bf16[512,256]{1,0:T(8,128)(2,1)}, u32[]{:S(2)}, u32[]{:S(2)}) %collective-permute-start.1) | collective-permute-done | bytes 262176 | tf_op jit(solution)/shard_map/ppermute | solution.py:43
  161.5 13.7 %base_kernel.1 = (f32[512,2048]{1,0:T(8,128)}, f32[512,256]{1,0:T(8,128)}, f32[512,256]{1,0:T(8,128)}, f32[512,256]{1,0:T(8,128)}, f32[512,256]{1,0:T(8,128)}) custom-call(s32[2]{0:T(128)} %pad_add_fusion.at, bf16[512,2048]{1,0:T(8,128)(2,1)} %tokens.1, bf16[8192,256]{1,0:T(8,128)(2,1)} %own.1, bf16[512,256]{1,0:T(8,128)(2,1)} %cot.1, ...), custom_call_target="tpu_custom_call" | custom-call | tf_op jit(solution)/shard_map/base_kernel/pallas_call | solution.py:273
  178.4 3.4 %collective-permute-start.19 = (f32[2,64,256]{2,1,0:T(8,128)S(1)}, f32[2,64,256]{2,1,0:T(8,128)S(1)}, u32[]{:S(2)}, u32[]{:S(2)}) collective-permute-start(f32[2,64,256]{2,1,0:T(8,128)S(1)} %dynamic-slice_bitcast_fusion.1), channel_id=1, source_target_pairs={{0,64},{32,96},{64,0},{96,32},{128,192},{160,224},{192,128},{224,1... | collective-permute-start | bytes 393224 | tf_op jit(solution)/shard_map/ppermute | solution.py:357
  183.4 4.4 %collective-permute-done.19 = f32[2,64,256]{2,1,0:T(8,128)S(1)} collective-permute-done((f32[2,64,256]{2,1,0:T(8,128)S(1)}, f32[2,64,256]{2,1,0:T(8,128)S(1)}, u32[]{:S(2)}, u32[]{:S(2)}) %collective-permute-start.19) | collective-permute-done | bytes 131104 | tf_op jit(solution)/shard_map/ppermute | solution.py:357
  187.8 6.9 %collective-permute-start.20 = (f32[1,64,256]{2,1,0:T(8,128)S(1)}, f32[1,64,256]{2,1,0:T(8,128)S(1)}, u32[]{:S(2)}, u32[]{:S(2)}) collective-permute-start(f32[1,64,256]{2,1,0:T(8,128)S(1)} %constant_dynamic-slice_fusion), channel_id=1, source_target_pairs={{0,128},{32,160},{64,192},{96,224},{128,0},{160,32},{192,64},{224,... | collective-permute-start | bytes 196616 | tf_op jit(solution)/shard_map/ppermute | solution.py:357
  194.6 7.6 %collective-permute-done.11 = f32[512,256]{1,0:T(8,128)S(1)} collective-permute-done((f32[512,256]{1,0:T(8,128)}, f32[512,256]{1,0:T(8,128)S(1)}, u32[]{:S(2)}, u32[]{:S(2)}) %collective-permute-start.11) | collective-permute-done | bytes 524320 | tf_op jit(solution)/shard_map/ppermute | solution.py:43
  203.8 3.1 %fusion.6 = f32[512,2048]{1,0:T(8,128)S(1)} fusion(bf16[768,512]{1,0:T(8,128)(2,1)} %get-tuple-element.23, bf16[768,2048]{1,0:T(8,128)(2,1)S(1)} %bitcast.51), kind=kOutput, calls=%fused_computation.24 | convolution fusion | flops 1610612736 | bytes 8126464 | tf_op jit(solution)/shard_map/dot_general | solution.py:47
  (90 shorter events, 48.0 us)
Async XLA Ops:
  7.2 47.3 %all-gather.2.cloned.1.call-start = ((), (), s32[]{:S(2)}) async-start(), calls=%async_computation.5 | async-start | bytes 2654208 | tf_op jit(solution)/shard_map/all_gather | solution.py:316
  11.6 13.1 %all-to-all-start.1 = ((bf16[8,96,256]{2,1,0:T(8,128)(2,1)}), bf16[8,96,256]{2,1,0:T(8,128)(2,1)S(1)}, u32[]{:S(2)}, u32[]{:S(2)}) async-start(bf16[8,96,256]{2,1,0:T(8,128)(2,1)} %bitcast.62), calls=%async_computation.1 | async-start | bytes 786432 | tf_op jit(solution)/shard_map/all_to_all | solution.py:325
  25.4 42.0 %all-to-all-start = ((bf16[8,96,2048]{2,1,0:T(8,128)(2,1)}), bf16[8,96,2048]{2,1,0:T(8,128)(2,1)S(1)}, u32[]{:S(2)}, u32[]{:S(2)}) async-start(bf16[8,96,2048]{2,1,0:T(8,128)(2,1)} %bitcast.55), calls=%async_computation | async-start | bytes 6291456 | tf_op jit(solution)/shard_map/all_to_all | solution.py:324
  30.4 178.5 %reduce-scatter.2.cloned.1.call-start = ((), (), s32[]{:S(2)}) async-start(), calls=%async_computation.6 | async-start | bytes 4718592 | tf_op jit(solution)/shard_map/reduce_scatter | solution.py:344
  56.7 10.7 %collective-permute-start.17 = (f32[384,128]{1,0:T(8,128)}, f32[384,128]{1,0:T(8,128)S(1)}, u32[]{:S(2)}, u32[]{:S(2)}) collective-permute-start(f32[384,128]{1,0:T(8,128)} %shard_map.174.a), channel_id=1, source_target_pairs={{0,3},{1,0},{2,1},{3,2},{4,7},{5,4},{6,5},{7,6},{8,11},{9,8},{10,9... | collective-permute-start | bytes 589832 | tf_op jit(solution)/shard_map/ppermute | solution.py:43
  80.8 10.7 %collective-permute-start.14 = (f32[384,128]{1,0:T(8,128)}, f32[384,128]{1,0:T(8,128)S(1)}, u32[]{:S(2)}, u32[]{:S(2)}) collective-permute-start(f32[384,128]{1,0:T(8,128)} %shard_map.172.a), channel_id=1, source_target_pairs={{0,3},{1,0},{2,1},{3,2},{4,7},{5,4},{6,5},{7,6},{8,11},{9,8},{10,9... | collective-permute-start | bytes 589832 | tf_op jit(solution)/shard_map/ppermute | solution.py:43
  83.0 9.5 %collective-permute-start.13 = (f32[384,128]{1,0:T(8,128)}, f32[384,128]{1,0:T(8,128)S(1)}, u32[]{:S(2)}, u32[]{:S(2)}) collective-permute-start(f32[384,128]{1,0:T(8,128)} %shard_map.172.a), channel_id=1, source_target_pairs={{0,2},{1,3},{2,0},{3,1},{4,6},{5,7},{6,4},{7,5},{8,10},{9,11},{10,... | collective-permute-start | bytes 589832 | tf_op jit(solution)/shard_map/ppermute | solution.py:43
  83.7 11.4 %collective-permute-start.12 = (f32[384,128]{1,0:T(8,128)}, f32[384,128]{1,0:T(8,128)S(1)}, u32[]{:S(2)}, u32[]{:S(2)}) collective-permute-start(f32[384,128]{1,0:T(8,128)} %shard_map.172.a), channel_id=1, source_target_pairs={{0,1},{1,2},{2,3},{3,0},{4,5},{5,6},{6,7},{7,4},{8,9},{9,10},{10,1... | collective-permute-start | bytes 589832 | tf_op jit(solution)/shard_map/ppermute | solution.py:43
  98.7 12.3 %all-to-all-start.2 = ((bf16[8,96,256]{2,1,0:T(8,128)(2,1)}), bf16[8,96,256]{2,1,0:T(8,128)(2,1)S(1)}, u32[]{:S(2)}, u32[]{:S(2)}) async-start(bf16[8,96,256]{2,1,0:T(8,128)(2,1)} %bitcast.61), calls=%async_computation.2 | async-start | bytes 786432 | tf_op jit(solution)/shard_map/all_to_all | solution.py:350
  111.7 92.1 %all-to-all-start.3 = ((bf16[8,96,2048]{2,1,0:T(8,128)(2,1)}), bf16[8,96,2048]{2,1,0:T(8,128)(2,1)S(1)}, u32[]{:S(2)}, u32[]{:S(2)}) async-start(bf16[8,96,2048]{2,1,0:T(8,128)(2,1)} %bitcast.52), calls=%async_computation.3 | async-start | bytes 6291456 | tf_op jit(solution)/shard_map/all_to_all | solution.py:346
  118.2 15.0 %collective-permute-start.5 = (bf16[1024,256]{1,0:T(8,128)(2,1)S(1)}, bf16[1024,256]{1,0:T(8,128)(2,1)}, u32[]{:S(2)}, u32[]{:S(2)}) collective-permute-start(bf16[1024,256]{1,0:T(8,128)(2,1)S(1)} %get-tuple-element.33), channel_id=1, source_target_pairs={{0,3},{1,0},{2,1},{3,2},{4,7},{5,4},{6,5},{7,6},{8,11},{9,8},{10,9... | collective-permute-start | bytes 1572872 | tf_op jit(solution)/shard_map/ppermute | solution.py:43
  119.0 16.5 %collective-permute-start.4 = (bf16[1024,256]{1,0:T(8,128)(2,1)S(1)}, bf16[1024,256]{1,0:T(8,128)(2,1)}, u32[]{:S(2)}, u32[]{:S(2)}) collective-permute-start(bf16[1024,256]{1,0:T(8,128)(2,1)S(1)} %get-tuple-element.34), channel_id=1, source_target_pairs={{0,2},{1,3},{2,0},{3,1},{4,6},{5,7},{6,4},{7,5},{8,10},{9,11},{10,... | collective-permute-start | bytes 1572872 | tf_op jit(solution)/shard_map/ppermute | solution.py:43
  119.5 26.0 %collective-permute-start.3 = (bf16[1024,256]{1,0:T(8,128)(2,1)S(1)}, bf16[1024,256]{1,0:T(8,128)(2,1)}, u32[]{:S(2)}, u32[]{:S(2)}) collective-permute-start(bf16[1024,256]{1,0:T(8,128)(2,1)S(1)} %get-tuple-element.35), channel_id=1, source_target_pairs={{0,1},{1,2},{2,3},{3,0},{4,5},{5,6},{6,7},{7,4},{8,9},{9,10},{10,1... | collective-permute-start | bytes 1572872 | tf_op jit(solution)/shard_map/ppermute | solution.py:43
  120.4 29.0 %collective-permute-start.2 = (bf16[512,256]{1,0:T(8,128)(2,1)S(1)}, bf16[512,256]{1,0:T(8,128)(2,1)}, u32[]{:S(2)}, u32[]{:S(2)}) collective-permute-start(bf16[512,256]{1,0:T(8,128)(2,1)S(1)} %copy-done.4), channel_id=1, source_target_pairs={{0,3},{1,0},{2,1},{3,2},{4,7},{5,4},{6,5},{7,6},{8,11},{9,8},{10,9... | collective-permute-start | bytes 786440 | tf_op jit(solution)/shard_map/ppermute | solution.py:43
  133.2 28.3 %collective-permute-start.8 = (bf16[1024,256]{1,0:T(8,128)(2,1)}, bf16[1024,256]{1,0:T(8,128)(2,1)}, u32[]{:S(2)}, u32[]{:S(2)}) collective-permute-start(bf16[1024,256]{1,0:T(8,128)(2,1)} %collective-permute-done.5.refs_6_), channel_id=1, source_target_pairs={{0,4},{4,0},{1,5},{5,1},{2,6},{6,2},{3,7},{7,3},{8,12},{12,8},{9,1... | collective-permute-start | bytes 1572872 | tf_op jit(solution)/shard_map/ppermute | solution.py:334
  135.5 26.0 %collective-permute-start.7 = (bf16[1024,256]{1,0:T(8,128)(2,1)}, bf16[1024,256]{1,0:T(8,128)(2,1)}, u32[]{:S(2)}, u32[]{:S(2)}) collective-permute-start(bf16[1024,256]{1,0:T(8,128)(2,1)} %collective-permute-done.4.refs_5_), channel_id=1, source_target_pairs={{0,4},{4,0},{1,5},{5,1},{2,6},{6,2},{3,7},{7,3},{8,12},{12,8},{9,1... | collective-permute-start | bytes 1572872 | tf_op jit(solution)/shard_map/ppermute | solution.py:334
  145.5 16.0 %collective-permute-start.6 = (bf16[1024,256]{1,0:T(8,128)(2,1)}, bf16[1024,256]{1,0:T(8,128)(2,1)}, u32[]{:S(2)}, u32[]{:S(2)}) collective-permute-start(bf16[1024,256]{1,0:T(8,128)(2,1)} %collective-permute-done.3.refs_4_), channel_id=1, source_target_pairs={{0,4},{4,0},{1,5},{5,1},{2,6},{6,2},{3,7},{7,3},{8,12},{12,8},{9,1... | collective-permute-start | bytes 1572872 | tf_op jit(solution)/shard_map/ppermute | solution.py:334
  145.6 10.8 %collective-permute-start.1 = (bf16[512,256]{1,0:T(8,128)(2,1)S(1)}, bf16[512,256]{1,0:T(8,128)(2,1)}, u32[]{:S(2)}, u32[]{:S(2)}) collective-permute-start(bf16[512,256]{1,0:T(8,128)(2,1)S(1)} %copy-done.4), channel_id=1, source_target_pairs={{0,2},{1,3},{2,0},{3,1},{4,6},{5,7},{6,4},{7,5},{8,10},{9,11},{10,... | collective-permute-start | bytes 786440 | tf_op jit(solution)/shard_map/ppermute | solution.py:43
  149.3 12.1 %collective-permute-start = (bf16[512,256]{1,0:T(8,128)(2,1)S(1)}, bf16[512,256]{1,0:T(8,128)(2,1)}, u32[]{:S(2)}, u32[]{:S(2)}) collective-permute-start(bf16[512,256]{1,0:T(8,128)(2,1)S(1)} %copy-done.4), channel_id=1, source_target_pairs={{0,1},{1,2},{2,3},{3,0},{4,5},{5,6},{6,7},{7,4},{8,9},{9,10},{10,1... | collective-permute-start | bytes 786440 | tf_op jit(solution)/shard_map/ppermute | solution.py:43
  156.4 21.0 %collective-permute-start.18 = (f32[4,64,256]{2,1,0:T(8,128)}, f32[4,64,256]{2,1,0:T(8,128)}, u32[]{:S(2)}, u32[]{:S(2)}) collective-permute-start(f32[4,64,256]{2,1,0:T(8,128)} %dynamic-slice_bitcast_fusion), channel_id=1, source_target_pairs={{0,32},{32,0},{64,96},{96,64},{128,160},{160,128},{192,224},{224,1... | collective-permute-start | bytes 786440 | tf_op jit(solution)/shard_map/ppermute | solution.py:357
  175.2 19.4 %collective-permute-start.9 = (f32[512,256]{1,0:T(8,128)}, f32[512,256]{1,0:T(8,128)S(1)}, u32[]{:S(2)}, u32[]{:S(2)}) collective-permute-start(f32[512,256]{1,0:T(8,128)} %get-tuple-element.20), channel_id=1, source_target_pairs={{0,3},{1,0},{2,1},{3,2},{4,7},{5,4},{6,5},{7,6},{8,11},{9,8},{10,9... | collective-permute-start | bytes 1572872 | tf_op jit(solution)/shard_map/ppermute | solution.py:43
  175.9 18.7 %collective-permute-start.10 = (f32[512,256]{1,0:T(8,128)}, f32[512,256]{1,0:T(8,128)S(1)}, u32[]{:S(2)}, u32[]{:S(2)}) collective-permute-start(f32[512,256]{1,0:T(8,128)} %get-tuple-element.21), channel_id=1, source_target_pairs={{0,2},{1,3},{2,0},{3,1},{4,6},{5,7},{6,4},{7,5},{8,10},{9,11},{10,... | collective-permute-start | bytes 1572872 | tf_op jit(solution)/shard_map/ppermute | solution.py:43
  176.4 25.8 %collective-permute-start.11 = (f32[512,256]{1,0:T(8,128)}, f32[512,256]{1,0:T(8,128)S(1)}, u32[]{:S(2)}, u32[]{:S(2)}) collective-permute-start(f32[512,256]{1,0:T(8,128)} %get-tuple-element.22), channel_id=1, source_target_pairs={{0,1},{1,2},{2,3},{3,0},{4,5},{5,6},{6,7},{7,4},{8,9},{9,10},{10,1... | collective-permute-start | bytes 1572872 | tf_op jit(solution)/shard_map/ppermute | solution.py:43
  187.8 15.3 %collective-permute-start.20 = (f32[1,64,256]{2,1,0:T(8,128)S(1)}, f32[1,64,256]{2,1,0:T(8,128)S(1)}, u32[]{:S(2)}, u32[]{:S(2)}) collective-permute-start(f32[1,64,256]{2,1,0:T(8,128)S(1)} %constant_dynamic-slice_fusion), channel_id=1, source_target_pairs={{0,128},{32,160},{64,192},{96,224},{128,0},{160,32},{192,64},{224,... | collective-permute-start | bytes 196616 | tf_op jit(solution)/shard_map/ppermute | solution.py:357
  (21 other events, 183.1 us)
Sparse Core Ops, SparseCore 0:
  10.3 44.1 all-gather.1
  75.5 56.5 reduce-scatter.1

commit v2 on v1

--- a/solution.py
+++ b/solution.py
@@ -126,20 +126,24 @@
     grad[...] = dot(cols[...], x[...])
 
 
-def adg_kernel(back16, down, out):
-    out[...] = dot(back16[...], down[...]).astype(bf16)
-
-
-def hid_kernel(x, down, out, acc):
+def adg_kernel(back16, first, second, out):
     @pl.when(pl.program_id(0) == 0)
     def _():
-        acc[...] = jnp.zeros_like(acc)
-
-    acc[...] += dot(x[...], down[...], ((1,), (1,)))
-
-    @pl.when(pl.program_id(0) == pl.num_programs(0) - 1)
-    def _():
-        out[...] = fold(acc[...])
+        out[...] = dot(back16[...], first[...]).astype(bf16)
+
+    @pl.when(pl.program_id(0) == 1)
+    def _():
+        out[...] = dot(back16[...], second[...]).astype(bf16)
+
+
+def hid_kernel(x, first, second, out, acc):
+    @pl.when(pl.program_id(0) == 0)
+    def _():
+        acc[...] = dot(x[...], first[...], ((1,), (1,)))
+
+    @pl.when(pl.program_id(0) == 1)
+    def _():
+        out[...] = fold(acc[...] + dot(x[...], second[...], ((1,), (1,))))
 
 
 def up_kernel(a, b, c, d, g, up, out, grad, rows, cols):
@@ -180,10 +184,18 @@
         half(other)
 
 
-def cast_kernel(down, up, out):
-    feat = down.shape[2]
-    out[:, :feat] = down[0].astype(bf16)
-    out[:, feat:] = up[0].astype(bf16)
+def cast_kernel(down, up, first, second):
+    half = second.shape[1]
+    first[:, :half] = down[0, :, :half].astype(bf16)
+    first[:, half:] = up[0].astype(bf16)
+    second[...] = down[0, :, half:].astype(bf16)
+
+
+def place_kernel(me, *refs):
+    out = refs[-1]
+    for k, ref in enumerate(refs[:-1]):
+        at = pl.multiple_of(lax.rem(me[0] + NS - k, NS) * ROWS, ROWS)
+        out[pl.ds(at, ROWS), :] = ref[...]
 
 
 def route_kernel(counts, holder, cot, route, out):
@@ -203,67 +215,65 @@
     out[...] = dot(route[...], cot[...]).astype(bf16)
 
 
-def run_back(g_rows, all16, feat, keyw):
+def run_back(g_rows, first):
+    keyw = g_rows.shape[1]
+    at = first.shape[1] // keyw - 1
     return call(
         back_kernel,
         jax.ShapeDtypeStruct((MID, PAIR), f32),
-        [whole((R, keyw)), pl.BlockSpec((WIDE, keyw), lambda i: (0, feat // keyw))],
+        [whole((R, keyw)), pl.BlockSpec((WIDE, keyw), lambda i: (0, at))],
         whole((MID, PAIR)),
         (1,),
-    )(g_rows, all16)
+    )(g_rows, first)
 
 
 def run_grad(parts, x_rows):
-    feat = x_rows.shape[1]
-    nb = 4
+    half = x_rows.shape[1] // 2
     return call(
         grad_kernel,
-        [jax.ShapeDtypeStruct((R, WIDE), bf16), jax.ShapeDtypeStruct((WIDE, feat), f32)],
-        [whole((MID, PAIR))] * 4 + [pl.BlockSpec((R, feat // nb), lambda j: (0, j))],
-        [whole((R, WIDE)), pl.BlockSpec((WIDE, feat // nb), lambda j: (0, j))],
-        (nb,),
+        [jax.ShapeDtypeStruct((R, WIDE), bf16), jax.ShapeDtypeStruct((WIDE, 2 * half), f32)],
+        [whole((MID, PAIR))] * 4 + [pl.BlockSpec((R, half), lambda j: (0, j))],
+        [whole((R, WIDE)), pl.BlockSpec((WIDE, half), lambda j: (0, j))],
+        (2,),
         [pltpu.VMEM((WIDE, R), bf16)],
     )(*parts, x_rows)
 
 
-def run_adg(back16, all16, feat):
-    nb = 4
+def run_adg(back16, first, second):
+    half = second.shape[1]
     return call(
         adg_kernel,
-        jax.ShapeDtypeStruct((R, feat), bf16),
-        [whole((R, WIDE)), pl.BlockSpec((WIDE, feat // nb), lambda j: (0, j))],
-        pl.BlockSpec((R, feat // nb), lambda j: (0, j)),
-        (nb,),
-    )(back16, all16)
-
-
-def run_hid(x_rows, all16):
-    feat = x_rows.shape[1]
-    nb = 4
+        jax.ShapeDtypeStruct((R, 2 * half), bf16),
+        [whole((R, WIDE)), whole((WIDE, half)), whole((WIDE, half))],
+        pl.BlockSpec((R, half), lambda j: (0, j)),
+        (2,),
+    )(back16, first, second)
+
+
+def run_hid(x_rows, first, second):
+    half = second.shape[1]
     return call(
         hid_kernel,
         jax.ShapeDtypeStruct((MID, PAIR), f32),
-        [
-            pl.BlockSpec((R, feat // nb), lambda j: (0, j)),
-            pl.BlockSpec((WIDE, feat // nb), lambda j: (0, j)),
-        ],
+        [pl.BlockSpec((R, half), lambda j: (0, j)), whole((WIDE, half)), whole((WIDE, half))],
         whole((MID, PAIR)),
-        (nb,),
+        (2,),
         [pltpu.VMEM((R, WIDE), f32)],
-    )(x_rows, all16)
-
-
-def run_up(parts, g_rows, all16, feat):
+    )(x_rows, first, second)
+
+
+def run_up(parts, g_rows, first):
     keyw = g_rows.shape[1]
+    at = first.shape[1] // keyw - 1
     return call(
         up_kernel,
         [jax.ShapeDtypeStruct((R, keyw), bf16), jax.ShapeDtypeStruct((WIDE, keyw), f32)],
         [whole((MID, PAIR))] * 4
-        + [whole((R, keyw)), pl.BlockSpec((WIDE, keyw), lambda i: (0, feat // keyw))],
+        + [whole((R, keyw)), pl.BlockSpec((WIDE, keyw), lambda i: (0, at))],
         [whole((R, keyw)), whole((WIDE, keyw))],
         (1,),
         [pltpu.VMEM((R, WIDE), bf16), pltpu.VMEM((WIDE, R), bf16)],
-    )(*parts, g_rows, all16)
+    )(*parts, g_rows, first)
 
 
 def run_base(c, t, tokens, weight, cots, mine, other):
@@ -309,11 +319,18 @@
     t = lax.axis_index("t")
     c = lax.axis_index("c")
     z = lax.axis_index("z")
-
-    both16 = call(cast_kernel, jax.ShapeDtypeStruct((rank, feat + keyw), bf16), [VM] * 2)(
-        adapter_down_matrix, adapter_up_matrix
-    )
-    all16 = lax.all_gather(both16, "z", axis=0, tiled=True)
+    xc = lax.axis_index(("x", "c"))
+
+    first16, second16 = call(
+        cast_kernel,
+        [
+            jax.ShapeDtypeStruct((rank, feat // 2 + keyw), bf16),
+            jax.ShapeDtypeStruct((rank, feat // 2), bf16),
+        ],
+        [VM] * 2,
+    )(adapter_down_matrix, adapter_up_matrix)
+    first = lax.all_gather(first16, "z", axis=0, tiled=True)
+    second = lax.all_gather(second16, "z", axis=0, tiled=True)
 
     route, g_send = call(
         route_kernel,
@@ -340,14 +357,26 @@
     def parts_of(own):
         return [own] + [shift(own, k) for k in range(1, NT)]
 
-    back16, grad_part = run_grad(parts_of(run_back(g_rows, all16, feat, keyw)), x_rows)
+    back16, grad_part = run_grad(parts_of(run_back(g_rows, first)), x_rows)
     grad_down = lax.psum_scatter(grad_part, "z", scatter_dimension=0, tiled=True)
-    adapter_grad = run_adg(back16, all16, feat)
+    adapter_grad = run_adg(back16, first, second)
     ret_grad = lax.all_to_all(adapter_grad, ("x", "c"), 0, 0, tiled=True)
 
-    hidden = parts_of(run_hid(x_rows, all16))
-    adapter_out, up_part = run_up(hidden, g_rows, all16, feat)
-    ret_out = lax.all_to_all(adapter_out, ("x", "c"), 0, 0, tiled=True)
+    hidden = parts_of(run_hid(x_rows, first, second))
+    adapter_out, up_part = run_up(hidden, g_rows, first)
+    chunks = [
+        lax.dynamic_slice(adapter_out, ((xc + k) % NS * ROWS, 0), (ROWS, keyw))
+        for k in range(NS)
+    ]
+    chunks[1:] = [
+        lax.ppermute(v, ("x", "c"), [(i, (i + k) % NS) for i in range(NS)])
+        for k, v in enumerate(chunks[1:], 1)
+    ]
+    ret_out = call(
+        place_kernel,
+        jax.ShapeDtypeStruct((R, keyw), bf16),
+        [pl.BlockSpec(memory_space=pltpu.SMEM)] + [VM] * NS,
+    )(xc.reshape(1), *chunks)
     grad_up = up_part
     for bit in range(3):
         split = grad_up.reshape(-1, 2, rank, keyw)

time: 220 us -> 232 us (1.055)
  starting transfers between devices: 48.3 us -> 54.1 us
  local copies, waits for them, and re-layouts: 5.56 us -> 9.07 us
    all_gather x1 -> x2, waiting for transfers between devices: 24.1 us -> 38.5 us  [the longest x1 21.2 us: step(): first = lax.all_gather(first16, 'z', axis=0, tiled=True)]
    ppermute x0 -> x7, starting transfers between devices: none -> 7.9 us  [step(): lax.ppermute(v, ('x', 'c'), [(i, (i + k) % NS) for i in range(NS)])]
    ppermute x15, starting transfers between devices: 15.6 us -> 23.2 us  [shift(): return lax.ppermute(v, 't', [(i, (i + k) % NT) for i in range(NT)])]
    ppermute x15, waiting for transfers between devices: 53.3 us -> 47 us  [shift(): return lax.ppermute(v, 't', [(i, (i + k) % NT) for i in range(NT)])]
    all_to_all x1, waiting for transfers between devices: 6.22 us -> 0.46 us  [step(): x_rows = lax.all_to_all(x_send, ('x', 'c'), 0, 0, tiled=True)]
    ppermute x3, starting transfers between devices: 12.2 us -> 6.89 us  [step(): lax.ppermute(give, 'z', [(i, i ^ 1 << bit) for i in range(NZ)])]
    all_to_all x1 -> x0, starting transfers between devices: 4.82 us -> none  [step(): ret_out = lax.all_to_all(adapter_out, ('x', 'c'), 0, 0, tiled=True)]
    pallas_call x2 -> x3, Pallas kernels: 7.19 us -> 8.51 us  [the longest x1 4.99 us: run_adg(): call(adg_kernel, jax.ShapeDtypeStruct((R, 2 * half), bf16), [whole((R, WI...]
  transfers between devices with their start and end apart: 27 -> 34, of which waited for: 16 -> 16; matrix products, arithmetic and copies ran while one was open for 8% -> 10% of each run, Pallas kernels for 15% -> 17%
where the time goes in v2:
time: 232 us; the launch traced here: 230 us
  waiting for transfers between devices  93.8 us (40%)
  starting transfers between devices  54.1 us (23%)
  Pallas kernels  39.9 us (17%)
  between operations  14 us (6%)
  matrix products  10.1 us (4%)
  other arithmetic  9.12 us (4%)
  local copies, waits for them, and re-layouts  9.07 us (4%)
    ppermute x15, waiting for transfers between devices, shift(): return lax.ppermute(v, 't', [(i, (i + k) % NT) for i in range(NT)])  47 us
    ppermute x15, starting transfers between devices, shift(): return lax.ppermute(v, 't', [(i, (i + k) % NT) for i in range(NT)])  23.2 us
    all_gather x1, waiting for transfers between devices, step(): first = lax.all_gather(first16, 'z', axis=0, tiled=True)  21.2 us
    all_gather x1, waiting for transfers between devices, step(): second = lax.all_gather(second16, 'z', axis=0, tiled=True)  17.3 us
    pallas_call x1, Pallas kernels, run_base(): pl.pallas_call(base_kernel, out_shape=[jax.ShapeDtypeStruct((rows, feat),...  13.4 us
    dot_general x3, matrix products, dot(): return lax.dot_general(a, b, (dims, ((), ())), preferred_element_type=out)  10.1 us
    ppermute x7, starting transfers between devices, step(): lax.ppermute(v, ('x', 'c'), [(i, (i + k) % NS) for i in range(NS)])  7.9 us
    ppermute x3, starting transfers between devices, step(): lax.ppermute(give, 'z', [(i, i ^ 1 << bit) for i in range(NZ)])  6.89 us
  transfers between devices with their start and end apart: 34, of which 16 were waited for; matrix products, arithmetic and copies ran while one was open for 10% of the time, Pallas kernels for 17%

profile of v2, /device:TPU:2, one launch (start us, length us, event | category | flops | bytes accessed | tf_op | source)
XLA Modules:
  0.0 230.0 jit_solution(5150765526134635021)
XLA Ops:
  11.5 5.6 %all-to-all-start.1 = ((bf16[8,96,256]{2,1,0:T(8,128)(2,1)}), bf16[8,96,256]{2,1,0:T(8,128)(2,1)S(1)}, u32[]{:S(2)}, u32[]{:S(2)}) async-start(bf16[8,96,256]{2,1,0:T(8,128)(2,1)} %bitcast.59), calls=%async_computation.1 | async-start | bytes 786432 | tf_op jit(solution)/shard_map/all_to_all | solution.py:342
  17.2 5.3 %fusion.4 = bf16[768,2048]{1,0:T(8,128)(2,1)} fusion(bf16[768,512]{1,0:T(8,128)(2,1)} %get-tuple-element.25, bf16[512,2048]{1,0:T(8,128)(2,1)} %tokens.1), kind=kOutput, calls=%fused_computation.30 | convolution fusion | flops 1610612736 | bytes 6029312 | tf_op jit(solution)/shard_map/dot_general | solution.py:47
  25.4 5.0 %all-to-all-start = ((bf16[8,96,2048]{2,1,0:T(8,128)(2,1)}), bf16[8,96,2048]{2,1,0:T(8,128)(2,1)S(1)}, u32[]{:S(2)}, u32[]{:S(2)}) async-start(bf16[8,96,2048]{2,1,0:T(8,128)(2,1)} %bitcast.54), calls=%async_computation | async-start | bytes 6291456 | tf_op jit(solution)/shard_map/all_to_all | solution.py:341
  31.2 21.2 %all-gather.3.cloned.1.call-done.first.up = bf16[512,1280]{1,0:T(8,128)(2,1)} async-done(((bf16[64,1280]{1,0:T(8,128)(2,1)}), bf16[512,1280]{1,0:T(8,128)(2,1)}) %all-gather.3.cloned.1.call-update) | async-done | bytes 1310736 | tf_op jit(solution)/shard_map/all_gather | solution.py:332
  54.6 2.7 %collective-permute-start.24 = (f32[384,128]{1,0:T(8,128)}, f32[384,128]{1,0:T(8,128)S(1)}, u32[]{:S(2)}, u32[]{:S(2)}) collective-permute-start(f32[384,128]{1,0:T(8,128)} %shard_map.175.a), channel_id=1, source_target_pairs={{0,3},{1,0},{2,1},{3,2},{4,7},{5,4},{6,5},{7,6},{8,11},{9,8},{10,9... | collective-permute-start | bytes 589832 | tf_op jit(solution)/shard_map/ppermute | solution.py:43
  59.0 4.0 %collective-permute-done.24.d = f32[384,128]{1,0:T(8,128)S(1)} collective-permute-done((f32[384,128]{1,0:T(8,128)}, f32[384,128]{1,0:T(8,128)S(1)}, u32[]{:S(2)}, u32[]{:S(2)}) %collective-permute-start.24) | collective-permute-done | bytes 196640 | tf_op jit(solution)/shard_map/ppermute | solution.py:43
  69.0 5.3 %shard_map.176 = (bf16[768,512]{1,0:T(8,128)(2,1)}, f32[512,2048]{1,0:T(8,128)}) custom-call(f32[384,128]{1,0:T(8,128)} %shard_map.175.a, f32[384,128]{1,0:T(8,128)} %collective-permute-done.22.b, f32[384,128]{1,0:T(8,128)} %copy-done.13, f32[384,128]{1,0:T(8,128)} %copy-done.12, bf16[768,2048]{1,0:T(8,128)(2,1)} %bitcast.48), custom_call_target="tpu_custom_call" | custom-call | tf_op jit(solution)/shard_map/pallas_call | solution.py:232
  74.4 17.3 %all-gather.5.cloned.1.call-done.second = bf16[512,1024]{1,0:T(8,128)(2,1)} async-done(((bf16[64,1024]{1,0:T(8,128)(2,1)}), bf16[512,1024]{1,0:T(8,128)(2,1)}) %all-gather.5.cloned.1.call-update) | async-done | bytes 1048592 | tf_op jit(solution)/shard_map/all_gather | solution.py:333
  91.8 5.0 %shard_map.177 = bf16[768,2048]{1,0:T(8,128)(2,1)} custom-call(bf16[768,512]{1,0:T(8,128)(2,1)} %get-tuple-element.31.back16, bf16[512,1280]{1,0:T(8,128)(2,1)} %all-gather.3.cloned.1.call-done.first.up, bf16[512,1024]{1,0:T(8,128)(2,1)} %all-gather.5.cloned.1.call-done.second), custom_call_target="tpu_custom_call" | custom-call | tf_op jit(solution)/shard_map/pallas_call | solution.py:244
  96.8 4.8 %all-to-all-start.2 = ((bf16[8,96,2048]{2,1,0:T(8,128)(2,1)}), bf16[8,96,2048]{2,1,0:T(8,128)(2,1)S(1)}, u32[]{:S(2)}, u32[]{:S(2)}) async-start(bf16[8,96,2048]{2,1,0:T(8,128)(2,1)} %bitcast.51), calls=%async_computation.2 | async-start | bytes 6291456 | tf_op jit(solution)/shard_map/all_to_all | solution.py:363
  104.2 2.7 %collective-permute-start.5 = (bf16[1024,256]{1,0:T(8,128)(2,1)}, bf16[1024,256]{1,0:T(8,128)(2,1)}, u32[]{:S(2)}, u32[]{:S(2)}) collective-permute-start(bf16[1024,256]{1,0:T(8,128)(2,1)} %get-tuple-element.37), channel_id=1, source_target_pairs={{0,3},{1,0},{2,1},{3,2},{4,7},{5,4},{6,5},{7,6},{8,11},{9,8},{10,9... | collective-permute-start | bytes 1572872 | tf_op jit(solution)/shard_map/ppermute | solution.py:43
  110.9 4.9 %shard_map.172.a = f32[384,128]{1,0:T(8,128)} custom-call(bf16[768,2048]{1,0:T(8,128)(2,1)} %bitcast.49, bf16[512,1280]{1,0:T(8,128)(2,1)} %all-gather.3.cloned.1.call-done.first.up, bf16[512,1024]{1,0:T(8,128)(2,1)} %all-gather.5.cloned.1.call-done.second), custom_call_target="tpu_custom_call" | custom-call | tf_op jit(solution)/shard_map/pallas_call | solution.py:255
  115.9 20.4 %collective-permute-done.2.refs_3_ = bf16[512,256]{1,0:T(8,128)(2,1)} collective-permute-done((bf16[512,256]{1,0:T(8,128)(2,1)S(1)}, bf16[512,256]{1,0:T(8,128)(2,1)}, u32[]{:S(2)}, u32[]{:S(2)}) %collective-permute-start.2) | collective-permute-done | bytes 262176 | tf_op jit(solution)/shard_map/ppermute | solution.py:43
  136.2 2.9 %collective-permute-start.13 = (f32[384,128]{1,0:T(8,128)}, f32[384,128]{1,0:T(8,128)S(1)}, u32[]{:S(2)}, u32[]{:S(2)}) collective-permute-start(f32[384,128]{1,0:T(8,128)} %shard_map.172.a), channel_id=1, source_target_pairs={{0,2},{1,3},{2,0},{3,1},{4,6},{5,7},{6,4},{7,5},{8,10},{9,11},{10,... | collective-permute-start | bytes 589832 | tf_op jit(solution)/shard_map/ppermute | solution.py:43
  143.6 5.4 %collective-permute-start.1 = (bf16[512,256]{1,0:T(8,128)(2,1)S(1)}, bf16[512,256]{1,0:T(8,128)(2,1)}, u32[]{:S(2)}, u32[]{:S(2)}) collective-permute-start(bf16[512,256]{1,0:T(8,128)(2,1)S(1)} %copy-done.4), channel_id=1, source_target_pairs={{0,2},{1,3},{2,0},{3,1},{4,6},{5,7},{6,4},{7,5},{8,10},{9,11},{10,... | collective-permute-start | bytes 786440 | tf_op jit(solution)/shard_map/ppermute | solution.py:43
  149.0 3.8 %collective-permute-done.12.b = f32[384,128]{1,0:T(8,128)S(1)} collective-permute-done((f32[384,128]{1,0:T(8,128)}, f32[384,128]{1,0:T(8,128)S(1)}, u32[]{:S(2)}, u32[]{:S(2)}) %collective-permute-start.12) | collective-permute-done | bytes 196640 | tf_op jit(solution)/shard_map/ppermute | solution.py:43
  153.5 2.9 %shard_map.173 = (bf16[768,256]{1,0:T(8,128)(2,1)}, f32[512,256]{1,0:T(8,128)}) custom-call(f32[384,128]{1,0:T(8,128)} %shard_map.172.a, f32[384,128]{1,0:T(8,128)} %copy-done.11, f32[384,128]{1,0:T(8,128)} %copy-done.10, f32[384,128]{1,0:T(8,128)} %copy-done.9, bf16[768,256]{1,0:T(8,128)(2,1)} %bitcast.53, ...), custom_call_target="tpu_custom_call" | custom-call | tf_op jit(solution)/shard_map/pallas_call | solution.py:268
  169.9 13.4 %base_kernel.1 = (f32[512,2048]{1,0:T(8,128)}, f32[512,256]{1,0:T(8,128)}, f32[512,256]{1,0:T(8,128)}, f32[512,256]{1,0:T(8,128)}, f32[512,256]{1,0:T(8,128)}) custom-call(s32[2]{0:T(128)} %pad_add_fusion.at, bf16[512,2048]{1,0:T(8,128)(2,1)} %tokens.1, bf16[8192,256]{1,0:T(8,128)(2,1)} %own.1, bf16[512,256]{1,0:T(8,128)(2,1)} %cot.1, ...), custom_call_target="tpu_custom_call" | custom-call | tf_op jit(solution)/shard_map/base_kernel/pallas_call | solution.py:283
  183.4 2.6 %collective-permute-start.9 = (f32[512,256]{1,0:T(8,128)}, f32[512,256]{1,0:T(8,128)}, u32[]{:S(2)}, u32[]{:S(2)}) collective-permute-start(f32[512,256]{1,0:T(8,128)} %get-tuple-element.22), channel_id=1, source_target_pairs={{0,3},{1,0},{2,1},{3,2},{4,7},{5,4},{6,5},{7,6},{8,11},{9,8},{10,9... | collective-permute-start | bytes 1572872 | tf_op jit(solution)/shard_map/ppermute | solution.py:43
  194.2 4.8 %collective-permute-done.26 = f32[2,64,256]{2,1,0:T(8,128)S(1)} collective-permute-done((f32[2,64,256]{2,1,0:T(8,128)S(1)}, f32[2,64,256]{2,1,0:T(8,128)S(1)}, u32[]{:S(2)}, u32[]{:S(2)}) %collective-permute-start.26) | collective-permute-done | bytes 131104 | tf_op jit(solution)/shard_map/ppermute | solution.py:386
  199.1 3.4 %collective-permute-start.27 = (f32[1,64,256]{2,1,0:T(8,128)S(1)}, f32[1,64,256]{2,1,0:T(8,128)S(1)}, u32[]{:S(2)}, u32[]{:S(2)}) collective-permute-start(f32[1,64,256]{2,1,0:T(8,128)S(1)} %constant_dynamic-slice_fusion), channel_id=1, source_target_pairs={{0,128},{32,160},{64,192},{96,224},{128,0},{160,32},{192,64},{224,... | collective-permute-start | bytes 196616 | tf_op jit(solution)/shard_map/ppermute | solution.py:386
  202.5 6.9 %collective-permute-done.9 = f32[512,256]{1,0:T(8,128)} collective-permute-done((f32[512,256]{1,0:T(8,128)}, f32[512,256]{1,0:T(8,128)}, u32[]{:S(2)}, u32[]{:S(2)}) %collective-permute-start.9) | collective-permute-done | bytes 524320 | tf_op jit(solution)/shard_map/ppermute | solution.py:43
  209.4 3.5 %collective-permute-done.11 = f32[512,256]{1,0:T(8,128)} collective-permute-done((f32[512,256]{1,0:T(8,128)}, f32[512,256]{1,0:T(8,128)}, u32[]{:S(2)}, u32[]{:S(2)}) %collective-permute-start.11) | collective-permute-done | bytes 524320 | tf_op jit(solution)/shard_map/ppermute | solution.py:43
  215.8 3.1 %fusion.6 = f32[512,2048]{1,0:T(8,128)S(1)} fusion(bf16[768,512]{1,0:T(8,128)(2,1)} %get-tuple-element.25, bf16[768,2048]{1,0:T(8,128)(2,1)S(1)} %bitcast.50), kind=kOutput, calls=%fused_computation.32 | convolution fusion | flops 1610612736 | bytes 8126464 | tf_op jit(solution)/shard_map/dot_general | solution.py:47
  (113 shorter events, 59.0 us)
Async XLA Ops:
  7.2 45.2 %all-gather.3.cloned.1.call-start = ((), (), s32[]{:S(2)}) async-start(), calls=%async_computation.4 | async-start | bytes 1474560 | tf_op jit(solution)/shard_map/all_gather | solution.py:332
  11.5 13.1 %all-to-all-start.1 = ((bf16[8,96,256]{2,1,0:T(8,128)(2,1)}), bf16[8,96,256]{2,1,0:T(8,128)(2,1)S(1)}, u32[]{:S(2)}, u32[]{:S(2)}) async-start(bf16[8,96,256]{2,1,0:T(8,128)(2,1)} %bitcast.59), calls=%async_computation.1 | async-start | bytes 786432 | tf_op jit(solution)/shard_map/all_to_all | solution.py:342
  25.4 42.0 %all-to-all-start = ((bf16[8,96,2048]{2,1,0:T(8,128)(2,1)}), bf16[8,96,2048]{2,1,0:T(8,128)(2,1)S(1)}, u32[]{:S(2)}, u32[]{:S(2)}) async-start(bf16[8,96,2048]{2,1,0:T(8,128)(2,1)} %bitcast.54), calls=%async_computation | async-start | bytes 6291456 | tf_op jit(solution)/shard_map/all_to_all | solution.py:341
  30.4 61.3 %all-gather.5.cloned.1.call-start = ((), (), s32[]{:S(2)}) async-start(), calls=%async_computation.5 | async-start | bytes 1179648 | tf_op jit(solution)/shard_map/all_gather | solution.py:333
  31.2 189.8 %reduce-scatter.2.cloned.1.call-start = ((), (), s32[]{:S(2)}) async-start(), calls=%async_computation.6 | async-start | bytes 4718592 | tf_op jit(solution)/shard_map/reduce_scatter | solution.py:361
  96.8 119.0 %all-to-all-start.2 = ((bf16[8,96,2048]{2,1,0:T(8,128)(2,1)}), bf16[8,96,2048]{2,1,0:T(8,128)(2,1)S(1)}, u32[]{:S(2)}, u32[]{:S(2)}) async-start(bf16[8,96,2048]{2,1,0:T(8,128)(2,1)} %bitcast.51), calls=%async_computation.2 | async-start | bytes 6291456 | tf_op jit(solution)/shard_map/all_to_all | solution.py:363
  104.2 35.0 %collective-permute-start.5 = (bf16[1024,256]{1,0:T(8,128)(2,1)}, bf16[1024,256]{1,0:T(8,128)(2,1)}, u32[]{:S(2)}, u32[]{:S(2)}) collective-permute-start(bf16[1024,256]{1,0:T(8,128)(2,1)} %get-tuple-element.37), channel_id=1, source_target_pairs={{0,3},{1,0},{2,1},{3,2},{4,7},{5,4},{6,5},{7,6},{8,11},{9,8},{10,9... | collective-permute-start | bytes 1572872 | tf_op jit(solution)/shard_map/ppermute | solution.py:43
  106.9 32.3 %collective-permute-start.4 = (bf16[1024,256]{1,0:T(8,128)(2,1)}, bf16[1024,256]{1,0:T(8,128)(2,1)}, u32[]{:S(2)}, u32[]{:S(2)}) collective-permute-start(bf16[1024,256]{1,0:T(8,128)(2,1)} %get-tuple-element.38), channel_id=1, source_target_pairs={{0,2},{1,3},{2,0},{3,1},{4,6},{5,7},{6,4},{7,5},{8,10},{9,11},{10,... | collective-permute-start | bytes 1572872 | tf_op jit(solution)/shard_map/ppermute | solution.py:43
  107.7 32.0 %collective-permute-start.3 = (bf16[1024,256]{1,0:T(8,128)(2,1)}, bf16[1024,256]{1,0:T(8,128)(2,1)}, u32[]{:S(2)}, u32[]{:S(2)}) collective-permute-start(bf16[1024,256]{1,0:T(8,128)(2,1)} %get-tuple-element.39), channel_id=1, source_target_pairs={{0,1},{1,2},{2,3},{3,0},{4,5},{5,6},{6,7},{7,4},{8,9},{9,10},{10,1... | collective-permute-start | bytes 1572872 | tf_op jit(solution)/shard_map/ppermute | solution.py:43
  108.6 27.7 %collective-permute-start.2 = (bf16[512,256]{1,0:T(8,128)(2,1)S(1)}, bf16[512,256]{1,0:T(8,128)(2,1)}, u32[]{:S(2)}, u32[]{:S(2)}) collective-permute-start(bf16[512,256]{1,0:T(8,128)(2,1)S(1)} %copy-done.4), channel_id=1, source_target_pairs={{0,3},{1,0},{2,1},{3,2},{4,7},{5,4},{6,5},{7,6},{8,11},{9,8},{10,9... | collective-permute-start | bytes 786440 | tf_op jit(solution)/shard_map/ppermute | solution.py:43
  115.9 26.0 %collective-permute-start.14 = (f32[384,128]{1,0:T(8,128)}, f32[384,128]{1,0:T(8,128)S(1)}, u32[]{:S(2)}, u32[]{:S(2)}) collective-permute-start(f32[384,128]{1,0:T(8,128)} %shard_map.172.a), channel_id=1, source_target_pairs={{0,3},{1,0},{2,1},{3,2},{4,7},{5,4},{6,5},{7,6},{8,11},{9,8},{10,9... | collective-permute-start | bytes 589832 | tf_op jit(solution)/shard_map/ppermute | solution.py:43
  139.2 22.2 %collective-permute-start.8 = (bf16[1024,256]{1,0:T(8,128)(2,1)}, bf16[1024,256]{1,0:T(8,128)(2,1)}, u32[]{:S(2)}, u32[]{:S(2)}) collective-permute-start(bf16[1024,256]{1,0:T(8,128)(2,1)} %collective-permute-done.5.refs_6_), channel_id=1, source_target_pairs={{0,4},{4,0},{1,5},{5,1},{2,6},{6,2},{3,7},{7,3},{8,12},{12,8},{9,1... | collective-permute-start | bytes 1572872 | tf_op jit(solution)/shard_map/ppermute | solution.py:351
  139.2 23.4 %collective-permute-start.7 = (bf16[1024,256]{1,0:T(8,128)(2,1)}, bf16[1024,256]{1,0:T(8,128)(2,1)}, u32[]{:S(2)}, u32[]{:S(2)}) collective-permute-start(bf16[1024,256]{1,0:T(8,128)(2,1)} %collective-permute-done.4.refs_5_), channel_id=1, source_target_pairs={{0,4},{4,0},{1,5},{5,1},{2,6},{6,2},{3,7},{7,3},{8,12},{12,8},{9,1... | collective-permute-start | bytes 1572872 | tf_op jit(solution)/shard_map/ppermute | solution.py:351
  139.7 24.4 %collective-permute-start.6 = (bf16[1024,256]{1,0:T(8,128)(2,1)}, bf16[1024,256]{1,0:T(8,128)(2,1)}, u32[]{:S(2)}, u32[]{:S(2)}) collective-permute-start(bf16[1024,256]{1,0:T(8,128)(2,1)} %collective-permute-done.3.refs_4_), channel_id=1, source_target_pairs={{0,4},{4,0},{1,5},{5,1},{2,6},{6,2},{3,7},{7,3},{8,12},{12,8},{9,1... | collective-permute-start | bytes 1572872 | tf_op jit(solution)/shard_map/ppermute | solution.py:351
  143.6 14.9 %collective-permute-start.1 = (bf16[512,256]{1,0:T(8,128)(2,1)S(1)}, bf16[512,256]{1,0:T(8,128)(2,1)}, u32[]{:S(2)}, u32[]{:S(2)}) collective-permute-start(bf16[512,256]{1,0:T(8,128)(2,1)S(1)} %copy-done.4), channel_id=1, source_target_pairs={{0,2},{1,3},{2,0},{3,1},{4,6},{5,7},{6,4},{7,5},{8,10},{9,11},{10,... | collective-permute-start | bytes 786440 | tf_op jit(solution)/shard_map/ppermute | solution.py:43
  158.6 30.3 %collective-permute-start.25 = (f32[4,64,256]{2,1,0:T(8,128)}, f32[4,64,256]{2,1,0:T(8,128)}, u32[]{:S(2)}, u32[]{:S(2)}) collective-permute-start(f32[4,64,256]{2,1,0:T(8,128)} %dynamic-slice_bitcast_fusion), channel_id=1, source_target_pairs={{0,32},{32,0},{64,96},{96,64},{128,160},{160,128},{192,224},{224,1... | collective-permute-start | bytes 786440 | tf_op jit(solution)/shard_map/ppermute | solution.py:386
  164.1 19.2 %collective-permute-start.18 = (bf16[96,256]{1,0:T(8,128)(2,1)}, bf16[96,256]{1,0:T(8,128)(2,1)S(1)}, u32[]{:S(2)}, u32[]{:S(2)}) collective-permute-start(bf16[96,256]{1,0:T(8,128)(2,1)} %get-tuple-element.46), channel_id=1, source_target_pairs={{0,16},{4,20},{8,24},{12,28},{16,0},{20,4},{24,8},{28,12},{1,17},{... | collective-permute-start | bytes 147464 | tf_op jit(solution)/shard_map/ppermute | solution.py:372
  166.0 20.0 %collective-permute-start.17 = (bf16[96,256]{1,0:T(8,128)(2,1)S(1)}, bf16[96,256]{1,0:T(8,128)(2,1)S(1)}, u32[]{:S(2)}, u32[]{:S(2)}) collective-permute-start(bf16[96,256]{1,0:T(8,128)(2,1)S(1)} %get-tuple-element.47), channel_id=1, source_target_pairs={{0,12},{4,16},{8,20},{12,24},{16,28},{20,0},{24,4},{28,8},{1,13},{... | collective-permute-start | bytes 147464 | tf_op jit(solution)/shard_map/ppermute | solution.py:372
  166.4 19.6 %collective-permute-start.16 = (bf16[96,256]{1,0:T(8,128)(2,1)S(1)}, bf16[96,256]{1,0:T(8,128)(2,1)}, u32[]{:S(2)}, u32[]{:S(2)}) collective-permute-start(bf16[96,256]{1,0:T(8,128)(2,1)S(1)} %get-tuple-element.48), channel_id=1, source_target_pairs={{0,8},{4,12},{8,16},{12,20},{16,24},{20,28},{24,0},{28,4},{1,9},{5... | collective-permute-start | bytes 147464 | tf_op jit(solution)/shard_map/ppermute | solution.py:372
  168.2 18.9 %collective-permute-start.15 = (bf16[96,256]{1,0:T(8,128)(2,1)S(1)}, bf16[96,256]{1,0:T(8,128)(2,1)}, u32[]{:S(2)}, u32[]{:S(2)}) collective-permute-start(bf16[96,256]{1,0:T(8,128)(2,1)S(1)} %get-tuple-element.49), channel_id=1, source_target_pairs={{0,4},{4,8},{8,12},{12,16},{16,20},{20,24},{24,28},{28,0},{1,5},{5... | collective-permute-start | bytes 147464 | tf_op jit(solution)/shard_map/ppermute | solution.py:372
  183.4 26.0 %collective-permute-start.9 = (f32[512,256]{1,0:T(8,128)}, f32[512,256]{1,0:T(8,128)}, u32[]{:S(2)}, u32[]{:S(2)}) collective-permute-start(f32[512,256]{1,0:T(8,128)} %get-tuple-element.22), channel_id=1, source_target_pairs={{0,3},{1,0},{2,1},{3,2},{4,7},{5,4},{6,5},{7,6},{8,11},{9,8},{10,9... | collective-permute-start | bytes 1572872 | tf_op jit(solution)/shard_map/ppermute | solution.py:43
  186.0 23.4 %collective-permute-start.10 = (f32[512,256]{1,0:T(8,128)}, f32[512,256]{1,0:T(8,128)}, u32[]{:S(2)}, u32[]{:S(2)}) collective-permute-start(f32[512,256]{1,0:T(8,128)} %get-tuple-element.23), channel_id=1, source_target_pairs={{0,2},{1,3},{2,0},{3,1},{4,6},{5,7},{6,4},{7,5},{8,10},{9,11},{10,... | collective-permute-start | bytes 1572872 | tf_op jit(solution)/shard_map/ppermute | solution.py:43
  186.0 26.8 %collective-permute-start.11 = (f32[512,256]{1,0:T(8,128)}, f32[512,256]{1,0:T(8,128)}, u32[]{:S(2)}, u32[]{:S(2)}) collective-permute-start(f32[512,256]{1,0:T(8,128)} %get-tuple-element.24), channel_id=1, source_target_pairs={{0,1},{1,2},{2,3},{3,0},{4,5},{5,6},{6,7},{7,4},{8,9},{9,10},{10,1... | collective-permute-start | bytes 1572872 | tf_op jit(solution)/shard_map/ppermute | solution.py:43
  199.1 16.0 %collective-permute-start.27 = (f32[1,64,256]{2,1,0:T(8,128)S(1)}, f32[1,64,256]{2,1,0:T(8,128)S(1)}, u32[]{:S(2)}, u32[]{:S(2)}) collective-permute-start(f32[1,64,256]{2,1,0:T(8,128)S(1)} %constant_dynamic-slice_fusion), channel_id=1, source_target_pairs={{0,128},{32,160},{64,192},{96,224},{128,0},{160,32},{192,64},{224,... | collective-permute-start | bytes 196616 | tf_op jit(solution)/shard_map/ppermute | solution.py:386
  (31 other events, 274.6 us)
Sparse Core Ops, SparseCore 0:
  10.3 41.9 all-gather.2
  54.7 36.9 all-gather.4
  94.3 53.6 reduce-scatter.1

commit v3 on v1

--- a/solution.py
+++ b/solution.py
@@ -150,9 +150,8 @@
     grad[...] = dot(cols[...], g[...])
 
 
-def base_kernel(at, tokens, own, *refs):
-    cots, mine, other = refs[:NT], refs[NT : 2 * NT - 1], refs[2 * NT - 1 : 3 * NT - 2]
-    grad, parts = refs[3 * NT - 2], refs[3 * NT - 1 :]
+def base_grad_kernel(at, own, *refs):
+    cots, mine, other, grad = refs[:NT], refs[NT : 2 * NT - 1], refs[2 * NT - 1 : -1], refs[-1]
     step = pl.program_id(0)
 
     def half(pieces):
@@ -160,16 +159,31 @@
         for cot, w in zip(cots[1:], pieces):
             total = total + dot(cot[...], w[...], ((1,), (1,)))
         grad[...] = total
-        for part, w in zip(parts, (own,) + pieces):
+
+    @pl.when(step == at[0])
+    def _():
+        half(mine)
+
+    @pl.when(step != at[0])
+    def _():
+        half(other)
+
+
+def base_out_kernel(at, tokens, own, *refs):
+    mine, other, parts = refs[: NT - 1], refs[NT - 1 : 2 * NT - 2], refs[2 * NT - 2 :]
+    step = pl.program_id(0)
+
+    def half(pieces):
+        for p, w in zip(parts, (own,) + pieces):
             v = dot(tokens[...], w[...])
 
             @pl.when(step == 0)
             def _():
-                part[...] = v
+                p[...] = v
 
             @pl.when(step != 0)
             def _():
-                part[...] += v
+                p[...] += v
 
     @pl.when(step == at[0])
     def _():
@@ -178,6 +192,10 @@
     @pl.when(step != at[0])
     def _():
         half(other)
+
+
+def final_kernel(route, ret, base, out):
+    out[...] = (base[...] + dot(route[...], ret[...], ((0,), (0,)))).astype(bf16)
 
 
 def cast_kernel(down, up, out):
@@ -215,7 +233,7 @@
 
 def run_grad(parts, x_rows):
     feat = x_rows.shape[1]
-    nb = 4
+    nb = 2
     return call(
         grad_kernel,
         [jax.ShapeDtypeStruct((R, WIDE), bf16), jax.ShapeDtypeStruct((WIDE, feat), f32)],
@@ -227,7 +245,7 @@
 
 
 def run_adg(back16, all16, feat):
-    nb = 4
+    nb = 2
     return call(
         adg_kernel,
         jax.ShapeDtypeStruct((R, feat), bf16),
@@ -239,7 +257,7 @@
 
 def run_hid(x_rows, all16):
     feat = x_rows.shape[1]
-    nb = 4
+    nb = 2
     return call(
         hid_kernel,
         jax.ShapeDtypeStruct((MID, PAIR), f32),
@@ -266,28 +284,66 @@
     )(*parts, g_rows, all16)
 
 
-def run_base(c, t, tokens, weight, cots, mine, other):
-    rows, feat = tokens.shape
+def run_base(kernel, at, lead, lead_specs, weight, pieces, outs, out_specs):
     keyw = weight.shape[1]
-    half = feat // NC
+    half = pieces[0].shape[0]
+    own = pl.BlockSpec((half, keyw), lambda i, at: (at[1] * NC + i, 0))
+    n = len(pieces)
+    first = kernel is base_out_kernel
     return pl.pallas_call(
-        base_kernel,
-        out_shape=[jax.ShapeDtypeStruct((rows, feat), f32)]
-        + [jax.ShapeDtypeStruct((rows, keyw), f32)] * NT,
+        kernel,
+        out_shape=outs,
         grid_spec=pltpu.PrefetchScalarGridSpec(
             num_scalar_prefetch=1,
             grid=(NC,),
-            in_specs=[
-                pl.BlockSpec((rows, half), lambda i, at: (0, i)),
-                pl.BlockSpec((half, keyw), lambda i, at: (at[1] * NC + i, 0)),
-            ]
-            + [whole((rows, keyw))] * NT
-            + [whole((half, keyw))] * (2 * NT - 2),
-            out_specs=[pl.BlockSpec((rows, half), lambda i, at: (0, i))]
-            + [whole((rows, keyw))] * NT,
+            in_specs=(lead_specs + [own] if first else [own] + lead_specs)
+            + [whole((half, keyw))] * n,
+            out_specs=out_specs,
         ),
-        name="base_kernel",
-    )(jnp.stack([c, t]), tokens, weight, *cots, *mine, *other)
+    )(at, *(lead + [weight] if first else [weight] + lead), *pieces)
+
+
+def run_base_grad(at, weight, cots, pieces):
+    rows, keyw = cots[0].shape
+    half = pieces[0].shape[0]
+    return run_base(
+        base_grad_kernel,
+        at,
+        cots,
+        [whole((rows, keyw))] * NT,
+        weight,
+        pieces,
+        jax.ShapeDtypeStruct((rows, NC * half), f32),
+        pl.BlockSpec((rows, half), lambda i, at: (0, i)),
+    )
+
+
+def run_base_out(at, weight, tokens, pieces):
+    rows = tokens.shape[0]
+    half, keyw = pieces[0].shape
+    return run_base(
+        base_out_kernel,
+        at,
+        [tokens],
+        [pl.BlockSpec((rows, half), lambda i, at: (0, i))],
+        weight,
+        pieces,
+        [jax.ShapeDtypeStruct((rows, keyw), f32)] * NT,
+        [whole((rows, keyw))] * NT,
+    )
+
+
+def run_final(route, ret, base):
+    rows, feat = base.shape
+    half = feat // 2
+    return call(
+        final_kernel,
+        jax.ShapeDtypeStruct((rows, feat), bf16),
+        [whole(route.shape)]
+        + [pl.BlockSpec((n, half), lambda j: (0, j)) for n in (ret.shape[0], rows)],
+        pl.BlockSpec((rows, half), lambda j: (0, j)),
+        (2,),
+    )(route, ret, base)
 
 
 def step(
@@ -333,7 +389,10 @@
         halves.append(shift(piece, k))
     other = [lax.ppermute(v, "c", [(0, 1), (1, 0)]) for v in halves]
     cots = [cotangent] + [shift(cotangent, k) for k in range(1, NT)]
-    base_grad, base_out, *outs = run_base(c, t, tokens, frozen_key_weight, cots, halves, other)
+    at = jnp.stack([c, t])
+    pieces = halves + other
+    base_grad = run_base_grad(at, frozen_key_weight, cots, pieces)
+    base_out, *outs = run_base_out(at, frozen_key_weight, tokens, pieces)
     for k in range(1, NT):
         base_out = base_out + shift(outs[k - 1], -k)
 
@@ -358,7 +417,7 @@
     grad_up = grad_up.reshape(rank, keyw)
 
     layer_out = (base_out + dot(route, ret_out, ((0,), (0,)))).astype(bf16)
-    input_grad = (base_grad + dot(route, ret_grad, ((0,), (0,)))).astype(bf16)
+    input_grad = run_final(route, ret_grad, base_grad)
     fresh_down = optimizer_update(
         adapter_down_matrix[0], down_first_moment[0], down_second_moment[0], grad_down
     )

time: 220 us -> 198 us (0.900)
  waiting for transfers between devices: 92.4 us -> 64.3 us
  Pallas kernels: 40.2 us -> 46.7 us
  matrix products: 9.95 us -> 6.9 us
  local copies, waits for them, and re-layouts: 5.56 us -> 8.13 us
    ppermute x15, waiting for transfers between devices: 53.3 us -> 28.6 us  [shift(): return lax.ppermute(v, 't', [(i, (i + k) % NT) for i in range(NT)])]
    pallas_call x1 -> x3, Pallas kernels: 13.7 us -> 22.5 us  [the longest x2 17.1 us: run_base(): pl.pallas_call(kernel, out_shape=outs, grid_spec=pltpu.PrefetchScalarGrid...]
    dot_general x3 -> x2, matrix products: 9.95 us -> 6.9 us  [dot(): return lax.dot_general(a, b, (dims, ((), ())), preferred_element_type=out)]
  transfers between devices with their start and end apart: 27 -> 27, of which waited for: 16 -> 12; matrix products, arithmetic and copies ran while one was open for 8% -> 8% of each run, Pallas kernels for 15% -> 20%
where the time goes in v3:
time: 198 us; the launch traced here: 197 us
  waiting for transfers between devices  64.3 us (32%)
  starting transfers between devices  49 us (25%)
  Pallas kernels  46.7 us (24%)
  between operations  14.2 us (7%)
  local copies, waits for them, and re-layouts  8.13 us (4%)
  other arithmetic  7.62 us (4%)
  matrix products  6.9 us (3%)
    ppermute x15, waiting for transfers between devices, shift(): return lax.ppermute(v, 't', [(i, (i + k) % NT) for i in range(NT)])  28.6 us
    all_gather x1, waiting for transfers between devices, step(): all16 = lax.all_gather(both16, 'z', axis=0, tiled=True)  24.1 us
    ppermute x15, starting transfers between devices, shift(): return lax.ppermute(v, 't', [(i, (i + k) % NT) for i in range(NT)])  17.3 us
    pallas_call x2, Pallas kernels, run_base(): pl.pallas_call(kernel, out_shape=outs, grid_spec=pltpu.PrefetchScalarGrid...  17.1 us
    ppermute x3, starting transfers between devices, step(): lax.ppermute(give, 'z', [(i, i ^ 1 << bit) for i in range(NZ)])  11.5 us
    dot_general x2, matrix products, dot(): return lax.dot_general(a, b, (dims, ((), ())), preferred_element_type=out)  6.9 us
    all_to_all x1, waiting for transfers between devices, step(): x_rows = lax.all_to_all(x_send, ('x', 'c'), 0, 0, tiled=True)  6.22 us
    all_to_all x1, starting transfers between devices, step(): g_rows = lax.all_to_all(g_send, ('x', 'c'), 0, 0, tiled=True)  5.6 us
  transfers between devices with their start and end apart: 27, of which 12 were waited for; matrix products, arithmetic and copies ran while one was open for 8% of the time, Pallas kernels for 20%

profile of v3, /device:TPU:2, one launch (start us, length us, event | category | flops | bytes accessed | tf_op | source)
XLA Modules:
  0.0 196.8 jit_solution(8318347823482498578)
XLA Ops:
  9.0 2.5 %shard_map.171 = (bf16[768,512]{1,0:T(8,128)(2,1)}, bf16[768,256]{1,0:T(8,128)(2,1)}) custom-call(s32[1,64]{1,0:T(1,128)} %counts.1, s32[1,64]{1,0:T(1,128)} %bitcast.61, bf16[512,256]{1,0:T(8,128)(2,1)} %refs_0_.1), custom_call_target="tpu_custom_call" | custom-call | tf_op jit(solution)/shard_map/pallas_call | solution.py:374
  11.6 5.6 %all-to-all-start.1 = ((bf16[8,96,256]{2,1,0:T(8,128)(2,1)}), bf16[8,96,256]{2,1,0:T(8,128)(2,1)S(1)}, u32[]{:S(2)}, u32[]{:S(2)}) async-start(bf16[8,96,256]{2,1,0:T(8,128)(2,1)} %bitcast.60), calls=%async_computation.1 | async-start | bytes 786432 | tf_op jit(solution)/shard_map/all_to_all | solution.py:381
  17.2 5.3 %fusion.4 = bf16[768,2048]{1,0:T(8,128)(2,1)} fusion(bf16[768,512]{1,0:T(8,128)(2,1)} %get-tuple-element.22.route, bf16[512,2048]{1,0:T(8,128)(2,1)} %tokens.1), kind=kOutput, calls=%fused_computation.21 | convolution fusion | flops 1610612736 | bytes 6029312 | tf_op jit(solution)/shard_map/dot_general | solution.py:47
  25.4 5.0 %all-to-all-start = ((bf16[8,96,2048]{2,1,0:T(8,128)(2,1)}), bf16[8,96,2048]{2,1,0:T(8,128)(2,1)S(1)}, u32[]{:S(2)}, u32[]{:S(2)}) async-start(bf16[8,96,2048]{2,1,0:T(8,128)(2,1)} %bitcast.53), calls=%async_computation | async-start | bytes 6291456 | tf_op jit(solution)/shard_map/all_to_all | solution.py:380
  30.4 24.1 %all-gather.2.cloned.1.call-done.down.up = bf16[512,2304]{1,0:T(8,128)(2,1)} async-done(((bf16[64,2304]{1,0:T(8,128)(2,1)}), bf16[512,2304]{1,0:T(8,128)(2,1)}) %all-gather.2.cloned.1.call-update) | async-done | bytes 2359312 | tf_op jit(solution)/shard_map/all_gather | solution.py:372
  56.7 2.7 %collective-permute-start.14 = (f32[384,128]{1,0:T(8,128)}, f32[384,128]{1,0:T(8,128)S(1)}, u32[]{:S(2)}, u32[]{:S(2)}) collective-permute-start(f32[384,128]{1,0:T(8,128)} %shard_map.175.a), channel_id=1, source_target_pairs={{0,3},{1,0},{2,1},{3,2},{4,7},{5,4},{6,5},{7,6},{8,11},{9,8},{10,9... | collective-permute-start | bytes 589832 | tf_op jit(solution)/shard_map/ppermute | solution.py:43
  61.2 6.2 %all-to-all-done = bf16[8,96,2048]{2,1,0:T(8,128)(2,1)S(1)} async-done(((bf16[8,96,2048]{2,1,0:T(8,128)(2,1)}), bf16[8,96,2048]{2,1,0:T(8,128)(2,1)S(1)}, u32[]{:S(2)}, u32[]{:S(2)}) %all-to-all-start) | async-done | bytes 3145760 | tf_op jit(solution)/shard_map/all_to_all | solution.py:380
  69.2 5.3 %shard_map.176 = (bf16[768,512]{1,0:T(8,128)(2,1)}, f32[512,2048]{1,0:T(8,128)}) custom-call(f32[384,128]{1,0:T(8,128)} %shard_map.175.a, f32[384,128]{1,0:T(8,128)} %collective-permute-done.12.b, f32[384,128]{1,0:T(8,128)} %copy-done.11, f32[384,128]{1,0:T(8,128)} %copy-done.10, bf16[768,2048]{1,0:T(8,128)(2,1)} %bitcast.47), custom_call_target="tpu_custom_call" | custom-call | tf_op jit(solution)/shard_map/pallas_call | solution.py:237
  74.5 4.7 %shard_map.173.a = f32[384,128]{1,0:T(8,128)} custom-call(bf16[768,2048]{1,0:T(8,128)(2,1)} %bitcast.48, bf16[512,2304]{1,0:T(8,128)(2,1)} %all-gather.2.cloned.1.call-done.down.up), custom_call_target="tpu_custom_call" | custom-call | tf_op jit(solution)/shard_map/pallas_call | solution.py:261
  83.0 6.8 %collective-permute-done.11.d = f32[384,128]{1,0:T(8,128)S(1)} collective-permute-done((f32[384,128]{1,0:T(8,128)}, f32[384,128]{1,0:T(8,128)S(1)}, u32[]{:S(2)}, u32[]{:S(2)}) %collective-permute-start.11) | collective-permute-done | bytes 196640 | tf_op jit(solution)/shard_map/ppermute | solution.py:43
  94.1 2.9 %shard_map.174 = (bf16[768,256]{1,0:T(8,128)(2,1)}, f32[512,256]{1,0:T(8,128)}) custom-call(f32[384,128]{1,0:T(8,128)} %shard_map.173.a, f32[384,128]{1,0:T(8,128)} %copy-done.9, f32[384,128]{1,0:T(8,128)} %copy-done.8, f32[384,128]{1,0:T(8,128)} %copy-done.7, bf16[768,256]{1,0:T(8,128)(2,1)} %bitcast.52, bf16[512,2304]{1,0:T(8,128)(2,1)} %all-gather.2.cloned.1.call-done.down.up), custom_call_target="tpu_custom_call" | custom-call | tf_op jit(solution)/shard_map/pallas_call | solution.py:276
  97.0 4.8 %all-to-all-start.2 = ((bf16[8,96,256]{2,1,0:T(8,128)(2,1)}), bf16[8,96,256]{2,1,0:T(8,128)(2,1)S(1)}, u32[]{:S(2)}, u32[]{:S(2)}) async-start(bf16[8,96,256]{2,1,0:T(8,128)(2,1)} %bitcast.59), calls=%async_computation.2 | async-start | bytes 786432 | tf_op jit(solution)/shard_map/all_to_all | solution.py:409
  101.8 2.5 %constant_dynamic-slice_fusion.1 = (bf16[1024,256]{1,0:T(8,128)(2,1)}, bf16[1024,256]{1,0:T(8,128)(2,1)}, bf16[1024,256]{1,0:T(8,128)(2,1)}) fusion(bf16[8192,256]{1,0:T(8,128)(2,1)} %own.3, s32[]{:T(128)S(6)} %select_n.50, s32[]{:T(128)S(6)} %select_n.48, s32[]{:T(128)S(6)} %select_n.46), kind=kLoop, calls=%fused_computation.17 | loop fusion | bytes 3145740 | tf_op jit(solution)/shard_map/dynamic_slice | solution.py:386
  105.5 4.7 %shard_map.177 = bf16[768,2048]{1,0:T(8,128)(2,1)} custom-call(bf16[768,512]{1,0:T(8,128)(2,1)} %get-tuple-element.25.back16, bf16[512,2304]{1,0:T(8,128)(2,1)} %all-gather.2.cloned.1.call-done.down.up), custom_call_target="tpu_custom_call" | custom-call | tf_op jit(solution)/shard_map/pallas_call | solution.py:249
  111.0 4.8 %all-to-all-start.3 = ((bf16[8,96,2048]{2,1,0:T(8,128)(2,1)}), bf16[8,96,2048]{2,1,0:T(8,128)(2,1)S(1)}, u32[]{:S(2)}, u32[]{:S(2)}) async-start(bf16[8,96,2048]{2,1,0:T(8,128)(2,1)} %bitcast.49), calls=%async_computation.3 | async-start | bytes 6291456 | tf_op jit(solution)/shard_map/all_to_all | solution.py:405
  116.6 2.9 %collective-permute-done.2.refs_2_.refs_6_ = bf16[1024,256]{1,0:T(8,128)(2,1)} collective-permute-done((bf16[1024,256]{1,0:T(8,128)(2,1)}, bf16[1024,256]{1,0:T(8,128)(2,1)}, u32[]{:S(2)}, u32[]{:S(2)}) %collective-permute-start.2) | collective-permute-done | bytes 524320 | tf_op jit(solution)/shard_map/ppermute | solution.py:43
  120.6 11.2 %collective-permute-done.refs_0_.refs_4_ = bf16[1024,256]{1,0:T(8,128)(2,1)} collective-permute-done((bf16[1024,256]{1,0:T(8,128)(2,1)}, bf16[1024,256]{1,0:T(8,128)(2,1)}, u32[]{:S(2)}, u32[]{:S(2)}) %collective-permute-start) | collective-permute-done | bytes 524320 | tf_op jit(solution)/shard_map/ppermute | solution.py:43
  140.5 10.2 %shard_map.170 = (f32[512,256]{1,0:T(8,128)}, f32[512,256]{1,0:T(8,128)}, f32[512,256]{1,0:T(8,128)}, f32[512,256]{1,0:T(8,128)}) custom-call(s32[2]{0:T(128)} %pad_add_fusion.at, bf16[512,2048]{1,0:T(8,128)(2,1)} %tokens.1, bf16[8192,256]{1,0:T(8,128)(2,1)} %own.3, bf16[1024,256]{1,0:T(8,128)(2,1)} %collective-permute-done.refs_0_.refs_4_, ...), custom_call_target="tpu_custom_call" | custom-call | tf_op jit(solution)/shard_map/pallas_call | solution.py:293
  153.2 7.0 %shard_map.178.base = f32[512,2048]{1,0:T(8,128)} custom-call(s32[2]{0:T(128)} %pad_add_fusion.at, bf16[8192,256]{1,0:T(8,128)(2,1)} %own.3, bf16[512,256]{1,0:T(8,128)(2,1)} %refs_0_.1, bf16[512,256]{1,0:T(8,128)(2,1)} %collective-permute-done.15.refs_1_, bf16[512,256]{1,0:T(8,128)(2,1)} %collective-permute-done.16.refs_2_, ...), custom_call_target="tpu_custom_call" | custom-call | tf_op jit(solution)/shard_map/pallas_call | solution.py:293
  161.4 3.6 %collective-permute-start.19 = (f32[2,64,256]{2,1,0:T(8,128)S(1)}, f32[2,64,256]{2,1,0:T(8,128)S(1)}, u32[]{:S(2)}, u32[]{:S(2)}) collective-permute-start(f32[2,64,256]{2,1,0:T(8,128)S(1)} %dynamic-slice_bitcast_fusion.1), channel_id=1, source_target_pairs={{0,64},{32,96},{64,0},{96,32},{128,192},{160,224},{192,128},{224,1... | collective-permute-start | bytes 393224 | tf_op jit(solution)/shard_map/ppermute | solution.py:416
  166.6 3.1 %collective-permute-done.19 = f32[2,64,256]{2,1,0:T(8,128)S(1)} collective-permute-done((f32[2,64,256]{2,1,0:T(8,128)S(1)}, f32[2,64,256]{2,1,0:T(8,128)S(1)}, u32[]{:S(2)}, u32[]{:S(2)}) %collective-permute-start.19) | collective-permute-done | bytes 131104 | tf_op jit(solution)/shard_map/ppermute | solution.py:416
  169.7 6.0 %collective-permute-start.20 = (f32[1,64,256]{2,1,0:T(8,128)S(1)}, f32[1,64,256]{2,1,0:T(8,128)S(1)}, u32[]{:S(2)}, u32[]{:S(2)}) collective-permute-start(f32[1,64,256]{2,1,0:T(8,128)S(1)} %constant_dynamic-slice_fusion), channel_id=1, source_target_pairs={{0,128},{32,160},{64,192},{96,224},{128,0},{160,32},{192,64},{224,... | collective-permute-start | bytes 196616 | tf_op jit(solution)/shard_map/ppermute | solution.py:416
  181.6 5.4 %shard_map.179 = bf16[512,2048]{1,0:T(8,128)(2,1)} custom-call(bf16[768,512]{1,0:T(8,128)(2,1)} %get-tuple-element.22.route, bf16[768,2048]{1,0:T(8,128)(2,1)} %bitcast.50, f32[512,2048]{1,0:T(8,128)} %shard_map.178.base), custom_call_target="tpu_custom_call" | custom-call | tf_op jit(solution)/shard_map/pallas_call | solution.py:339
  186.9 3.0 %fusion.3 = (f32[1,64,2048]{2,1,0:T(8,128)}, f32[1,64,2048]{2,1,0:T(8,128)}, f32[1,64,2048]{2,1,0:T(8,128)}) fusion(f32[64,2048]{1,0:T(8,128)} %reduce-scatter.2.cloned.1.call-done, f32[1,64,2048]{2,1,0:T(8,128)} %param.19, f32[1,64,2048]{2,1,0:T(8,128)} %param.18, f32[1,64,2048]{2,1,0:T(8,128)} %down.1), kind=kLoop, calls=%fused_computation.9 | loop fusion | flops 1572864 | bytes 3670016 | tf_op jit(solution)/shard_map/broadcast_in_dim | solution.py:427
  (82 shorter events, 42.3 us)
Async XLA Ops:
  7.2 47.3 %all-gather.2.cloned.1.call-start = ((), (), s32[]{:S(2)}) async-start(), calls=%async_computation.5 | async-start | bytes 2654208 | tf_op jit(solution)/shard_map/all_gather | solution.py:372
  11.6 13.1 %all-to-all-start.1 = ((bf16[8,96,256]{2,1,0:T(8,128)(2,1)}), bf16[8,96,256]{2,1,0:T(8,128)(2,1)S(1)}, u32[]{:S(2)}, u32[]{:S(2)}) async-start(bf16[8,96,256]{2,1,0:T(8,128)(2,1)} %bitcast.60), calls=%async_computation.1 | async-start | bytes 786432 | tf_op jit(solution)/shard_map/all_to_all | solution.py:381
  25.4 42.0 %all-to-all-start = ((bf16[8,96,2048]{2,1,0:T(8,128)(2,1)}), bf16[8,96,2048]{2,1,0:T(8,128)(2,1)S(1)}, u32[]{:S(2)}, u32[]{:S(2)}) async-start(bf16[8,96,2048]{2,1,0:T(8,128)(2,1)} %bitcast.53), calls=%async_computation | async-start | bytes 6291456 | tf_op jit(solution)/shard_map/all_to_all | solution.py:380
  30.4 156.5 %reduce-scatter.2.cloned.1.call-start = ((), (), s32[]{:S(2)}) async-start(), calls=%async_computation.6 | async-start | bytes 4718592 | tf_op jit(solution)/shard_map/reduce_scatter | solution.py:403
  56.7 10.7 %collective-permute-start.14 = (f32[384,128]{1,0:T(8,128)}, f32[384,128]{1,0:T(8,128)S(1)}, u32[]{:S(2)}, u32[]{:S(2)}) collective-permute-start(f32[384,128]{1,0:T(8,128)} %shard_map.175.a), channel_id=1, source_target_pairs={{0,3},{1,0},{2,1},{3,2},{4,7},{5,4},{6,5},{7,6},{8,11},{9,8},{10,9... | collective-permute-start | bytes 589832 | tf_op jit(solution)/shard_map/ppermute | solution.py:43
  60.3 8.8 %collective-permute-start.12 = (f32[384,128]{1,0:T(8,128)}, f32[384,128]{1,0:T(8,128)}, u32[]{:S(2)}, u32[]{:S(2)}) collective-permute-start(f32[384,128]{1,0:T(8,128)} %shard_map.175.a), channel_id=1, source_target_pairs={{0,1},{1,2},{2,3},{3,0},{4,5},{5,6},{6,7},{7,4},{8,9},{9,10},{10,1... | collective-permute-start | bytes 589832 | tf_op jit(solution)/shard_map/ppermute | solution.py:43
  79.2 10.7 %collective-permute-start.11 = (f32[384,128]{1,0:T(8,128)}, f32[384,128]{1,0:T(8,128)S(1)}, u32[]{:S(2)}, u32[]{:S(2)}) collective-permute-start(f32[384,128]{1,0:T(8,128)} %shard_map.173.a), channel_id=1, source_target_pairs={{0,3},{1,0},{2,1},{3,2},{4,7},{5,4},{6,5},{7,6},{8,11},{9,8},{10,9... | collective-permute-start | bytes 589832 | tf_op jit(solution)/shard_map/ppermute | solution.py:43
  81.4 9.5 %collective-permute-start.10 = (f32[384,128]{1,0:T(8,128)}, f32[384,128]{1,0:T(8,128)S(1)}, u32[]{:S(2)}, u32[]{:S(2)}) collective-permute-start(f32[384,128]{1,0:T(8,128)} %shard_map.173.a), channel_id=1, source_target_pairs={{0,2},{1,3},{2,0},{3,1},{4,6},{5,7},{6,4},{7,5},{8,10},{9,11},{10,... | collective-permute-start | bytes 589832 | tf_op jit(solution)/shard_map/ppermute | solution.py:43
  82.0 11.4 %collective-permute-start.9 = (f32[384,128]{1,0:T(8,128)}, f32[384,128]{1,0:T(8,128)S(1)}, u32[]{:S(2)}, u32[]{:S(2)}) collective-permute-start(f32[384,128]{1,0:T(8,128)} %shard_map.173.a), channel_id=1, source_target_pairs={{0,1},{1,2},{2,3},{3,0},{4,5},{5,6},{6,7},{7,4},{8,9},{9,10},{10,1... | collective-permute-start | bytes 589832 | tf_op jit(solution)/shard_map/ppermute | solution.py:43
  97.0 13.2 %all-to-all-start.2 = ((bf16[8,96,256]{2,1,0:T(8,128)(2,1)}), bf16[8,96,256]{2,1,0:T(8,128)(2,1)S(1)}, u32[]{:S(2)}, u32[]{:S(2)}) async-start(bf16[8,96,256]{2,1,0:T(8,128)(2,1)} %bitcast.59), calls=%async_computation.2 | async-start | bytes 786432 | tf_op jit(solution)/shard_map/all_to_all | solution.py:409
  104.4 15.1 %collective-permute-start.2 = (bf16[1024,256]{1,0:T(8,128)(2,1)}, bf16[1024,256]{1,0:T(8,128)(2,1)}, u32[]{:S(2)}, u32[]{:S(2)}) collective-permute-start(bf16[1024,256]{1,0:T(8,128)(2,1)} %get-tuple-element.31), channel_id=1, source_target_pairs={{0,3},{1,0},{2,1},{3,2},{4,7},{5,4},{6,5},{7,6},{8,11},{9,8},{10,9... | collective-permute-start | bytes 1572872 | tf_op jit(solution)/shard_map/ppermute | solution.py:43
  105.1 15.5 %collective-permute-start.1 = (bf16[1024,256]{1,0:T(8,128)(2,1)}, bf16[1024,256]{1,0:T(8,128)(2,1)}, u32[]{:S(2)}, u32[]{:S(2)}) collective-permute-start(bf16[1024,256]{1,0:T(8,128)(2,1)} %get-tuple-element.32), channel_id=1, source_target_pairs={{0,2},{1,3},{2,0},{3,1},{4,6},{5,7},{6,4},{7,5},{8,10},{9,11},{10,... | collective-permute-start | bytes 1572872 | tf_op jit(solution)/shard_map/ppermute | solution.py:43
  111.0 69.0 %all-to-all-start.3 = ((bf16[8,96,2048]{2,1,0:T(8,128)(2,1)}), bf16[8,96,2048]{2,1,0:T(8,128)(2,1)S(1)}, u32[]{:S(2)}, u32[]{:S(2)}) async-start(bf16[8,96,2048]{2,1,0:T(8,128)(2,1)} %bitcast.49), calls=%async_computation.3 | async-start | bytes 6291456 | tf_op jit(solution)/shard_map/all_to_all | solution.py:405
  115.8 16.1 %collective-permute-start = (bf16[1024,256]{1,0:T(8,128)(2,1)}, bf16[1024,256]{1,0:T(8,128)(2,1)}, u32[]{:S(2)}, u32[]{:S(2)}) collective-permute-start(bf16[1024,256]{1,0:T(8,128)(2,1)} %get-tuple-element.33), channel_id=1, source_target_pairs={{0,1},{1,2},{2,3},{3,0},{4,5},{5,6},{6,7},{7,4},{8,9},{9,10},{10,1... | collective-permute-start | bytes 1572872 | tf_op jit(solution)/shard_map/ppermute | solution.py:43
  119.5 16.6 %collective-permute-start.5 = (bf16[1024,256]{1,0:T(8,128)(2,1)}, bf16[1024,256]{1,0:T(8,128)(2,1)}, u32[]{:S(2)}, u32[]{:S(2)}) collective-permute-start(bf16[1024,256]{1,0:T(8,128)(2,1)} %collective-permute-done.2.refs_2_.refs_6_), channel_id=1, source_target_pairs={{0,4},{4,0},{1,5},{5,1},{2,6},{6,2},{3,7},{7,3},{8,12},{12,8},{9,1... | collective-permute-start | bytes 1572872 | tf_op jit(solution)/shard_map/ppermute | solution.py:390
  120.6 17.5 %collective-permute-start.4 = (bf16[1024,256]{1,0:T(8,128)(2,1)}, bf16[1024,256]{1,0:T(8,128)(2,1)}, u32[]{:S(2)}, u32[]{:S(2)}) collective-permute-start(bf16[1024,256]{1,0:T(8,128)(2,1)} %collective-permute-done.1.refs_1_.refs_5_), channel_id=1, source_target_pairs={{0,4},{4,0},{1,5},{5,1},{2,6},{6,2},{3,7},{7,3},{8,12},{12,8},{9,1... | collective-permute-start | bytes 1572872 | tf_op jit(solution)/shard_map/ppermute | solution.py:390
  131.8 18.9 %collective-permute-start.16 = (bf16[512,256]{1,0:T(8,128)(2,1)S(1)}, bf16[512,256]{1,0:T(8,128)(2,1)}, u32[]{:S(2)}, u32[]{:S(2)}) collective-permute-start(bf16[512,256]{1,0:T(8,128)(2,1)S(1)} %copy-done.3), channel_id=1, source_target_pairs={{0,2},{1,3},{2,0},{3,1},{4,6},{5,7},{6,4},{7,5},{8,10},{9,11},{10,... | collective-permute-start | bytes 786440 | tf_op jit(solution)/shard_map/ppermute | solution.py:43
  133.2 19.7 %collective-permute-start.15 = (bf16[512,256]{1,0:T(8,128)(2,1)S(1)}, bf16[512,256]{1,0:T(8,128)(2,1)}, u32[]{:S(2)}, u32[]{:S(2)}) collective-permute-start(bf16[512,256]{1,0:T(8,128)(2,1)S(1)} %copy-done.3), channel_id=1, source_target_pairs={{0,1},{1,2},{2,3},{3,0},{4,5},{5,6},{6,7},{7,4},{8,9},{9,10},{10,1... | collective-permute-start | bytes 786440 | tf_op jit(solution)/shard_map/ppermute | solution.py:43
  136.0 17.1 %collective-permute-start.17 = (bf16[512,256]{1,0:T(8,128)(2,1)S(1)}, bf16[512,256]{1,0:T(8,128)(2,1)}, u32[]{:S(2)}, u32[]{:S(2)}) collective-permute-start(bf16[512,256]{1,0:T(8,128)(2,1)S(1)} %copy-done.3), channel_id=1, source_target_pairs={{0,3},{1,0},{2,1},{3,2},{4,7},{5,4},{6,5},{7,6},{8,11},{9,8},{10,9... | collective-permute-start | bytes 786440 | tf_op jit(solution)/shard_map/ppermute | solution.py:43
  138.1 22.1 %collective-permute-start.18 = (f32[4,64,256]{2,1,0:T(8,128)}, f32[4,64,256]{2,1,0:T(8,128)}, u32[]{:S(2)}, u32[]{:S(2)}) collective-permute-start(f32[4,64,256]{2,1,0:T(8,128)} %dynamic-slice_bitcast_fusion), channel_id=1, source_target_pairs={{0,32},{32,0},{64,96},{96,64},{128,160},{160,128},{192,224},{224,1... | collective-permute-start | bytes 786440 | tf_op jit(solution)/shard_map/ppermute | solution.py:416
  150.7 25.1 %collective-permute-start.6 = (f32[512,256]{1,0:T(8,128)}, f32[512,256]{1,0:T(8,128)}, u32[]{:S(2)}, u32[]{:S(2)}) collective-permute-start(f32[512,256]{1,0:T(8,128)} %get-tuple-element.19), channel_id=1, source_target_pairs={{0,3},{1,0},{2,1},{3,2},{4,7},{5,4},{6,5},{7,6},{8,11},{9,8},{10,9... | collective-permute-start | bytes 1572872 | tf_op jit(solution)/shard_map/ppermute | solution.py:43
  150.8 25.0 %collective-permute-start.7 = (f32[512,256]{1,0:T(8,128)}, f32[512,256]{1,0:T(8,128)}, u32[]{:S(2)}, u32[]{:S(2)}) collective-permute-start(f32[512,256]{1,0:T(8,128)} %get-tuple-element.20), channel_id=1, source_target_pairs={{0,2},{1,3},{2,0},{3,1},{4,6},{5,7},{6,4},{7,5},{8,10},{9,11},{10,... | collective-permute-start | bytes 1572872 | tf_op jit(solution)/shard_map/ppermute | solution.py:43
  152.9 24.1 %collective-permute-start.8 = (f32[512,256]{1,0:T(8,128)}, f32[512,256]{1,0:T(8,128)}, u32[]{:S(2)}, u32[]{:S(2)}) collective-permute-start(f32[512,256]{1,0:T(8,128)} %get-tuple-element.21), channel_id=1, source_target_pairs={{0,1},{1,2},{2,3},{3,0},{4,5},{5,6},{6,7},{7,4},{8,9},{9,10},{10,1... | collective-permute-start | bytes 1572872 | tf_op jit(solution)/shard_map/ppermute | solution.py:43
  169.7 9.5 %collective-permute-start.20 = (f32[1,64,256]{2,1,0:T(8,128)S(1)}, f32[1,64,256]{2,1,0:T(8,128)S(1)}, u32[]{:S(2)}, u32[]{:S(2)}) collective-permute-start(f32[1,64,256]{2,1,0:T(8,128)S(1)} %constant_dynamic-slice_fusion), channel_id=1, source_target_pairs={{0,128},{32,160},{64,192},{96,224},{128,0},{160,32},{192,64},{224,... | collective-permute-start | bytes 196616 | tf_op jit(solution)/shard_map/ppermute | solution.py:416
  (17 other events, 135.5 us)
Sparse Core Ops, SparseCore 0:
  10.3 44.1 all-gather.1
  74.6 56.5 reduce-scatter.1

commit v4 on v3

--- a/solution.py
+++ b/solution.py
@@ -407,14 +407,17 @@
     hidden = parts_of(run_hid(x_rows, all16))
     adapter_out, up_part = run_up(hidden, g_rows, all16, feat)
     ret_out = lax.all_to_all(adapter_out, ("x", "c"), 0, 0, tiled=True)
-    grad_up = up_part
-    for bit in range(3):
-        split = grad_up.reshape(-1, 2, rank, keyw)
-        here = lax.shift_right_logical(z, bit) & 1
-        keep = lax.dynamic_index_in_dim(split, here, 1, keepdims=False)
-        give = lax.dynamic_index_in_dim(split, 1 - here, 1, keepdims=False)
-        grad_up = keep + lax.ppermute(give, "z", [(i, i ^ (1 << bit)) for i in range(NZ)])
-    grad_up = grad_up.reshape(rank, keyw)
+    split = up_part.reshape(NZ // 2, 2, rank, keyw)
+    keep = lax.dynamic_index_in_dim(split, z % 2, 1, keepdims=False)
+    give = lax.dynamic_index_in_dim(split, 1 - z % 2, 1, keepdims=False)
+    keep = keep + lax.ppermute(give, "z", [(i, i ^ 1) for i in range(NZ)])
+    nq = NZ // 2
+    grad_up = lax.dynamic_index_in_dim(keep, z // 2, 0, keepdims=False)
+    for k in range(1, nq):
+        give = lax.dynamic_index_in_dim(keep, (z // 2 + k) % nq, 0, keepdims=False)
+        grad_up = grad_up + lax.ppermute(
+            give, "z", [(i, (i // 2 + k) % nq * 2 + i % 2) for i in range(NZ)]
+        )
 
     layer_out = (base_out + dot(route, ret_out, ((0,), (0,)))).astype(bf16)
     input_grad = run_final(route, ret_grad, base_grad)

time: 198 us -> 223 us (1.13)
  waiting for transfers between devices: 64.3 us -> 81.4 us
  starting transfers between devices: 49 us -> 53.7 us
  other arithmetic: 7.62 us -> 10.1 us
    ppermute x15, waiting for transfers between devices: 28.6 us -> 46 us  [shift(): return lax.ppermute(v, 't', [(i, (i + k) % NT) for i in range(NT)])]
    broadcast_in_dim x1 -> x3, other arithmetic: 2.99 us -> 6.2 us  [step(): v[None]]
    ppermute x3 -> x4, waiting for transfers between devices: 3.07 us -> 0.01 us  [the longest x3 0.01 us: step(): lax.ppermute(give, 'z', [(i, (i // 2 + k) % nq * 2 + i % 2) for i in rang...]
    all_to_all x1, waiting for transfers between devices: 0.01 us -> 2.79 us  [step(): ret_out = lax.all_to_all(adapter_out, ('x', 'c'), 0, 0, tiled=True)]
    ppermute x15, starting transfers between devices: 17.3 us -> 20 us  [shift(): return lax.ppermute(v, 't', [(i, (i + k) % NT) for i in range(NT)])]
    ppermute x3 -> x4, starting transfers between devices: 11.5 us -> 13.2 us  [the longest x3 11.3 us: step(): lax.ppermute(give, 'z', [(i, (i // 2 + k) % nq * 2 + i % 2) for i in rang...]
    unnamed x28 -> x24, local copies, waits for them, and re-layouts: 3.89 us -> 4.61 us
  transfers between devices with their start and end apart: 27 -> 28, of which waited for: 12 -> 15; matrix products, arithmetic and copies ran while one was open for 8% -> 8% of each run, Pallas kernels for 20% -> 18%
where the time goes in v4:
time: 223 us; the launch traced here: 222 us
  waiting for transfers between devices  81.4 us (37%)
  starting transfers between devices  53.7 us (24%)
  Pallas kernels  46.8 us (21%)
  between operations  14.1 us (6%)
  other arithmetic  10.1 us (5%)
  local copies, waits for them, and re-layouts  9.56 us (4%)
  matrix products  6.81 us (3%)
    ppermute x15, waiting for transfers between devices, shift(): return lax.ppermute(v, 't', [(i, (i + k) % NT) for i in range(NT)])  46 us
    all_gather x1, waiting for transfers between devices, step(): all16 = lax.all_gather(both16, 'z', axis=0, tiled=True)  24.1 us
    ppermute x15, starting transfers between devices, shift(): return lax.ppermute(v, 't', [(i, (i + k) % NT) for i in range(NT)])  20 us
    pallas_call x2, Pallas kernels, run_base(): pl.pallas_call(kernel, out_shape=outs, grid_spec=pltpu.PrefetchScalarGrid...  17.2 us
    ppermute x3, starting transfers between devices, step(): lax.ppermute(give, 'z', [(i, (i // 2 + k) % nq * 2 + i % 2) for i in rang...  11.3 us
    dot_general x2, matrix products, dot(): return lax.dot_general(a, b, (dims, ((), ())), preferred_element_type=out)  6.81 us
    all_to_all x1, waiting for transfers between devices, step(): x_rows = lax.all_to_all(x_send, ('x', 'c'), 0, 0, tiled=True)  6.22 us
    broadcast_in_dim x3, other arithmetic, step(): v[None]  6.2 us
  transfers between devices with their start and end apart: 28, of which 15 were waited for; matrix products, arithmetic and copies ran while one was open for 8% of the time, Pallas kernels for 18%

profile of v4, /device:TPU:2, one launch (start us, length us, event | category | flops | bytes accessed | tf_op | source)
XLA Modules:
  0.0 222.5 jit_solution(16984092131257718202)
XLA Ops:
  11.6 5.6 %all-to-all-start.1 = ((bf16[8,96,256]{2,1,0:T(8,128)(2,1)}), bf16[8,96,256]{2,1,0:T(8,128)(2,1)S(1)}, u32[]{:S(2)}, u32[]{:S(2)}) async-start(bf16[8,96,256]{2,1,0:T(8,128)(2,1)} %bitcast.88), calls=%async_computation.1 | async-start | bytes 786432 | tf_op jit(solution)/shard_map/all_to_all | solution.py:381
  17.2 5.3 %fusion.10 = bf16[768,2048]{1,0:T(8,128)(2,1)} fusion(bf16[768,512]{1,0:T(8,128)(2,1)} %get-tuple-element.22.route, bf16[512,2048]{1,0:T(8,128)(2,1)} %tokens.1), kind=kOutput, calls=%fused_computation.26 | convolution fusion | flops 1610612736 | bytes 6029312 | tf_op jit(solution)/shard_map/dot_general | solution.py:47
  25.4 5.0 %all-to-all-start = ((bf16[8,96,2048]{2,1,0:T(8,128)(2,1)}), bf16[8,96,2048]{2,1,0:T(8,128)(2,1)S(1)}, u32[]{:S(2)}, u32[]{:S(2)}) async-start(bf16[8,96,2048]{2,1,0:T(8,128)(2,1)} %bitcast.83), calls=%async_computation | async-start | bytes 6291456 | tf_op jit(solution)/shard_map/all_to_all | solution.py:380
  30.4 24.1 %all-gather.2.cloned.1.call-done.down.up = bf16[512,2304]{1,0:T(8,128)(2,1)} async-done(((bf16[64,2304]{1,0:T(8,128)(2,1)}), bf16[512,2304]{1,0:T(8,128)(2,1)}) %all-gather.2.cloned.1.call-update) | async-done | bytes 2359312 | tf_op jit(solution)/shard_map/all_gather | solution.py:372
  61.2 6.2 %all-to-all-done = bf16[8,96,2048]{2,1,0:T(8,128)(2,1)S(1)} async-done(((bf16[8,96,2048]{2,1,0:T(8,128)(2,1)}), bf16[8,96,2048]{2,1,0:T(8,128)(2,1)S(1)}, u32[]{:S(2)}, u32[]{:S(2)}) %all-to-all-start) | async-done | bytes 3145760 | tf_op jit(solution)/shard_map/all_to_all | solution.py:380
  69.2 5.3 %shard_map.176 = (bf16[768,512]{1,0:T(8,128)(2,1)}, f32[512,2048]{1,0:T(8,128)}) custom-call(f32[384,128]{1,0:T(8,128)} %shard_map.175.a, f32[384,128]{1,0:T(8,128)} %collective-permute-done.12.b, f32[384,128]{1,0:T(8,128)} %copy-done.11, f32[384,128]{1,0:T(8,128)} %copy-done.10, bf16[768,2048]{1,0:T(8,128)(2,1)} %bitcast.77), custom_call_target="tpu_custom_call" | custom-call | tf_op jit(solution)/shard_map/pallas_call | solution.py:237
  74.5 4.7 %shard_map.173.a = f32[384,128]{1,0:T(8,128)} custom-call(bf16[768,2048]{1,0:T(8,128)(2,1)} %bitcast.78, bf16[512,2304]{1,0:T(8,128)(2,1)} %all-gather.2.cloned.1.call-done.down.up), custom_call_target="tpu_custom_call" | custom-call | tf_op jit(solution)/shard_map/pallas_call | solution.py:261
  83.0 6.8 %collective-permute-done.11.d = f32[384,128]{1,0:T(8,128)S(1)} collective-permute-done((f32[384,128]{1,0:T(8,128)}, f32[384,128]{1,0:T(8,128)S(1)}, u32[]{:S(2)}, u32[]{:S(2)}) %collective-permute-start.11) | collective-permute-done | bytes 196640 | tf_op jit(solution)/shard_map/ppermute | solution.py:43
  97.0 4.8 %all-to-all-start.2 = ((bf16[8,96,256]{2,1,0:T(8,128)(2,1)}), bf16[8,96,256]{2,1,0:T(8,128)(2,1)S(1)}, u32[]{:S(2)}, u32[]{:S(2)}) async-start(bf16[8,96,256]{2,1,0:T(8,128)(2,1)} %bitcast.87), calls=%async_computation.2 | async-start | bytes 786432 | tf_op jit(solution)/shard_map/all_to_all | solution.py:409
  101.9 4.7 %shard_map.177 = bf16[768,2048]{1,0:T(8,128)(2,1)} custom-call(bf16[768,512]{1,0:T(8,128)(2,1)} %get-tuple-element.25.back16, bf16[512,2304]{1,0:T(8,128)(2,1)} %all-gather.2.cloned.1.call-done.down.up), custom_call_target="tpu_custom_call" | custom-call | tf_op jit(solution)/shard_map/pallas_call | solution.py:249
  110.1 5.0 %all-to-all-start.3 = ((bf16[8,96,2048]{2,1,0:T(8,128)(2,1)}), bf16[8,96,2048]{2,1,0:T(8,128)(2,1)S(1)}, u32[]{:S(2)}, u32[]{:S(2)}) async-start(bf16[8,96,2048]{2,1,0:T(8,128)(2,1)} %bitcast.79), calls=%async_computation.3 | async-start | bytes 6291456 | tf_op jit(solution)/shard_map/all_to_all | solution.py:405
  119.8 4.1 %collective-permute-start.16 = (bf16[512,256]{1,0:T(8,128)(2,1)S(1)}, bf16[512,256]{1,0:T(8,128)(2,1)}, u32[]{:S(2)}, u32[]{:S(2)}) collective-permute-start(bf16[512,256]{1,0:T(8,128)(2,1)S(1)} %copy-done.3), channel_id=1, source_target_pairs={{0,2},{1,3},{2,0},{3,1},{4,6},{5,7},{6,4},{7,5},{8,10},{9,11},{10,... | collective-permute-start | bytes 786440 | tf_op jit(solution)/shard_map/ppermute | solution.py:43
  127.5 5.3 %collective-permute-done.2.refs_2_.refs_6_ = bf16[1024,256]{1,0:T(8,128)(2,1)} collective-permute-done((bf16[1024,256]{1,0:T(8,128)(2,1)}, bf16[1024,256]{1,0:T(8,128)(2,1)}, u32[]{:S(2)}, u32[]{:S(2)}) %collective-permute-start.2) | collective-permute-done | bytes 524320 | tf_op jit(solution)/shard_map/ppermute | solution.py:43
  135.1 11.1 %collective-permute-done.refs_0_.refs_4_ = bf16[1024,256]{1,0:T(8,128)(2,1)} collective-permute-done((bf16[1024,256]{1,0:T(8,128)(2,1)}, bf16[1024,256]{1,0:T(8,128)(2,1)}, u32[]{:S(2)}, u32[]{:S(2)}) %collective-permute-start) | collective-permute-done | bytes 524320 | tf_op jit(solution)/shard_map/ppermute | solution.py:43
  146.3 4.6 %collective-permute-done.16.refs_2_ = bf16[512,256]{1,0:T(8,128)(2,1)} collective-permute-done((bf16[512,256]{1,0:T(8,128)(2,1)S(1)}, bf16[512,256]{1,0:T(8,128)(2,1)}, u32[]{:S(2)}, u32[]{:S(2)}) %collective-permute-start.16) | collective-permute-done | bytes 262176 | tf_op jit(solution)/shard_map/ppermute | solution.py:43
  150.9 3.2 %collective-permute-start.17 = (bf16[512,256]{1,0:T(8,128)(2,1)S(1)}, bf16[512,256]{1,0:T(8,128)(2,1)}, u32[]{:S(2)}, u32[]{:S(2)}) collective-permute-start(bf16[512,256]{1,0:T(8,128)(2,1)S(1)} %copy-done.3), channel_id=1, source_target_pairs={{0,3},{1,0},{2,1},{3,2},{4,7},{5,4},{6,5},{7,6},{8,11},{9,8},{10,9... | collective-permute-start | bytes 786440 | tf_op jit(solution)/shard_map/ppermute | solution.py:43
  156.6 3.2 %collective-permute-start.19 = (f32[64,256]{1,0:T(8,128)}, f32[64,256]{1,0:T(8,128)}, u32[]{:S(2)}, u32[]{:S(2)}) collective-permute-start(f32[64,256]{1,0:T(8,128)} %get-tuple-element.36), channel_id=1, source_target_pairs={{0,64},{32,96},{64,128},{96,160},{128,192},{160,224},{192,0},{224,... | collective-permute-start | bytes 196616 | tf_op jit(solution)/shard_map/ppermute | solution.py:418
  159.8 3.1 %collective-permute-start.21 = (f32[64,256]{1,0:T(8,128)}, f32[64,256]{1,0:T(8,128)}, u32[]{:S(2)}, u32[]{:S(2)}) collective-permute-start(f32[64,256]{1,0:T(8,128)} %get-tuple-element.37), channel_id=1, source_target_pairs={{0,192},{32,224},{64,0},{96,32},{128,64},{160,96},{192,128},{224,1... | collective-permute-start | bytes 196616 | tf_op jit(solution)/shard_map/ppermute | solution.py:418
  163.0 4.9 %collective-permute-start.20 = (f32[64,256]{1,0:T(8,128)}, f32[64,256]{1,0:T(8,128)}, u32[]{:S(2)}, u32[]{:S(2)}) collective-permute-start(f32[64,256]{1,0:T(8,128)} %get-tuple-element.38), channel_id=1, source_target_pairs={{0,128},{32,160},{64,192},{96,224},{128,0},{160,32},{192,64},{224,... | collective-permute-start | bytes 196616 | tf_op jit(solution)/shard_map/ppermute | solution.py:418
  168.5 10.2 %shard_map.170 = (f32[512,256]{1,0:T(8,128)}, f32[512,256]{1,0:T(8,128)}, f32[512,256]{1,0:T(8,128)}, f32[512,256]{1,0:T(8,128)}) custom-call(s32[2]{0:T(128)} %pad_add_fusion.at, bf16[512,2048]{1,0:T(8,128)(2,1)} %tokens.1, bf16[8192,256]{1,0:T(8,128)(2,1)} %own.3, bf16[1024,256]{1,0:T(8,128)(2,1)} %collective-permute-done.refs_0_.refs_4_, ...), custom_call_target="tpu_custom_call" | custom-call | tf_op jit(solution)/shard_map/pallas_call | solution.py:293
  179.6 7.1 %shard_map.178.base = f32[512,2048]{1,0:T(8,128)} custom-call(s32[2]{0:T(128)} %pad_add_fusion.at, bf16[8192,256]{1,0:T(8,128)(2,1)} %own.3, bf16[512,256]{1,0:T(8,128)(2,1)} %refs_0_.1, bf16[512,256]{1,0:T(8,128)(2,1)} %collective-permute-done.15.refs_1_, bf16[512,256]{1,0:T(8,128)(2,1)} %collective-permute-done.16.refs_2_, ...), custom_call_target="tpu_custom_call" | custom-call | tf_op jit(solution)/shard_map/pallas_call | solution.py:293
  194.7 8.8 %collective-permute-done.8 = f32[512,256]{1,0:T(8,128)S(1)} collective-permute-done((f32[512,256]{1,0:T(8,128)}, f32[512,256]{1,0:T(8,128)S(1)}, u32[]{:S(2)}, u32[]{:S(2)}) %collective-permute-start.8) | collective-permute-done | bytes 524320 | tf_op jit(solution)/shard_map/ppermute | solution.py:43
  207.2 5.4 %shard_map.179 = bf16[512,2048]{1,0:T(8,128)(2,1)} custom-call(bf16[768,512]{1,0:T(8,128)(2,1)} %get-tuple-element.22.route, bf16[768,2048]{1,0:T(8,128)(2,1)} %bitcast.80, f32[512,2048]{1,0:T(8,128)} %shard_map.178.base), custom_call_target="tpu_custom_call" | custom-call | tf_op jit(solution)/shard_map/pallas_call | solution.py:339
  212.6 3.0 %fusion.3 = (f32[1,64,2048]{2,1,0:T(8,128)}, f32[1,64,2048]{2,1,0:T(8,128)}, f32[1,64,2048]{2,1,0:T(8,128)}) fusion(f32[64,2048]{1,0:T(8,128)} %reduce-scatter.2.cloned.1.call-done, f32[1,64,2048]{2,1,0:T(8,128)} %param.19, f32[1,64,2048]{2,1,0:T(8,128)} %param.18, f32[1,64,2048]{2,1,0:T(8,128)} %down.1), kind=kLoop, calls=%fused_computation.9 | loop fusion | flops 1572864 | bytes 3670016 | tf_op jit(solution)/shard_map/broadcast_in_dim | solution.py:430
  (79 shorter events, 56.7 us)
Async XLA Ops:
  7.2 47.3 %all-gather.2.cloned.1.call-start = ((), (), s32[]{:S(2)}) async-start(), calls=%async_computation.5 | async-start | bytes 2654208 | tf_op jit(solution)/shard_map/all_gather | solution.py:372
  11.6 13.1 %all-to-all-start.1 = ((bf16[8,96,256]{2,1,0:T(8,128)(2,1)}), bf16[8,96,256]{2,1,0:T(8,128)(2,1)S(1)}, u32[]{:S(2)}, u32[]{:S(2)}) async-start(bf16[8,96,256]{2,1,0:T(8,128)(2,1)} %bitcast.88), calls=%async_computation.1 | async-start | bytes 786432 | tf_op jit(solution)/shard_map/all_to_all | solution.py:381
  25.4 42.0 %all-to-all-start = ((bf16[8,96,2048]{2,1,0:T(8,128)(2,1)}), bf16[8,96,2048]{2,1,0:T(8,128)(2,1)S(1)}, u32[]{:S(2)}, u32[]{:S(2)}) async-start(bf16[8,96,2048]{2,1,0:T(8,128)(2,1)} %bitcast.83), calls=%async_computation | async-start | bytes 6291456 | tf_op jit(solution)/shard_map/all_to_all | solution.py:380
  30.4 182.2 %reduce-scatter.2.cloned.1.call-start = ((), (), s32[]{:S(2)}) async-start(), calls=%async_computation.6 | async-start | bytes 4718592 | tf_op jit(solution)/shard_map/reduce_scatter | solution.py:403
  56.7 10.7 %collective-permute-start.14 = (f32[384,128]{1,0:T(8,128)}, f32[384,128]{1,0:T(8,128)S(1)}, u32[]{:S(2)}, u32[]{:S(2)}) collective-permute-start(f32[384,128]{1,0:T(8,128)} %shard_map.175.a), channel_id=1, source_target_pairs={{0,3},{1,0},{2,1},{3,2},{4,7},{5,4},{6,5},{7,6},{8,11},{9,8},{10,9... | collective-permute-start | bytes 589832 | tf_op jit(solution)/shard_map/ppermute | solution.py:43
  82.1 11.4 %collective-permute-start.9 = (f32[384,128]{1,0:T(8,128)}, f32[384,128]{1,0:T(8,128)S(1)}, u32[]{:S(2)}, u32[]{:S(2)}) collective-permute-start(f32[384,128]{1,0:T(8,128)} %shard_map.173.a), channel_id=1, source_target_pairs={{0,1},{1,2},{2,3},{3,0},{4,5},{5,6},{6,7},{7,4},{8,9},{9,10},{10,1... | collective-permute-start | bytes 589832 | tf_op jit(solution)/shard_map/ppermute | solution.py:43
  97.0 12.3 %all-to-all-start.2 = ((bf16[8,96,256]{2,1,0:T(8,128)(2,1)}), bf16[8,96,256]{2,1,0:T(8,128)(2,1)S(1)}, u32[]{:S(2)}, u32[]{:S(2)}) async-start(bf16[8,96,256]{2,1,0:T(8,128)(2,1)} %bitcast.87), calls=%async_computation.2 | async-start | bytes 786432 | tf_op jit(solution)/shard_map/all_to_all | solution.py:409
  110.1 95.5 %all-to-all-start.3 = ((bf16[8,96,2048]{2,1,0:T(8,128)(2,1)}), bf16[8,96,2048]{2,1,0:T(8,128)(2,1)S(1)}, u32[]{:S(2)}, u32[]{:S(2)}) async-start(bf16[8,96,2048]{2,1,0:T(8,128)(2,1)} %bitcast.79), calls=%async_computation.3 | async-start | bytes 6291456 | tf_op jit(solution)/shard_map/all_to_all | solution.py:405
  117.7 15.1 %collective-permute-start.2 = (bf16[1024,256]{1,0:T(8,128)(2,1)}, bf16[1024,256]{1,0:T(8,128)(2,1)}, u32[]{:S(2)}, u32[]{:S(2)}) collective-permute-start(bf16[1024,256]{1,0:T(8,128)(2,1)} %get-tuple-element.30), channel_id=1, source_target_pairs={{0,3},{1,0},{2,1},{3,2},{4,7},{5,4},{6,5},{7,6},{8,11},{9,8},{10,9... | collective-permute-start | bytes 1572872 | tf_op jit(solution)/shard_map/ppermute | solution.py:43
  118.5 16.7 %collective-permute-start.1 = (bf16[1024,256]{1,0:T(8,128)(2,1)}, bf16[1024,256]{1,0:T(8,128)(2,1)}, u32[]{:S(2)}, u32[]{:S(2)}) collective-permute-start(bf16[1024,256]{1,0:T(8,128)(2,1)} %get-tuple-element.31), channel_id=1, source_target_pairs={{0,2},{1,3},{2,0},{3,1},{4,6},{5,7},{6,4},{7,5},{8,10},{9,11},{10,... | collective-permute-start | bytes 1572872 | tf_op jit(solution)/shard_map/ppermute | solution.py:43
  118.9 27.4 %collective-permute-start = (bf16[1024,256]{1,0:T(8,128)(2,1)}, bf16[1024,256]{1,0:T(8,128)(2,1)}, u32[]{:S(2)}, u32[]{:S(2)}) collective-permute-start(bf16[1024,256]{1,0:T(8,128)(2,1)} %get-tuple-element.32), channel_id=1, source_target_pairs={{0,1},{1,2},{2,3},{3,0},{4,5},{5,6},{6,7},{7,4},{8,9},{9,10},{10,1... | collective-permute-start | bytes 1572872 | tf_op jit(solution)/shard_map/ppermute | solution.py:43
  119.8 31.1 %collective-permute-start.16 = (bf16[512,256]{1,0:T(8,128)(2,1)S(1)}, bf16[512,256]{1,0:T(8,128)(2,1)}, u32[]{:S(2)}, u32[]{:S(2)}) collective-permute-start(bf16[512,256]{1,0:T(8,128)(2,1)S(1)} %copy-done.3), channel_id=1, source_target_pairs={{0,2},{1,3},{2,0},{3,1},{4,6},{5,7},{6,4},{7,5},{8,10},{9,11},{10,... | collective-permute-start | bytes 786440 | tf_op jit(solution)/shard_map/ppermute | solution.py:43
  125.6 25.3 %collective-permute-start.18 = (f32[4,64,256]{2,1,0:T(8,128)}, f32[4,64,256]{2,1,0:T(8,128)}, u32[]{:S(2)}, u32[]{:S(2)}) collective-permute-start(f32[4,64,256]{2,1,0:T(8,128)} %dynamic-slice_bitcast_fusion), channel_id=1, source_target_pairs={{0,32},{32,0},{64,96},{96,64},{128,160},{160,128},{192,224},{224,1... | collective-permute-start | bytes 786440 | tf_op jit(solution)/shard_map/ppermute | solution.py:413
  132.8 23.7 %collective-permute-start.5 = (bf16[1024,256]{1,0:T(8,128)(2,1)}, bf16[1024,256]{1,0:T(8,128)(2,1)}, u32[]{:S(2)}, u32[]{:S(2)}) collective-permute-start(bf16[1024,256]{1,0:T(8,128)(2,1)} %collective-permute-done.2.refs_2_.refs_6_), channel_id=1, source_target_pairs={{0,4},{4,0},{1,5},{5,1},{2,6},{6,2},{3,7},{7,3},{8,12},{12,8},{9,1... | collective-permute-start | bytes 1572872 | tf_op jit(solution)/shard_map/ppermute | solution.py:390
  135.1 24.7 %collective-permute-start.4 = (bf16[1024,256]{1,0:T(8,128)(2,1)}, bf16[1024,256]{1,0:T(8,128)(2,1)}, u32[]{:S(2)}, u32[]{:S(2)}) collective-permute-start(bf16[1024,256]{1,0:T(8,128)(2,1)} %collective-permute-done.1.refs_1_.refs_5_), channel_id=1, source_target_pairs={{0,4},{4,0},{1,5},{5,1},{2,6},{6,2},{3,7},{7,3},{8,12},{12,8},{9,1... | collective-permute-start | bytes 1572872 | tf_op jit(solution)/shard_map/ppermute | solution.py:390
  146.3 16.7 %collective-permute-start.3 = (bf16[1024,256]{1,0:T(8,128)(2,1)}, bf16[1024,256]{1,0:T(8,128)(2,1)}, u32[]{:S(2)}, u32[]{:S(2)}) collective-permute-start(bf16[1024,256]{1,0:T(8,128)(2,1)} %collective-permute-done.refs_0_.refs_4_), channel_id=1, source_target_pairs={{0,4},{4,0},{1,5},{5,1},{2,6},{6,2},{3,7},{7,3},{8,12},{12,8},{9,1... | collective-permute-start | bytes 1572872 | tf_op jit(solution)/shard_map/ppermute | solution.py:390
  150.9 27.8 %collective-permute-start.15 = (bf16[512,256]{1,0:T(8,128)(2,1)S(1)}, bf16[512,256]{1,0:T(8,128)(2,1)}, u32[]{:S(2)}, u32[]{:S(2)}) collective-permute-start(bf16[512,256]{1,0:T(8,128)(2,1)S(1)} %copy-done.3), channel_id=1, source_target_pairs={{0,1},{1,2},{2,3},{3,0},{4,5},{5,6},{6,7},{7,4},{8,9},{9,10},{10,1... | collective-permute-start | bytes 786440 | tf_op jit(solution)/shard_map/ppermute | solution.py:43
  150.9 27.9 %collective-permute-start.17 = (bf16[512,256]{1,0:T(8,128)(2,1)S(1)}, bf16[512,256]{1,0:T(8,128)(2,1)}, u32[]{:S(2)}, u32[]{:S(2)}) collective-permute-start(bf16[512,256]{1,0:T(8,128)(2,1)S(1)} %copy-done.3), channel_id=1, source_target_pairs={{0,3},{1,0},{2,1},{3,2},{4,7},{5,4},{6,5},{7,6},{8,11},{9,8},{10,9... | collective-permute-start | bytes 786440 | tf_op jit(solution)/shard_map/ppermute | solution.py:43
  156.6 30.1 %collective-permute-start.19 = (f32[64,256]{1,0:T(8,128)}, f32[64,256]{1,0:T(8,128)}, u32[]{:S(2)}, u32[]{:S(2)}) collective-permute-start(f32[64,256]{1,0:T(8,128)} %get-tuple-element.36), channel_id=1, source_target_pairs={{0,64},{32,96},{64,128},{96,160},{128,192},{160,224},{192,0},{224,... | collective-permute-start | bytes 196616 | tf_op jit(solution)/shard_map/ppermute | solution.py:418
  159.8 28.3 %collective-permute-start.21 = (f32[64,256]{1,0:T(8,128)}, f32[64,256]{1,0:T(8,128)}, u32[]{:S(2)}, u32[]{:S(2)}) collective-permute-start(f32[64,256]{1,0:T(8,128)} %get-tuple-element.37), channel_id=1, source_target_pairs={{0,192},{32,224},{64,0},{96,32},{128,64},{160,96},{192,128},{224,1... | collective-permute-start | bytes 196616 | tf_op jit(solution)/shard_map/ppermute | solution.py:418
  163.0 25.1 %collective-permute-start.20 = (f32[64,256]{1,0:T(8,128)}, f32[64,256]{1,0:T(8,128)}, u32[]{:S(2)}, u32[]{:S(2)}) collective-permute-start(f32[64,256]{1,0:T(8,128)} %get-tuple-element.38), channel_id=1, source_target_pairs={{0,128},{32,160},{64,192},{96,224},{128,0},{160,32},{192,64},{224,... | collective-permute-start | bytes 196616 | tf_op jit(solution)/shard_map/ppermute | solution.py:418
  178.7 15.2 %collective-permute-start.6 = (f32[512,256]{1,0:T(8,128)}, f32[512,256]{1,0:T(8,128)}, u32[]{:S(2)}, u32[]{:S(2)}) collective-permute-start(f32[512,256]{1,0:T(8,128)} %get-tuple-element.19), channel_id=1, source_target_pairs={{0,3},{1,0},{2,1},{3,2},{4,7},{5,4},{6,5},{7,6},{8,11},{9,8},{10,9... | collective-permute-start | bytes 1572872 | tf_op jit(solution)/shard_map/ppermute | solution.py:43
  178.8 15.9 %collective-permute-start.7 = (f32[512,256]{1,0:T(8,128)}, f32[512,256]{1,0:T(8,128)}, u32[]{:S(2)}, u32[]{:S(2)}) collective-permute-start(f32[512,256]{1,0:T(8,128)} %get-tuple-element.20), channel_id=1, source_target_pairs={{0,2},{1,3},{2,0},{3,1},{4,6},{5,7},{6,4},{7,5},{8,10},{9,11},{10,... | collective-permute-start | bytes 1572872 | tf_op jit(solution)/shard_map/ppermute | solution.py:43
  186.7 16.7 %collective-permute-start.8 = (f32[512,256]{1,0:T(8,128)}, f32[512,256]{1,0:T(8,128)S(1)}, u32[]{:S(2)}, u32[]{:S(2)}) collective-permute-start(f32[512,256]{1,0:T(8,128)} %get-tuple-element.21), channel_id=1, source_target_pairs={{0,1},{1,2},{2,3},{3,0},{4,5},{5,6},{6,7},{7,4},{8,9},{9,10},{10,1... | collective-permute-start | bytes 1572872 | tf_op jit(solution)/shard_map/ppermute | solution.py:43
  (16 other events, 69.8 us)
Sparse Core Ops, SparseCore 0:
  10.3 44.1 all-gather.1
  74.6 56.5 reduce-scatter.1

commit v5 on v4

--- a/solution.py
+++ b/solution.py
@@ -330,6 +330,17 @@
         pieces,
         [jax.ShapeDtypeStruct((rows, keyw), f32)] * NT,
         [whole((rows, keyw))] * NT,
+    )
+
+
+def layer_kernel(route, ret, a, b, c, d, out):
+    total = a[...] + b[...] + c[...] + d[...]
+    out[...] = (total + dot(route[...], ret[...], ((0,), (0,)))).astype(bf16)
+
+
+def run_layer(route, ret, parts):
+    return call(layer_kernel, jax.ShapeDtypeStruct(parts[0].shape, bf16), [VM] * 6)(
+        route, ret, *parts
     )
 
 
@@ -393,8 +404,7 @@
     pieces = halves + other
     base_grad = run_base_grad(at, frozen_key_weight, cots, pieces)
     base_out, *outs = run_base_out(at, frozen_key_weight, tokens, pieces)
-    for k in range(1, NT):
-        base_out = base_out + shift(outs[k - 1], -k)
+    base_parts = [base_out] + [shift(outs[k - 1], -k) for k in range(1, NT)]
 
     def parts_of(own):
         return [own] + [shift(own, k) for k in range(1, NT)]
@@ -419,7 +429,7 @@
             give, "z", [(i, (i // 2 + k) % nq * 2 + i % 2) for i in range(NZ)]
         )
 
-    layer_out = (base_out + dot(route, ret_out, ((0,), (0,)))).astype(bf16)
+    layer_out = run_layer(route, ret_out, base_parts)
     input_grad = run_final(route, ret_grad, base_grad)
     fresh_down = optimizer_update(
         adapter_down_matrix[0], down_first_moment[0], down_second_moment[0], grad_down

time: 223 us -> 225 us (level)
  Pallas kernels: 46.8 us -> 50 us
  other arithmetic: 10.1 us -> 6.93 us
    pallas_call x0 -> x1, Pallas kernels: none -> 2.99 us  [run_layer(): call(layer_kernel, jax.ShapeDtypeStruct(parts[0].shape, bf16), [VM] * 6)]
    dot_general x2 -> x1, matrix products: 6.81 us -> 5.27 us  [dot(): return lax.dot_general(a, b, (dims, ((), ())), preferred_element_type=out)]
    unnamed x24 -> x28, local copies, waits for them, and re-layouts: 4.61 us -> 4.64 us
  transfers between devices with their start and end apart: 28 -> 28, of which waited for: 15 -> 15; matrix products, arithmetic and copies ran while one was open for 8% -> 6% of each run, Pallas kernels for 18% -> 19%
where the time goes in v5:
time: 225 us; the launch traced here: 223 us
  waiting for transfers between devices  83.5 us (37%)
  starting transfers between devices  53.8 us (24%)
  Pallas kernels  50 us (22%)
  between operations  14.1 us (6%)
  local copies, waits for them, and re-layouts  9.57 us (4%)
  other arithmetic  6.93 us (3%)
  matrix products  5.27 us (2%)
    ppermute x15, waiting for transfers between devices, shift(): return lax.ppermute(v, 't', [(i, (i + k) % NT) for i in range(NT)])  48.1 us
    all_gather x1, waiting for transfers between devices, step(): all16 = lax.all_gather(both16, 'z', axis=0, tiled=True)  24.1 us
    ppermute x15, starting transfers between devices, shift(): return lax.ppermute(v, 't', [(i, (i + k) % NT) for i in range(NT)])  20 us
    pallas_call x2, Pallas kernels, run_base(): pl.pallas_call(kernel, out_shape=outs, grid_spec=pltpu.PrefetchScalarGrid...  17.4 us
    ppermute x3, starting transfers between devices, step(): lax.ppermute(give, 'z', [(i, (i // 2 + k) % nq * 2 + i % 2) for i in rang...  11.3 us
    all_to_all x1, waiting for transfers between devices, step(): x_rows = lax.all_to_all(x_send, ('x', 'c'), 0, 0, tiled=True)  6.22 us
    all_to_all x1, starting transfers between devices, step(): g_rows = lax.all_to_all(g_send, ('x', 'c'), 0, 0, tiled=True)  5.6 us
    pallas_call x1, Pallas kernels, run_final(): call(final_kernel, jax.ShapeDtypeStruct((rows, feat), bf16), [whole(route...  5.39 us
  transfers between devices with their start and end apart: 28, of which 15 were waited for; matrix products, arithmetic and copies ran while one was open for 6% of the time, Pallas kernels for 19%

profile of v5, /device:TPU:2, one launch (start us, length us, event | category | flops | bytes accessed | tf_op | source)
XLA Modules:
  0.0 223.1 jit_solution(6034164230589994938)
XLA Ops:
  11.6 5.6 %all-to-all-start.1 = ((bf16[8,96,256]{2,1,0:T(8,128)(2,1)}), bf16[8,96,256]{2,1,0:T(8,128)(2,1)S(1)}, u32[]{:S(2)}, u32[]{:S(2)}) async-start(bf16[8,96,256]{2,1,0:T(8,128)(2,1)} %bitcast.86), calls=%async_computation.1 | async-start | bytes 786432 | tf_op jit(solution)/shard_map/all_to_all | solution.py:392
  17.2 5.3 %fusion.10 = bf16[768,2048]{1,0:T(8,128)(2,1)} fusion(bf16[768,512]{1,0:T(8,128)(2,1)} %get-tuple-element.18.route, bf16[512,2048]{1,0:T(8,128)(2,1)} %tokens.1), kind=kOutput, calls=%fused_computation.25 | convolution fusion | flops 1610612736 | bytes 6029312 | tf_op jit(solution)/shard_map/dot_general | solution.py:47
  25.4 5.0 %all-to-all-start = ((bf16[8,96,2048]{2,1,0:T(8,128)(2,1)}), bf16[8,96,2048]{2,1,0:T(8,128)(2,1)S(1)}, u32[]{:S(2)}, u32[]{:S(2)}) async-start(bf16[8,96,2048]{2,1,0:T(8,128)(2,1)} %bitcast.81), calls=%async_computation | async-start | bytes 6291456 | tf_op jit(solution)/shard_map/all_to_all | solution.py:391
  30.4 24.1 %all-gather.2.cloned.1.call-done.down.up = bf16[512,2304]{1,0:T(8,128)(2,1)} async-done(((bf16[64,2304]{1,0:T(8,128)(2,1)}), bf16[512,2304]{1,0:T(8,128)(2,1)}) %all-gather.2.cloned.1.call-update) | async-done | bytes 2359312 | tf_op jit(solution)/shard_map/all_gather | solution.py:383
  61.2 6.2 %all-to-all-done = bf16[8,96,2048]{2,1,0:T(8,128)(2,1)S(1)} async-done(((bf16[8,96,2048]{2,1,0:T(8,128)(2,1)}), bf16[8,96,2048]{2,1,0:T(8,128)(2,1)S(1)}, u32[]{:S(2)}, u32[]{:S(2)}) %all-to-all-start) | async-done | bytes 3145760 | tf_op jit(solution)/shard_map/all_to_all | solution.py:391
  69.2 5.3 %shard_map.177 = (bf16[768,512]{1,0:T(8,128)(2,1)}, f32[512,2048]{1,0:T(8,128)}) custom-call(f32[384,128]{1,0:T(8,128)} %shard_map.176.a, f32[384,128]{1,0:T(8,128)} %collective-permute-done.12.b, f32[384,128]{1,0:T(8,128)} %copy-done.12, f32[384,128]{1,0:T(8,128)} %copy-done.11, bf16[768,2048]{1,0:T(8,128)(2,1)} %bitcast.75), custom_call_target="tpu_custom_call" | custom-call | tf_op jit(solution)/shard_map/pallas_call | solution.py:237
  74.5 4.7 %shard_map.172.a = f32[384,128]{1,0:T(8,128)} custom-call(bf16[768,2048]{1,0:T(8,128)(2,1)} %bitcast.76, bf16[512,2304]{1,0:T(8,128)(2,1)} %all-gather.2.cloned.1.call-done.down.up), custom_call_target="tpu_custom_call" | custom-call | tf_op jit(solution)/shard_map/pallas_call | solution.py:261
  83.0 6.8 %collective-permute-done.2.d = f32[384,128]{1,0:T(8,128)S(1)} collective-permute-done((f32[384,128]{1,0:T(8,128)}, f32[384,128]{1,0:T(8,128)S(1)}, u32[]{:S(2)}, u32[]{:S(2)}) %collective-permute-start.2) | collective-permute-done | bytes 196640 | tf_op jit(solution)/shard_map/ppermute | solution.py:43
  97.1 4.8 %all-to-all-start.2 = ((bf16[8,96,256]{2,1,0:T(8,128)(2,1)}), bf16[8,96,256]{2,1,0:T(8,128)(2,1)S(1)}, u32[]{:S(2)}, u32[]{:S(2)}) async-start(bf16[8,96,256]{2,1,0:T(8,128)(2,1)} %bitcast.85), calls=%async_computation.2 | async-start | bytes 786432 | tf_op jit(solution)/shard_map/all_to_all | solution.py:419
  101.9 4.7 %shard_map.178 = bf16[768,2048]{1,0:T(8,128)(2,1)} custom-call(bf16[768,512]{1,0:T(8,128)(2,1)} %get-tuple-element.25.back16, bf16[512,2304]{1,0:T(8,128)(2,1)} %all-gather.2.cloned.1.call-done.down.up), custom_call_target="tpu_custom_call" | custom-call | tf_op jit(solution)/shard_map/pallas_call | solution.py:249
  110.1 5.0 %all-to-all-start.3 = ((bf16[8,96,2048]{2,1,0:T(8,128)(2,1)}), bf16[8,96,2048]{2,1,0:T(8,128)(2,1)S(1)}, u32[]{:S(2)}, u32[]{:S(2)}) async-start(bf16[8,96,2048]{2,1,0:T(8,128)(2,1)} %bitcast.77), calls=%async_computation.3 | async-start | bytes 6291456 | tf_op jit(solution)/shard_map/all_to_all | solution.py:415
  119.8 4.1 %collective-permute-start.16 = (bf16[512,256]{1,0:T(8,128)(2,1)S(1)}, bf16[512,256]{1,0:T(8,128)(2,1)}, u32[]{:S(2)}, u32[]{:S(2)}) collective-permute-start(bf16[512,256]{1,0:T(8,128)(2,1)S(1)} %copy-done.4), channel_id=1, source_target_pairs={{0,2},{1,3},{2,0},{3,1},{4,6},{5,7},{6,4},{7,5},{8,10},{9,11},{10,... | collective-permute-start | bytes 786440 | tf_op jit(solution)/shard_map/ppermute | solution.py:43
  127.5 5.3 %collective-permute-done.5.refs_2_.refs_6_ = bf16[1024,256]{1,0:T(8,128)(2,1)} collective-permute-done((bf16[1024,256]{1,0:T(8,128)(2,1)}, bf16[1024,256]{1,0:T(8,128)(2,1)}, u32[]{:S(2)}, u32[]{:S(2)}) %collective-permute-start.5) | collective-permute-done | bytes 524320 | tf_op jit(solution)/shard_map/ppermute | solution.py:43
  135.1 11.1 %collective-permute-done.3.refs_0_.refs_4_ = bf16[1024,256]{1,0:T(8,128)(2,1)} collective-permute-done((bf16[1024,256]{1,0:T(8,128)(2,1)}, bf16[1024,256]{1,0:T(8,128)(2,1)}, u32[]{:S(2)}, u32[]{:S(2)}) %collective-permute-start.3) | collective-permute-done | bytes 524320 | tf_op jit(solution)/shard_map/ppermute | solution.py:43
  146.3 4.6 %collective-permute-done.16.refs_2_ = bf16[512,256]{1,0:T(8,128)(2,1)} collective-permute-done((bf16[512,256]{1,0:T(8,128)(2,1)S(1)}, bf16[512,256]{1,0:T(8,128)(2,1)}, u32[]{:S(2)}, u32[]{:S(2)}) %collective-permute-start.16) | collective-permute-done | bytes 262176 | tf_op jit(solution)/shard_map/ppermute | solution.py:43
  150.9 3.2 %collective-permute-start.17 = (bf16[512,256]{1,0:T(8,128)(2,1)S(1)}, bf16[512,256]{1,0:T(8,128)(2,1)}, u32[]{:S(2)}, u32[]{:S(2)}) collective-permute-start(bf16[512,256]{1,0:T(8,128)(2,1)S(1)} %copy-done.4), channel_id=1, source_target_pairs={{0,3},{1,0},{2,1},{3,2},{4,7},{5,4},{6,5},{7,6},{8,11},{9,8},{10,9... | collective-permute-start | bytes 786440 | tf_op jit(solution)/shard_map/ppermute | solution.py:43
  156.6 3.2 %collective-permute-start.19 = (f32[64,256]{1,0:T(8,128)}, f32[64,256]{1,0:T(8,128)S(1)}, u32[]{:S(2)}, u32[]{:S(2)}) collective-permute-start(f32[64,256]{1,0:T(8,128)} %get-tuple-element.36), channel_id=1, source_target_pairs={{0,64},{32,96},{64,128},{96,160},{128,192},{160,224},{192,0},{224,... | collective-permute-start | bytes 196616 | tf_op jit(solution)/shard_map/ppermute | solution.py:428
  159.8 3.1 %collective-permute-start.21 = (f32[64,256]{1,0:T(8,128)}, f32[64,256]{1,0:T(8,128)}, u32[]{:S(2)}, u32[]{:S(2)}) collective-permute-start(f32[64,256]{1,0:T(8,128)} %get-tuple-element.37), channel_id=1, source_target_pairs={{0,192},{32,224},{64,0},{96,32},{128,64},{160,96},{192,128},{224,1... | collective-permute-start | bytes 196616 | tf_op jit(solution)/shard_map/ppermute | solution.py:428
  162.9 4.9 %collective-permute-start.20 = (f32[64,256]{1,0:T(8,128)S(1)}, f32[64,256]{1,0:T(8,128)}, u32[]{:S(2)}, u32[]{:S(2)}) collective-permute-start(f32[64,256]{1,0:T(8,128)S(1)} %get-tuple-element.38), channel_id=1, source_target_pairs={{0,128},{32,160},{64,192},{96,224},{128,0},{160,32},{192,64},{224,... | collective-permute-start | bytes 196616 | tf_op jit(solution)/shard_map/ppermute | solution.py:428
  168.5 10.2 %shard_map.174 = (f32[512,256]{1,0:T(8,128)}, f32[512,256]{1,0:T(8,128)}, f32[512,256]{1,0:T(8,128)}, f32[512,256]{1,0:T(8,128)}) custom-call(s32[2]{0:T(128)} %pad_add_fusion.at, bf16[512,2048]{1,0:T(8,128)(2,1)} %tokens.1, bf16[8192,256]{1,0:T(8,128)(2,1)} %own.3, bf16[1024,256]{1,0:T(8,128)(2,1)} %collective-permute-done.3.refs_0_.refs_4_, ...), custom_call_target="tpu_custom_call" | custom-call | tf_op jit(solution)/shard_map/pallas_call | solution.py:293
  181.1 7.2 %shard_map.179.base = f32[512,2048]{1,0:T(8,128)} custom-call(s32[2]{0:T(128)} %pad_add_fusion.at, bf16[8192,256]{1,0:T(8,128)(2,1)} %own.3, bf16[512,256]{1,0:T(8,128)(2,1)} %refs_0_.1, bf16[512,256]{1,0:T(8,128)(2,1)} %collective-permute-done.15.refs_1_, bf16[512,256]{1,0:T(8,128)(2,1)} %collective-permute-done.16.refs_2_, ...), custom_call_target="tpu_custom_call" | custom-call | tf_op jit(solution)/shard_map/pallas_call | solution.py:293
  190.6 3.3 %collective-permute-done.9.b = f32[512,256]{1,0:T(8,128)} collective-permute-done((f32[512,256]{1,0:T(8,128)}, f32[512,256]{1,0:T(8,128)}, u32[]{:S(2)}, u32[]{:S(2)}) %collective-permute-start.9) | collective-permute-done | bytes 524320 | tf_op jit(solution)/shard_map/ppermute | solution.py:43
  195.5 7.8 %collective-permute-done.11.d = f32[512,256]{1,0:T(8,128)} collective-permute-done((f32[512,256]{1,0:T(8,128)}, f32[512,256]{1,0:T(8,128)}, u32[]{:S(2)}, u32[]{:S(2)}) %collective-permute-start.11) | collective-permute-done | bytes 524320 | tf_op jit(solution)/shard_map/ppermute | solution.py:43
  207.9 5.4 %shard_map.180 = bf16[512,2048]{1,0:T(8,128)(2,1)} custom-call(bf16[768,512]{1,0:T(8,128)(2,1)} %get-tuple-element.18.route, bf16[768,2048]{1,0:T(8,128)(2,1)} %bitcast.78, f32[512,2048]{1,0:T(8,128)} %shard_map.179.base), custom_call_target="tpu_custom_call" | custom-call | tf_op jit(solution)/shard_map/pallas_call | solution.py:350
  (82 shorter events, 57.9 us)
Async XLA Ops:
  7.2 47.3 %all-gather.2.cloned.1.call-start = ((), (), s32[]{:S(2)}) async-start(), calls=%async_computation.5 | async-start | bytes 2654208 | tf_op jit(solution)/shard_map/all_gather | solution.py:383
  11.6 13.1 %all-to-all-start.1 = ((bf16[8,96,256]{2,1,0:T(8,128)(2,1)}), bf16[8,96,256]{2,1,0:T(8,128)(2,1)S(1)}, u32[]{:S(2)}, u32[]{:S(2)}) async-start(bf16[8,96,256]{2,1,0:T(8,128)(2,1)} %bitcast.86), calls=%async_computation.1 | async-start | bytes 786432 | tf_op jit(solution)/shard_map/all_to_all | solution.py:392
  25.4 42.0 %all-to-all-start = ((bf16[8,96,2048]{2,1,0:T(8,128)(2,1)}), bf16[8,96,2048]{2,1,0:T(8,128)(2,1)S(1)}, u32[]{:S(2)}, u32[]{:S(2)}) async-start(bf16[8,96,2048]{2,1,0:T(8,128)(2,1)} %bitcast.81), calls=%async_computation | async-start | bytes 6291456 | tf_op jit(solution)/shard_map/all_to_all | solution.py:391
  30.4 182.9 %reduce-scatter.2.cloned.1.call-start = ((), (), s32[]{:S(2)}) async-start(), calls=%async_computation.6 | async-start | bytes 4718592 | tf_op jit(solution)/shard_map/reduce_scatter | solution.py:413
  56.7 10.7 %collective-permute-start.14 = (f32[384,128]{1,0:T(8,128)}, f32[384,128]{1,0:T(8,128)S(1)}, u32[]{:S(2)}, u32[]{:S(2)}) collective-permute-start(f32[384,128]{1,0:T(8,128)} %shard_map.176.a), channel_id=1, source_target_pairs={{0,3},{1,0},{2,1},{3,2},{4,7},{5,4},{6,5},{7,6},{8,11},{9,8},{10,9... | collective-permute-start | bytes 589832 | tf_op jit(solution)/shard_map/ppermute | solution.py:43
  82.1 11.4 %collective-permute-start = (f32[384,128]{1,0:T(8,128)}, f32[384,128]{1,0:T(8,128)S(1)}, u32[]{:S(2)}, u32[]{:S(2)}) collective-permute-start(f32[384,128]{1,0:T(8,128)} %shard_map.172.a), channel_id=1, source_target_pairs={{0,1},{1,2},{2,3},{3,0},{4,5},{5,6},{6,7},{7,4},{8,9},{9,10},{10,1... | collective-permute-start | bytes 589832 | tf_op jit(solution)/shard_map/ppermute | solution.py:43
  97.1 12.3 %all-to-all-start.2 = ((bf16[8,96,256]{2,1,0:T(8,128)(2,1)}), bf16[8,96,256]{2,1,0:T(8,128)(2,1)S(1)}, u32[]{:S(2)}, u32[]{:S(2)}) async-start(bf16[8,96,256]{2,1,0:T(8,128)(2,1)} %bitcast.85), calls=%async_computation.2 | async-start | bytes 786432 | tf_op jit(solution)/shard_map/all_to_all | solution.py:419
  110.1 96.2 %all-to-all-start.3 = ((bf16[8,96,2048]{2,1,0:T(8,128)(2,1)}), bf16[8,96,2048]{2,1,0:T(8,128)(2,1)S(1)}, u32[]{:S(2)}, u32[]{:S(2)}) async-start(bf16[8,96,2048]{2,1,0:T(8,128)(2,1)} %bitcast.77), calls=%async_computation.3 | async-start | bytes 6291456 | tf_op jit(solution)/shard_map/all_to_all | solution.py:415
  117.7 15.1 %collective-permute-start.5 = (bf16[1024,256]{1,0:T(8,128)(2,1)}, bf16[1024,256]{1,0:T(8,128)(2,1)}, u32[]{:S(2)}, u32[]{:S(2)}) collective-permute-start(bf16[1024,256]{1,0:T(8,128)(2,1)} %get-tuple-element.30), channel_id=1, source_target_pairs={{0,3},{1,0},{2,1},{3,2},{4,7},{5,4},{6,5},{7,6},{8,11},{9,8},{10,9... | collective-permute-start | bytes 1572872 | tf_op jit(solution)/shard_map/ppermute | solution.py:43
  118.5 16.7 %collective-permute-start.4 = (bf16[1024,256]{1,0:T(8,128)(2,1)}, bf16[1024,256]{1,0:T(8,128)(2,1)}, u32[]{:S(2)}, u32[]{:S(2)}) collective-permute-start(bf16[1024,256]{1,0:T(8,128)(2,1)} %get-tuple-element.31), channel_id=1, source_target_pairs={{0,2},{1,3},{2,0},{3,1},{4,6},{5,7},{6,4},{7,5},{8,10},{9,11},{10,... | collective-permute-start | bytes 1572872 | tf_op jit(solution)/shard_map/ppermute | solution.py:43
  118.9 27.3 %collective-permute-start.3 = (bf16[1024,256]{1,0:T(8,128)(2,1)}, bf16[1024,256]{1,0:T(8,128)(2,1)}, u32[]{:S(2)}, u32[]{:S(2)}) collective-permute-start(bf16[1024,256]{1,0:T(8,128)(2,1)} %get-tuple-element.32), channel_id=1, source_target_pairs={{0,1},{1,2},{2,3},{3,0},{4,5},{5,6},{6,7},{7,4},{8,9},{9,10},{10,1... | collective-permute-start | bytes 1572872 | tf_op jit(solution)/shard_map/ppermute | solution.py:43
  119.8 31.1 %collective-permute-start.16 = (bf16[512,256]{1,0:T(8,128)(2,1)S(1)}, bf16[512,256]{1,0:T(8,128)(2,1)}, u32[]{:S(2)}, u32[]{:S(2)}) collective-permute-start(bf16[512,256]{1,0:T(8,128)(2,1)S(1)} %copy-done.4), channel_id=1, source_target_pairs={{0,2},{1,3},{2,0},{3,1},{4,6},{5,7},{6,4},{7,5},{8,10},{9,11},{10,... | collective-permute-start | bytes 786440 | tf_op jit(solution)/shard_map/ppermute | solution.py:43
  125.6 25.3 %collective-permute-start.18 = (f32[4,64,256]{2,1,0:T(8,128)}, f32[4,64,256]{2,1,0:T(8,128)}, u32[]{:S(2)}, u32[]{:S(2)}) collective-permute-start(f32[4,64,256]{2,1,0:T(8,128)} %dynamic-slice_bitcast_fusion), channel_id=1, source_target_pairs={{0,32},{32,0},{64,96},{96,64},{128,160},{160,128},{192,224},{224,1... | collective-permute-start | bytes 786440 | tf_op jit(solution)/shard_map/ppermute | solution.py:423
  132.8 23.7 %collective-permute-start.8 = (bf16[1024,256]{1,0:T(8,128)(2,1)}, bf16[1024,256]{1,0:T(8,128)(2,1)}, u32[]{:S(2)}, u32[]{:S(2)}) collective-permute-start(bf16[1024,256]{1,0:T(8,128)(2,1)} %collective-permute-done.5.refs_2_.refs_6_), channel_id=1, source_target_pairs={{0,4},{4,0},{1,5},{5,1},{2,6},{6,2},{3,7},{7,3},{8,12},{12,8},{9,1... | collective-permute-start | bytes 1572872 | tf_op jit(solution)/shard_map/ppermute | solution.py:401
  135.1 24.7 %collective-permute-start.7 = (bf16[1024,256]{1,0:T(8,128)(2,1)}, bf16[1024,256]{1,0:T(8,128)(2,1)}, u32[]{:S(2)}, u32[]{:S(2)}) collective-permute-start(bf16[1024,256]{1,0:T(8,128)(2,1)} %collective-permute-done.4.refs_1_.refs_5_), channel_id=1, source_target_pairs={{0,4},{4,0},{1,5},{5,1},{2,6},{6,2},{3,7},{7,3},{8,12},{12,8},{9,1... | collective-permute-start | bytes 1572872 | tf_op jit(solution)/shard_map/ppermute | solution.py:401
  146.3 16.7 %collective-permute-start.6 = (bf16[1024,256]{1,0:T(8,128)(2,1)}, bf16[1024,256]{1,0:T(8,128)(2,1)}, u32[]{:S(2)}, u32[]{:S(2)}) collective-permute-start(bf16[1024,256]{1,0:T(8,128)(2,1)} %collective-permute-done.3.refs_0_.refs_4_), channel_id=1, source_target_pairs={{0,4},{4,0},{1,5},{5,1},{2,6},{6,2},{3,7},{7,3},{8,12},{12,8},{9,1... | collective-permute-start | bytes 1572872 | tf_op jit(solution)/shard_map/ppermute | solution.py:401
  150.9 27.8 %collective-permute-start.15 = (bf16[512,256]{1,0:T(8,128)(2,1)S(1)}, bf16[512,256]{1,0:T(8,128)(2,1)}, u32[]{:S(2)}, u32[]{:S(2)}) collective-permute-start(bf16[512,256]{1,0:T(8,128)(2,1)S(1)} %copy-done.4), channel_id=1, source_target_pairs={{0,1},{1,2},{2,3},{3,0},{4,5},{5,6},{6,7},{7,4},{8,9},{9,10},{10,1... | collective-permute-start | bytes 786440 | tf_op jit(solution)/shard_map/ppermute | solution.py:43
  150.9 27.9 %collective-permute-start.17 = (bf16[512,256]{1,0:T(8,128)(2,1)S(1)}, bf16[512,256]{1,0:T(8,128)(2,1)}, u32[]{:S(2)}, u32[]{:S(2)}) collective-permute-start(bf16[512,256]{1,0:T(8,128)(2,1)S(1)} %copy-done.4), channel_id=1, source_target_pairs={{0,3},{1,0},{2,1},{3,2},{4,7},{5,4},{6,5},{7,6},{8,11},{9,8},{10,9... | collective-permute-start | bytes 786440 | tf_op jit(solution)/shard_map/ppermute | solution.py:43
  156.6 23.1 %collective-permute-start.19 = (f32[64,256]{1,0:T(8,128)}, f32[64,256]{1,0:T(8,128)S(1)}, u32[]{:S(2)}, u32[]{:S(2)}) collective-permute-start(f32[64,256]{1,0:T(8,128)} %get-tuple-element.36), channel_id=1, source_target_pairs={{0,64},{32,96},{64,128},{96,160},{128,192},{160,224},{192,0},{224,... | collective-permute-start | bytes 196616 | tf_op jit(solution)/shard_map/ppermute | solution.py:428
  159.8 28.5 %collective-permute-start.21 = (f32[64,256]{1,0:T(8,128)}, f32[64,256]{1,0:T(8,128)}, u32[]{:S(2)}, u32[]{:S(2)}) collective-permute-start(f32[64,256]{1,0:T(8,128)} %get-tuple-element.37), channel_id=1, source_target_pairs={{0,192},{32,224},{64,0},{96,32},{128,64},{160,96},{192,128},{224,1... | collective-permute-start | bytes 196616 | tf_op jit(solution)/shard_map/ppermute | solution.py:428
  162.9 25.4 %collective-permute-start.20 = (f32[64,256]{1,0:T(8,128)S(1)}, f32[64,256]{1,0:T(8,128)}, u32[]{:S(2)}, u32[]{:S(2)}) collective-permute-start(f32[64,256]{1,0:T(8,128)S(1)} %get-tuple-element.38), channel_id=1, source_target_pairs={{0,128},{32,160},{64,192},{96,224},{128,0},{160,32},{192,64},{224,... | collective-permute-start | bytes 196616 | tf_op jit(solution)/shard_map/ppermute | solution.py:428
  178.7 15.2 %collective-permute-start.9 = (f32[512,256]{1,0:T(8,128)}, f32[512,256]{1,0:T(8,128)}, u32[]{:S(2)}, u32[]{:S(2)}) collective-permute-start(f32[512,256]{1,0:T(8,128)} %get-tuple-element.22), channel_id=1, source_target_pairs={{0,3},{1,0},{2,1},{3,2},{4,7},{5,4},{6,5},{7,6},{8,11},{9,8},{10,9... | collective-permute-start | bytes 1572872 | tf_op jit(solution)/shard_map/ppermute | solution.py:43
  178.8 16.7 %collective-permute-start.10 = (f32[512,256]{1,0:T(8,128)}, f32[512,256]{1,0:T(8,128)}, u32[]{:S(2)}, u32[]{:S(2)}) collective-permute-start(f32[512,256]{1,0:T(8,128)} %get-tuple-element.23), channel_id=1, source_target_pairs={{0,2},{1,3},{2,0},{3,1},{4,6},{5,7},{6,4},{7,5},{8,10},{9,11},{10,... | collective-permute-start | bytes 1572872 | tf_op jit(solution)/shard_map/ppermute | solution.py:43
  179.6 23.7 %collective-permute-start.11 = (f32[512,256]{1,0:T(8,128)}, f32[512,256]{1,0:T(8,128)}, u32[]{:S(2)}, u32[]{:S(2)}) collective-permute-start(f32[512,256]{1,0:T(8,128)} %get-tuple-element.24), channel_id=1, source_target_pairs={{0,1},{1,2},{2,3},{3,0},{4,5},{5,6},{6,7},{7,4},{8,9},{9,10},{10,1... | collective-permute-start | bytes 1572872 | tf_op jit(solution)/shard_map/ppermute | solution.py:43
  (18 other events, 82.2 us)
Sparse Core Ops, SparseCore 0:
  10.3 44.1 all-gather.1
  74.6 56.5 reduce-scatter.1

commit v6 on v5

--- a/solution.py
+++ b/solution.py
@@ -174,8 +174,11 @@
     step = pl.program_id(0)
 
     def half(pieces):
-        for p, w in zip(parts, (own,) + pieces):
-            v = dot(tokens[...], w[...])
+        keyw = own.shape[1]
+        w = jnp.concatenate([v[...] for v in (own,) + pieces], axis=1)
+        total = dot(tokens[...], w)
+        for k, p in enumerate(parts):
+            v = total[:, k * keyw : (k + 1) * keyw]
 
             @pl.when(step == 0)
             def _():

time: 225 us -> 222 us (0.987)
  Pallas kernels: 50 us -> 47 us
    pallas_call x2, Pallas kernels: 17.4 us -> 14.5 us  [run_base(): pl.pallas_call(kernel, out_shape=outs, grid_spec=pltpu.PrefetchScalarGrid...]
  transfers between devices with their start and end apart: 28 -> 28, of which waited for: 15 -> 15; matrix products, arithmetic and copies ran while one was open for 6% -> 6% of each run, Pallas kernels for 19% -> 18%
where the time goes in v6:
time: 222 us; the launch traced here: 220 us
  waiting for transfers between devices  83.5 us (38%)
  starting transfers between devices  53.8 us (24%)
  Pallas kernels  47 us (21%)
  between operations  14.1 us (6%)
  local copies, waits for them, and re-layouts  9.57 us (4%)
  other arithmetic  6.93 us (3%)
  matrix products  5.27 us (2%)
    ppermute x15, waiting for transfers between devices, shift(): return lax.ppermute(v, 't', [(i, (i + k) % NT) for i in range(NT)])  48.1 us
    all_gather x1, waiting for transfers between devices, step(): all16 = lax.all_gather(both16, 'z', axis=0, tiled=True)  24.1 us
    ppermute x15, starting transfers between devices, shift(): return lax.ppermute(v, 't', [(i, (i + k) % NT) for i in range(NT)])  20 us
    pallas_call x2, Pallas kernels, run_base(): pl.pallas_call(kernel, out_shape=outs, grid_spec=pltpu.PrefetchScalarGrid...  14.5 us
    ppermute x3, starting transfers between devices, step(): lax.ppermute(give, 'z', [(i, (i // 2 + k) % nq * 2 + i % 2) for i in rang...  11.3 us
    all_to_all x1, waiting for transfers between devices, step(): x_rows = lax.all_to_all(x_send, ('x', 'c'), 0, 0, tiled=True)  6.22 us
    all_to_all x1, starting transfers between devices, step(): g_rows = lax.all_to_all(g_send, ('x', 'c'), 0, 0, tiled=True)  5.6 us
    pallas_call x1, Pallas kernels, run_final(): call(final_kernel, jax.ShapeDtypeStruct((rows, feat), bf16), [whole(route...  5.39 us
  transfers between devices with their start and end apart: 28, of which 15 were waited for; matrix products, arithmetic and copies ran while one was open for 6% of the time, Pallas kernels for 18%

profile of v6, /device:TPU:2, one launch (start us, length us, event | category | flops | bytes accessed | tf_op | source)
XLA Modules:
  0.0 220.2 jit_solution(12916877878196801008)
XLA Ops:
  11.6 5.6 %all-to-all-start.1 = ((bf16[8,96,256]{2,1,0:T(8,128)(2,1)}), bf16[8,96,256]{2,1,0:T(8,128)(2,1)S(1)}, u32[]{:S(2)}, u32[]{:S(2)}) async-start(bf16[8,96,256]{2,1,0:T(8,128)(2,1)} %bitcast.86), calls=%async_computation.1 | async-start | bytes 786432 | tf_op jit(solution)/shard_map/all_to_all | solution.py:395
  17.2 5.3 %fusion.10 = bf16[768,2048]{1,0:T(8,128)(2,1)} fusion(bf16[768,512]{1,0:T(8,128)(2,1)} %get-tuple-element.18.route, bf16[512,2048]{1,0:T(8,128)(2,1)} %tokens.1), kind=kOutput, calls=%fused_computation.25 | convolution fusion | flops 1610612736 | bytes 6029312 | tf_op jit(solution)/shard_map/dot_general | solution.py:47
  25.4 5.0 %all-to-all-start = ((bf16[8,96,2048]{2,1,0:T(8,128)(2,1)}), bf16[8,96,2048]{2,1,0:T(8,128)(2,1)S(1)}, u32[]{:S(2)}, u32[]{:S(2)}) async-start(bf16[8,96,2048]{2,1,0:T(8,128)(2,1)} %bitcast.81), calls=%async_computation | async-start | bytes 6291456 | tf_op jit(solution)/shard_map/all_to_all | solution.py:394
  30.4 24.1 %all-gather.2.cloned.1.call-done.down.up = bf16[512,2304]{1,0:T(8,128)(2,1)} async-done(((bf16[64,2304]{1,0:T(8,128)(2,1)}), bf16[512,2304]{1,0:T(8,128)(2,1)}) %all-gather.2.cloned.1.call-update) | async-done | bytes 2359312 | tf_op jit(solution)/shard_map/all_gather | solution.py:386
  61.2 6.2 %all-to-all-done = bf16[8,96,2048]{2,1,0:T(8,128)(2,1)S(1)} async-done(((bf16[8,96,2048]{2,1,0:T(8,128)(2,1)}), bf16[8,96,2048]{2,1,0:T(8,128)(2,1)S(1)}, u32[]{:S(2)}, u32[]{:S(2)}) %all-to-all-start) | async-done | bytes 3145760 | tf_op jit(solution)/shard_map/all_to_all | solution.py:394
  69.2 5.3 %shard_map.177 = (bf16[768,512]{1,0:T(8,128)(2,1)}, f32[512,2048]{1,0:T(8,128)}) custom-call(f32[384,128]{1,0:T(8,128)} %shard_map.176.a, f32[384,128]{1,0:T(8,128)} %collective-permute-done.12.b, f32[384,128]{1,0:T(8,128)} %copy-done.12, f32[384,128]{1,0:T(8,128)} %copy-done.11, bf16[768,2048]{1,0:T(8,128)(2,1)} %bitcast.75), custom_call_target="tpu_custom_call" | custom-call | tf_op jit(solution)/shard_map/pallas_call | solution.py:240
  74.5 4.7 %shard_map.172.a = f32[384,128]{1,0:T(8,128)} custom-call(bf16[768,2048]{1,0:T(8,128)(2,1)} %bitcast.76, bf16[512,2304]{1,0:T(8,128)(2,1)} %all-gather.2.cloned.1.call-done.down.up), custom_call_target="tpu_custom_call" | custom-call | tf_op jit(solution)/shard_map/pallas_call | solution.py:264
  83.0 6.8 %collective-permute-done.2.d = f32[384,128]{1,0:T(8,128)S(1)} collective-permute-done((f32[384,128]{1,0:T(8,128)}, f32[384,128]{1,0:T(8,128)S(1)}, u32[]{:S(2)}, u32[]{:S(2)}) %collective-permute-start.2) | collective-permute-done | bytes 196640 | tf_op jit(solution)/shard_map/ppermute | solution.py:43
  97.1 4.8 %all-to-all-start.2 = ((bf16[8,96,256]{2,1,0:T(8,128)(2,1)}), bf16[8,96,256]{2,1,0:T(8,128)(2,1)S(1)}, u32[]{:S(2)}, u32[]{:S(2)}) async-start(bf16[8,96,256]{2,1,0:T(8,128)(2,1)} %bitcast.85), calls=%async_computation.2 | async-start | bytes 786432 | tf_op jit(solution)/shard_map/all_to_all | solution.py:422
  101.9 4.7 %shard_map.178 = bf16[768,2048]{1,0:T(8,128)(2,1)} custom-call(bf16[768,512]{1,0:T(8,128)(2,1)} %get-tuple-element.25.back16, bf16[512,2304]{1,0:T(8,128)(2,1)} %all-gather.2.cloned.1.call-done.down.up), custom_call_target="tpu_custom_call" | custom-call | tf_op jit(solution)/shard_map/pallas_call | solution.py:252
  110.1 5.0 %all-to-all-start.3 = ((bf16[8,96,2048]{2,1,0:T(8,128)(2,1)}), bf16[8,96,2048]{2,1,0:T(8,128)(2,1)S(1)}, u32[]{:S(2)}, u32[]{:S(2)}) async-start(bf16[8,96,2048]{2,1,0:T(8,128)(2,1)} %bitcast.77), calls=%async_computation.3 | async-start | bytes 6291456 | tf_op jit(solution)/shard_map/all_to_all | solution.py:418
  119.8 4.1 %collective-permute-start.16 = (bf16[512,256]{1,0:T(8,128)(2,1)S(1)}, bf16[512,256]{1,0:T(8,128)(2,1)}, u32[]{:S(2)}, u32[]{:S(2)}) collective-permute-start(bf16[512,256]{1,0:T(8,128)(2,1)S(1)} %copy-done.4), channel_id=1, source_target_pairs={{0,2},{1,3},{2,0},{3,1},{4,6},{5,7},{6,4},{7,5},{8,10},{9,11},{10,... | collective-permute-start | bytes 786440 | tf_op jit(solution)/shard_map/ppermute | solution.py:43
  127.5 5.3 %collective-permute-done.5.refs_2_.refs_6_ = bf16[1024,256]{1,0:T(8,128)(2,1)} collective-permute-done((bf16[1024,256]{1,0:T(8,128)(2,1)}, bf16[1024,256]{1,0:T(8,128)(2,1)}, u32[]{:S(2)}, u32[]{:S(2)}) %collective-permute-start.5) | collective-permute-done | bytes 524320 | tf_op jit(solution)/shard_map/ppermute | solution.py:43
  135.1 11.1 %collective-permute-done.3.refs_0_.refs_4_ = bf16[1024,256]{1,0:T(8,128)(2,1)} collective-permute-done((bf16[1024,256]{1,0:T(8,128)(2,1)}, bf16[1024,256]{1,0:T(8,128)(2,1)}, u32[]{:S(2)}, u32[]{:S(2)}) %collective-permute-start.3) | collective-permute-done | bytes 524320 | tf_op jit(solution)/shard_map/ppermute | solution.py:43
  146.3 4.6 %collective-permute-done.16.refs_2_ = bf16[512,256]{1,0:T(8,128)(2,1)} collective-permute-done((bf16[512,256]{1,0:T(8,128)(2,1)S(1)}, bf16[512,256]{1,0:T(8,128)(2,1)}, u32[]{:S(2)}, u32[]{:S(2)}) %collective-permute-start.16) | collective-permute-done | bytes 262176 | tf_op jit(solution)/shard_map/ppermute | solution.py:43
  150.9 3.2 %collective-permute-start.17 = (bf16[512,256]{1,0:T(8,128)(2,1)S(1)}, bf16[512,256]{1,0:T(8,128)(2,1)}, u32[]{:S(2)}, u32[]{:S(2)}) collective-permute-start(bf16[512,256]{1,0:T(8,128)(2,1)S(1)} %copy-done.4), channel_id=1, source_target_pairs={{0,3},{1,0},{2,1},{3,2},{4,7},{5,4},{6,5},{7,6},{8,11},{9,8},{10,9... | collective-permute-start | bytes 786440 | tf_op jit(solution)/shard_map/ppermute | solution.py:43
  156.6 3.2 %collective-permute-start.19 = (f32[64,256]{1,0:T(8,128)}, f32[64,256]{1,0:T(8,128)S(1)}, u32[]{:S(2)}, u32[]{:S(2)}) collective-permute-start(f32[64,256]{1,0:T(8,128)} %get-tuple-element.36), channel_id=1, source_target_pairs={{0,64},{32,96},{64,128},{96,160},{128,192},{160,224},{192,0},{224,... | collective-permute-start | bytes 196616 | tf_op jit(solution)/shard_map/ppermute | solution.py:431
  159.8 3.1 %collective-permute-start.21 = (f32[64,256]{1,0:T(8,128)}, f32[64,256]{1,0:T(8,128)}, u32[]{:S(2)}, u32[]{:S(2)}) collective-permute-start(f32[64,256]{1,0:T(8,128)} %get-tuple-element.37), channel_id=1, source_target_pairs={{0,192},{32,224},{64,0},{96,32},{128,64},{160,96},{192,128},{224,1... | collective-permute-start | bytes 196616 | tf_op jit(solution)/shard_map/ppermute | solution.py:431
  162.9 4.9 %collective-permute-start.20 = (f32[64,256]{1,0:T(8,128)S(1)}, f32[64,256]{1,0:T(8,128)}, u32[]{:S(2)}, u32[]{:S(2)}) collective-permute-start(f32[64,256]{1,0:T(8,128)S(1)} %get-tuple-element.38), channel_id=1, source_target_pairs={{0,128},{32,160},{64,192},{96,224},{128,0},{160,32},{192,64},{224,... | collective-permute-start | bytes 196616 | tf_op jit(solution)/shard_map/ppermute | solution.py:431
  168.5 7.2 %shard_map.174 = (f32[512,256]{1,0:T(8,128)}, f32[512,256]{1,0:T(8,128)}, f32[512,256]{1,0:T(8,128)}, f32[512,256]{1,0:T(8,128)}) custom-call(s32[2]{0:T(128)} %pad_add_fusion.at, bf16[512,2048]{1,0:T(8,128)(2,1)} %tokens.1, bf16[8192,256]{1,0:T(8,128)(2,1)} %own.3, bf16[1024,256]{1,0:T(8,128)(2,1)} %collective-permute-done.3.refs_0_.refs_4_, ...), custom_call_target="tpu_custom_call" | custom-call | tf_op jit(solution)/shard_map/pallas_call | solution.py:296
  178.2 7.2 %shard_map.179.base = f32[512,2048]{1,0:T(8,128)} custom-call(s32[2]{0:T(128)} %pad_add_fusion.at, bf16[8192,256]{1,0:T(8,128)(2,1)} %own.3, bf16[512,256]{1,0:T(8,128)(2,1)} %refs_0_.1, bf16[512,256]{1,0:T(8,128)(2,1)} %collective-permute-done.15.refs_1_, bf16[512,256]{1,0:T(8,128)(2,1)} %collective-permute-done.16.refs_2_, ...), custom_call_target="tpu_custom_call" | custom-call | tf_op jit(solution)/shard_map/pallas_call | solution.py:296
  187.7 3.3 %collective-permute-done.9.b = f32[512,256]{1,0:T(8,128)} collective-permute-done((f32[512,256]{1,0:T(8,128)}, f32[512,256]{1,0:T(8,128)}, u32[]{:S(2)}, u32[]{:S(2)}) %collective-permute-start.9) | collective-permute-done | bytes 524320 | tf_op jit(solution)/shard_map/ppermute | solution.py:43
  192.5 7.8 %collective-permute-done.11.d = f32[512,256]{1,0:T(8,128)} collective-permute-done((f32[512,256]{1,0:T(8,128)}, f32[512,256]{1,0:T(8,128)}, u32[]{:S(2)}, u32[]{:S(2)}) %collective-permute-start.11) | collective-permute-done | bytes 524320 | tf_op jit(solution)/shard_map/ppermute | solution.py:43
  205.0 5.4 %shard_map.180 = bf16[512,2048]{1,0:T(8,128)(2,1)} custom-call(bf16[768,512]{1,0:T(8,128)(2,1)} %get-tuple-element.18.route, bf16[768,2048]{1,0:T(8,128)(2,1)} %bitcast.78, f32[512,2048]{1,0:T(8,128)} %shard_map.179.base), custom_call_target="tpu_custom_call" | custom-call | tf_op jit(solution)/shard_map/pallas_call | solution.py:353
  (82 shorter events, 57.9 us)
Async XLA Ops:
  7.2 47.3 %all-gather.2.cloned.1.call-start = ((), (), s32[]{:S(2)}) async-start(), calls=%async_computation.5 | async-start | bytes 2654208 | tf_op jit(solution)/shard_map/all_gather | solution.py:386
  11.6 13.1 %all-to-all-start.1 = ((bf16[8,96,256]{2,1,0:T(8,128)(2,1)}), bf16[8,96,256]{2,1,0:T(8,128)(2,1)S(1)}, u32[]{:S(2)}, u32[]{:S(2)}) async-start(bf16[8,96,256]{2,1,0:T(8,128)(2,1)} %bitcast.86), calls=%async_computation.1 | async-start | bytes 786432 | tf_op jit(solution)/shard_map/all_to_all | solution.py:395
  25.4 42.0 %all-to-all-start = ((bf16[8,96,2048]{2,1,0:T(8,128)(2,1)}), bf16[8,96,2048]{2,1,0:T(8,128)(2,1)S(1)}, u32[]{:S(2)}, u32[]{:S(2)}) async-start(bf16[8,96,2048]{2,1,0:T(8,128)(2,1)} %bitcast.81), calls=%async_computation | async-start | bytes 6291456 | tf_op jit(solution)/shard_map/all_to_all | solution.py:394
  30.4 180.0 %reduce-scatter.2.cloned.1.call-start = ((), (), s32[]{:S(2)}) async-start(), calls=%async_computation.6 | async-start | bytes 4718592 | tf_op jit(solution)/shard_map/reduce_scatter | solution.py:416
  56.7 10.7 %collective-permute-start.14 = (f32[384,128]{1,0:T(8,128)}, f32[384,128]{1,0:T(8,128)S(1)}, u32[]{:S(2)}, u32[]{:S(2)}) collective-permute-start(f32[384,128]{1,0:T(8,128)} %shard_map.176.a), channel_id=1, source_target_pairs={{0,3},{1,0},{2,1},{3,2},{4,7},{5,4},{6,5},{7,6},{8,11},{9,8},{10,9... | collective-permute-start | bytes 589832 | tf_op jit(solution)/shard_map/ppermute | solution.py:43
  82.1 11.4 %collective-permute-start = (f32[384,128]{1,0:T(8,128)}, f32[384,128]{1,0:T(8,128)S(1)}, u32[]{:S(2)}, u32[]{:S(2)}) collective-permute-start(f32[384,128]{1,0:T(8,128)} %shard_map.172.a), channel_id=1, source_target_pairs={{0,1},{1,2},{2,3},{3,0},{4,5},{5,6},{6,7},{7,4},{8,9},{9,10},{10,1... | collective-permute-start | bytes 589832 | tf_op jit(solution)/shard_map/ppermute | solution.py:43
  97.1 12.3 %all-to-all-start.2 = ((bf16[8,96,256]{2,1,0:T(8,128)(2,1)}), bf16[8,96,256]{2,1,0:T(8,128)(2,1)S(1)}, u32[]{:S(2)}, u32[]{:S(2)}) async-start(bf16[8,96,256]{2,1,0:T(8,128)(2,1)} %bitcast.85), calls=%async_computation.2 | async-start | bytes 786432 | tf_op jit(solution)/shard_map/all_to_all | solution.py:422
  110.1 93.3 %all-to-all-start.3 = ((bf16[8,96,2048]{2,1,0:T(8,128)(2,1)}), bf16[8,96,2048]{2,1,0:T(8,128)(2,1)S(1)}, u32[]{:S(2)}, u32[]{:S(2)}) async-start(bf16[8,96,2048]{2,1,0:T(8,128)(2,1)} %bitcast.77), calls=%async_computation.3 | async-start | bytes 6291456 | tf_op jit(solution)/shard_map/all_to_all | solution.py:418
  117.7 15.1 %collective-permute-start.5 = (bf16[1024,256]{1,0:T(8,128)(2,1)}, bf16[1024,256]{1,0:T(8,128)(2,1)}, u32[]{:S(2)}, u32[]{:S(2)}) collective-permute-start(bf16[1024,256]{1,0:T(8,128)(2,1)} %get-tuple-element.30), channel_id=1, source_target_pairs={{0,3},{1,0},{2,1},{3,2},{4,7},{5,4},{6,5},{7,6},{8,11},{9,8},{10,9... | collective-permute-start | bytes 1572872 | tf_op jit(solution)/shard_map/ppermute | solution.py:43
  118.5 16.7 %collective-permute-start.4 = (bf16[1024,256]{1,0:T(8,128)(2,1)}, bf16[1024,256]{1,0:T(8,128)(2,1)}, u32[]{:S(2)}, u32[]{:S(2)}) collective-permute-start(bf16[1024,256]{1,0:T(8,128)(2,1)} %get-tuple-element.31), channel_id=1, source_target_pairs={{0,2},{1,3},{2,0},{3,1},{4,6},{5,7},{6,4},{7,5},{8,10},{9,11},{10,... | collective-permute-start | bytes 1572872 | tf_op jit(solution)/shard_map/ppermute | solution.py:43
  118.9 27.3 %collective-permute-start.3 = (bf16[1024,256]{1,0:T(8,128)(2,1)}, bf16[1024,256]{1,0:T(8,128)(2,1)}, u32[]{:S(2)}, u32[]{:S(2)}) collective-permute-start(bf16[1024,256]{1,0:T(8,128)(2,1)} %get-tuple-element.32), channel_id=1, source_target_pairs={{0,1},{1,2},{2,3},{3,0},{4,5},{5,6},{6,7},{7,4},{8,9},{9,10},{10,1... | collective-permute-start | bytes 1572872 | tf_op jit(solution)/shard_map/ppermute | solution.py:43
  119.8 31.1 %collective-permute-start.16 = (bf16[512,256]{1,0:T(8,128)(2,1)S(1)}, bf16[512,256]{1,0:T(8,128)(2,1)}, u32[]{:S(2)}, u32[]{:S(2)}) collective-permute-start(bf16[512,256]{1,0:T(8,128)(2,1)S(1)} %copy-done.4), channel_id=1, source_target_pairs={{0,2},{1,3},{2,0},{3,1},{4,6},{5,7},{6,4},{7,5},{8,10},{9,11},{10,... | collective-permute-start | bytes 786440 | tf_op jit(solution)/shard_map/ppermute | solution.py:43
  125.6 25.3 %collective-permute-start.18 = (f32[4,64,256]{2,1,0:T(8,128)}, f32[4,64,256]{2,1,0:T(8,128)}, u32[]{:S(2)}, u32[]{:S(2)}) collective-permute-start(f32[4,64,256]{2,1,0:T(8,128)} %dynamic-slice_bitcast_fusion), channel_id=1, source_target_pairs={{0,32},{32,0},{64,96},{96,64},{128,160},{160,128},{192,224},{224,1... | collective-permute-start | bytes 786440 | tf_op jit(solution)/shard_map/ppermute | solution.py:426
  132.8 23.7 %collective-permute-start.8 = (bf16[1024,256]{1,0:T(8,128)(2,1)}, bf16[1024,256]{1,0:T(8,128)(2,1)}, u32[]{:S(2)}, u32[]{:S(2)}) collective-permute-start(bf16[1024,256]{1,0:T(8,128)(2,1)} %collective-permute-done.5.refs_2_.refs_6_), channel_id=1, source_target_pairs={{0,4},{4,0},{1,5},{5,1},{2,6},{6,2},{3,7},{7,3},{8,12},{12,8},{9,1... | collective-permute-start | bytes 1572872 | tf_op jit(solution)/shard_map/ppermute | solution.py:404
  135.1 24.7 %collective-permute-start.7 = (bf16[1024,256]{1,0:T(8,128)(2,1)}, bf16[1024,256]{1,0:T(8,128)(2,1)}, u32[]{:S(2)}, u32[]{:S(2)}) collective-permute-start(bf16[1024,256]{1,0:T(8,128)(2,1)} %collective-permute-done.4.refs_1_.refs_5_), channel_id=1, source_target_pairs={{0,4},{4,0},{1,5},{5,1},{2,6},{6,2},{3,7},{7,3},{8,12},{12,8},{9,1... | collective-permute-start | bytes 1572872 | tf_op jit(solution)/shard_map/ppermute | solution.py:404
  146.3 16.7 %collective-permute-start.6 = (bf16[1024,256]{1,0:T(8,128)(2,1)}, bf16[1024,256]{1,0:T(8,128)(2,1)}, u32[]{:S(2)}, u32[]{:S(2)}) collective-permute-start(bf16[1024,256]{1,0:T(8,128)(2,1)} %collective-permute-done.3.refs_0_.refs_4_), channel_id=1, source_target_pairs={{0,4},{4,0},{1,5},{5,1},{2,6},{6,2},{3,7},{7,3},{8,12},{12,8},{9,1... | collective-permute-start | bytes 1572872 | tf_op jit(solution)/shard_map/ppermute | solution.py:404
  150.9 24.8 %collective-permute-start.15 = (bf16[512,256]{1,0:T(8,128)(2,1)S(1)}, bf16[512,256]{1,0:T(8,128)(2,1)}, u32[]{:S(2)}, u32[]{:S(2)}) collective-permute-start(bf16[512,256]{1,0:T(8,128)(2,1)S(1)} %copy-done.4), channel_id=1, source_target_pairs={{0,1},{1,2},{2,3},{3,0},{4,5},{5,6},{6,7},{7,4},{8,9},{9,10},{10,1... | collective-permute-start | bytes 786440 | tf_op jit(solution)/shard_map/ppermute | solution.py:43
  150.9 24.9 %collective-permute-start.17 = (bf16[512,256]{1,0:T(8,128)(2,1)S(1)}, bf16[512,256]{1,0:T(8,128)(2,1)}, u32[]{:S(2)}, u32[]{:S(2)}) collective-permute-start(bf16[512,256]{1,0:T(8,128)(2,1)S(1)} %copy-done.4), channel_id=1, source_target_pairs={{0,3},{1,0},{2,1},{3,2},{4,7},{5,4},{6,5},{7,6},{8,11},{9,8},{10,9... | collective-permute-start | bytes 786440 | tf_op jit(solution)/shard_map/ppermute | solution.py:43
  156.6 20.1 %collective-permute-start.19 = (f32[64,256]{1,0:T(8,128)}, f32[64,256]{1,0:T(8,128)S(1)}, u32[]{:S(2)}, u32[]{:S(2)}) collective-permute-start(f32[64,256]{1,0:T(8,128)} %get-tuple-element.36), channel_id=1, source_target_pairs={{0,64},{32,96},{64,128},{96,160},{128,192},{160,224},{192,0},{224,... | collective-permute-start | bytes 196616 | tf_op jit(solution)/shard_map/ppermute | solution.py:431
  159.8 25.6 %collective-permute-start.21 = (f32[64,256]{1,0:T(8,128)}, f32[64,256]{1,0:T(8,128)}, u32[]{:S(2)}, u32[]{:S(2)}) collective-permute-start(f32[64,256]{1,0:T(8,128)} %get-tuple-element.37), channel_id=1, source_target_pairs={{0,192},{32,224},{64,0},{96,32},{128,64},{160,96},{192,128},{224,1... | collective-permute-start | bytes 196616 | tf_op jit(solution)/shard_map/ppermute | solution.py:431
  162.9 22.4 %collective-permute-start.20 = (f32[64,256]{1,0:T(8,128)S(1)}, f32[64,256]{1,0:T(8,128)}, u32[]{:S(2)}, u32[]{:S(2)}) collective-permute-start(f32[64,256]{1,0:T(8,128)S(1)} %get-tuple-element.38), channel_id=1, source_target_pairs={{0,128},{32,160},{64,192},{96,224},{128,0},{160,32},{192,64},{224,... | collective-permute-start | bytes 196616 | tf_op jit(solution)/shard_map/ppermute | solution.py:431
  175.7 15.2 %collective-permute-start.9 = (f32[512,256]{1,0:T(8,128)}, f32[512,256]{1,0:T(8,128)}, u32[]{:S(2)}, u32[]{:S(2)}) collective-permute-start(f32[512,256]{1,0:T(8,128)} %get-tuple-element.22), channel_id=1, source_target_pairs={{0,3},{1,0},{2,1},{3,2},{4,7},{5,4},{6,5},{7,6},{8,11},{9,8},{10,9... | collective-permute-start | bytes 1572872 | tf_op jit(solution)/shard_map/ppermute | solution.py:43
  175.8 16.7 %collective-permute-start.10 = (f32[512,256]{1,0:T(8,128)}, f32[512,256]{1,0:T(8,128)}, u32[]{:S(2)}, u32[]{:S(2)}) collective-permute-start(f32[512,256]{1,0:T(8,128)} %get-tuple-element.23), channel_id=1, source_target_pairs={{0,2},{1,3},{2,0},{3,1},{4,6},{5,7},{6,4},{7,5},{8,10},{9,11},{10,... | collective-permute-start | bytes 1572872 | tf_op jit(solution)/shard_map/ppermute | solution.py:43
  176.7 23.7 %collective-permute-start.11 = (f32[512,256]{1,0:T(8,128)}, f32[512,256]{1,0:T(8,128)}, u32[]{:S(2)}, u32[]{:S(2)}) collective-permute-start(f32[512,256]{1,0:T(8,128)} %get-tuple-element.24), channel_id=1, source_target_pairs={{0,1},{1,2},{2,3},{3,0},{4,5},{5,6},{6,7},{7,4},{8,9},{9,10},{10,1... | collective-permute-start | bytes 1572872 | tf_op jit(solution)/shard_map/ppermute | solution.py:43
  (18 other events, 82.2 us)
Sparse Core Ops, SparseCore 0:
  10.3 44.1 all-gather.1
  74.6 56.5 reduce-scatter.1
